TPU v7x, 32 devices: a whole 2x2x4 slice. The times are simulated.
32 devices in a mesh: rows: 4 (over y, x), ffn: 8 (over z, core).
Axes of the slice: x: 2, y: 2, z: 4, core: 2. Of those that a mesh axis runs over, the one named last changes fastest.
Arguments:
- tokens: bfloat16 [32768, 1024], P(('rows', 'ffn')), may hold values from -6 to 6
- lengths: int32 [32], P(('rows', 'ffn')), may hold values from 128 to 1024, as said below
- cotangent: bfloat16 [32768, 1024], P(('rows', 'ffn')), may hold values from -6 to 6
- ln_attn_gain: float32 [1024], replicated, may hold values from 0.1 to 1.9
- ln_attn_bias: float32 [1024], replicated, may hold values from -1.75 to 1.75
- w_query: bfloat16 [1024, 1024], P(('rows', 'ffn')), may hold values from -0.1875 to 0.1875
- query_bias: float32 [1024], replicated, may hold values from -3 to 3
- w_key: bfloat16 [1024, 1024], P(('rows', 'ffn')), may hold values from -0.1875 to 0.1875
- w_value: bfloat16 [1024, 1024], P(('rows', 'ffn')), may hold values from -0.1875 to 0.1875
- value_bias: float32 [1024], replicated, may hold values from -3 to 3
- head_scale: float32 [16], replicated, may hold values from 0.3 to 3
- w_out: bfloat16 [1024, 1024], P(('rows', 'ffn')), may hold values from -0.1875 to 0.1875
- out_bias: float32 [1024], replicated, may hold values from -3 to 3
- post_gain: float32 [1024], replicated, may hold values from 0.1 to 1.9
- post_bias: float32 [1024], replicated, may hold values from -1.75 to 1.75
- ffn_gain: float32 [1024], replicated, may hold values from 0.1 to 1.9
- ffn_bias: float32 [1024], replicated, may hold values from -1.75 to 1.75
- w_up: bfloat16 [1024, 4096], P('rows', 'ffn'), may hold values from -1 to 1
- up_bias: float32 [4096], replicated, may hold values from -3 to 3
- mid_gain: float32 [4096], replicated, may hold values from 0.1 to 1.9
- mid_bias: float32 [4096], replicated, may hold values from -1.75 to 1.75
- w_down: bfloat16 [1024, 4096], P('rows', 'ffn'), may hold values from -0.09375 to 0.09375
- down_bias: float32 [1024], replicated, may hold values from -3 to 3
Outputs:
- result: float32 [32768, 1024], P(('rows', 'ffn'))
- grad_tokens: float32 [32768, 1024], P(('rows', 'ffn'))
- grad_ln_attn_gain: float32 [1024], replicated
- grad_ln_attn_bias: float32 [1024], replicated
- grad_w_query: float32 [1024, 1024], P(('rows', 'ffn'))
- grad_query_bias: float32 [1024], replicated
- grad_w_key: float32 [1024, 1024], P(('rows', 'ffn'))
- grad_w_value: float32 [1024, 1024], P(('rows', 'ffn'))
- grad_value_bias: float32 [1024], replicated
- grad_head_scale: float32 [16], replicated
- grad_w_out: float32 [1024, 1024], P(('rows', 'ffn'))
- grad_out_bias: float32 [1024], replicated
- grad_post_gain: float32 [1024], replicated
- grad_post_bias: float32 [1024], replicated
- grad_ffn_gain: float32 [1024], replicated
- grad_ffn_bias: float32 [1024], replicated
- grad_w_up: float32 [1024, 4096], P('rows', 'ffn')
- grad_up_bias: float32 [4096], P('ffn')
- grad_mid_gain: float32 [4096], P('ffn')
- grad_mid_bias: float32 [4096], P('ffn')
- grad_w_down: float32 [1024, 4096], P('rows', 'ffn')
- grad_down_bias: float32 [1024], replicated
Inputs may be any that keep to these rules, and one draw needn't show every extreme that they name: `lengths`: each sequence has between 128 and 1024 valid tokens, at the start of its slots; some sequence has exactly 1024.
All inputs are finite; a program needn't handle non-finite values.
Results may differ from a plain program's by a relative error of at most 0.013.
Values may be sent and summed in bfloat16 or wider, within the bound.
A program may use at most 320 MiB of HBM per device.

v0:
```python
import jax
import jax.numpy as jnp
from jax import lax
from jax.sharding import PartitionSpec as P

epsilon = 1e-05
masked_score = -1e30


def layer_norm(values, gain, shift):
    center = jnp.mean(values, axis=-1, keepdims=True)
    centered = values - center
    spread = jnp.mean(centered * centered, axis=-1, keepdims=True)
    return centered * lax.rsqrt(spread + epsilon) * gain + shift


def exact_gelu(values):
    return jax.nn.gelu(values, approximate=False)


def plain_dot(left, right):
    return jnp.dot(left, right, preferred_element_type=jnp.float32)


def contract_rows(left, right):
    return lax.dot_general(
        left, right, (((0,), (0,)), ((), ())), preferred_element_type=jnp.float32
    )


def contract_cols(left, right):
    return lax.dot_general(
        left, right, (((1,), (1,)), ((), ())), preferred_element_type=jnp.float32
    )


def block_scores(queries, key_rows, first, block_rows, length):
    rows_here = lax.dynamic_slice_in_dim(queries, first, block_rows, 0)
    factor = queries.shape[-1] ** (-0.5)
    scores = (
        jnp.einsum("qhd,khd->hqk", rows_here, key_rows, preferred_element_type=jnp.float32) * factor
    )
    key_pos = jnp.arange(key_rows.shape[0])
    query_pos = first + jnp.arange(block_rows)
    allowed = (key_pos[None, :] <= query_pos[:, None]) & (key_pos[None, :] < length)
    return (rows_here, jnp.where(allowed[None], scores, masked_score))


def attend_forward(queries, key_rows, value_rows, length, block_rows):

    def one_block(first):
        rows_here, scores = block_scores(queries, key_rows, first, block_rows, length)
        peak = jnp.max(scores, axis=-1, keepdims=True)
        weights = jnp.exp(scores - peak)
        totals = jnp.sum(weights, axis=-1, keepdims=True)
        probs = (weights / totals).astype(jnp.bfloat16)
        context = jnp.einsum("hqk,khd->qhd", probs, value_rows, preferred_element_type=jnp.float32)
        return (context, peak[..., 0] + jnp.log(totals[..., 0]))

    firsts = jnp.arange(queries.shape[0] // block_rows) * block_rows
    context, log_totals = lax.map(one_block, firsts)
    return (context.reshape(queries.shape), log_totals)


def attend_backward(queries, key_rows, value_rows, grad_context, log_totals, length, block_rows):
    factor = queries.shape[-1] ** (-0.5)

    def one_block(carry, inputs_here):
        grad_keys, grad_values = carry
        first, block_log = inputs_here
        rows_here, scores = block_scores(queries, key_rows, first, block_rows, length)
        grad_rows = lax.dynamic_slice_in_dim(grad_context, first, block_rows, 0)
        probs = jnp.exp(scores - block_log[..., None])
        grad_probs = jnp.einsum(
            "qhd,khd->hqk", grad_rows, value_rows, preferred_element_type=jnp.float32
        )
        grad_values = grad_values + jnp.einsum(
            "hqk,qhd->khd",
            probs.astype(jnp.bfloat16),
            grad_rows,
            preferred_element_type=jnp.float32,
        )
        inner = jnp.sum(probs * grad_probs, axis=-1, keepdims=True)
        grad_scores = (probs * (grad_probs - inner)).astype(jnp.bfloat16)
        grad_queries = (
            jnp.einsum("hqk,khd->qhd", grad_scores, key_rows, preferred_element_type=jnp.float32)
            * factor
        )
        grad_keys = (
            grad_keys
            + jnp.einsum("hqk,qhd->khd", grad_scores, rows_here, preferred_element_type=jnp.float32)
            * factor
        )
        return ((grad_keys, grad_values), grad_queries)

    firsts = jnp.arange(queries.shape[0] // block_rows) * block_rows
    zeros_like_keys = jnp.zeros(key_rows.shape, jnp.float32)
    (grad_keys, grad_values), grad_queries = lax.scan(
        one_block, (zeros_like_keys, zeros_like_keys), (firsts, log_totals)
    )
    return (grad_queries.reshape(queries.shape), grad_keys, grad_values)


def shards(
    tokens,
    lengths,
    cotangent,
    ln_attn_gain,
    ln_attn_bias,
    w_query,
    query_bias,
    w_key,
    w_value,
    value_bias,
    head_scale,
    w_out,
    out_bias,
    post_gain,
    post_bias,
    ffn_gain,
    ffn_bias,
    w_up,
    up_bias,
    mid_gain,
    mid_bias,
    w_down,
    down_bias,
):
    seq_len, width = tokens.shape
    head_count = head_scale.shape[0]
    head_size = width // head_count
    heads_shape = (seq_len, head_count, head_size)
    block_rows = min(seq_len, 512)
    length = lengths[0]
    valid_rows = (jnp.arange(seq_len) < length)[:, None]
    inputs = tokens.astype(jnp.float32)
    full_query, full_key, full_value, full_out = (
        lax.all_gather(w_query, ("rows", "ffn"), axis=0, tiled=True),
        lax.all_gather(w_key, ("rows", "ffn"), axis=0, tiled=True),
        lax.all_gather(w_value, ("rows", "ffn"), axis=0, tiled=True),
        lax.all_gather(w_out, ("rows", "ffn"), axis=0, tiled=True),
    )
    normed, first_back = jax.vjp(layer_norm, inputs, ln_attn_gain, ln_attn_bias)
    normed_low = normed.astype(jnp.bfloat16)
    queries = (
        (plain_dot(normed_low, full_query) + query_bias).astype(jnp.bfloat16).reshape(heads_shape)
    )
    key_rows = plain_dot(normed_low, full_key).astype(jnp.bfloat16).reshape(heads_shape)
    value_rows = (
        (plain_dot(normed_low, full_value) + value_bias).astype(jnp.bfloat16).reshape(heads_shape)
    )
    context, log_totals = attend_forward(queries, key_rows, value_rows, length, block_rows)
    scaled_low = (context * head_scale[None, :, None]).reshape(seq_len, width).astype(jnp.bfloat16)
    projected = plain_dot(scaled_low, full_out) + out_bias
    branch, second_back = jax.vjp(layer_norm, projected, post_gain, post_bias)
    mixed = inputs + branch
    second, third_back = jax.vjp(layer_norm, mixed, ffn_gain, ffn_bias)
    second_low = second.astype(jnp.bfloat16)
    grad_result = jnp.where(valid_rows, cotangent.astype(jnp.float32), 0.0)
    grad_result_low = grad_result.astype(jnp.bfloat16)
    up_rows, down_rows = (
        lax.all_gather(w_up, "rows", axis=0, tiled=True),
        lax.all_gather(w_down, "rows", axis=0, tiled=True),
    )
    up_full, down_full = (
        lax.all_gather(up_rows, "ffn", axis=1, tiled=True),
        lax.all_gather(down_rows, "ffn", axis=1, tiled=True),
    )
    pre_act = plain_dot(second_low, up_full) + up_bias
    activated, gelu_back = jax.vjp(exact_gelu, pre_act)
    row_mean = jnp.mean(activated, axis=1, keepdims=True)
    inverse = lax.rsqrt(
        jnp.mean(activated * activated, axis=1, keepdims=True) - row_mean * row_mean + epsilon
    )
    unit_rows = (activated - row_mean) * inverse
    mid_low = (unit_rows * mid_gain + mid_bias).astype(jnp.bfloat16)
    ffn_part = contract_cols(mid_low, down_full)
    grad_mid = plain_dot(grad_result_low, down_full)
    grad_down_full = contract_rows(grad_result_low, mid_low)
    scaled_grad = grad_mid * mid_gain
    grad_act = (
        scaled_grad
        - jnp.mean(scaled_grad, axis=1, keepdims=True)
        - unit_rows * jnp.mean(scaled_grad * unit_rows, axis=1, keepdims=True)
    ) * inverse
    grad_pre_low = gelu_back(grad_act)[0].astype(jnp.bfloat16)
    grad_up_full = contract_rows(second_low, grad_pre_low)
    grad_second = contract_cols(grad_pre_low, up_full)
    stacked = jnp.stack(
        [
            jnp.sum(grad_pre_low.astype(jnp.float32), axis=0),
            jnp.sum(grad_mid * unit_rows, axis=0),
            jnp.sum(grad_mid, axis=0),
        ]
    )
    grad_up, grad_down, stacked_own = (
        lax.psum_scatter(grad_up_full, "ffn", scatter_dimension=1, tiled=True),
        lax.psum_scatter(grad_down_full, "ffn", scatter_dimension=1, tiled=True),
        lax.psum_scatter(stacked, "ffn", scatter_dimension=1, tiled=True),
    )
    grad_up, grad_down = (
        lax.psum_scatter(
            grad_up.astype(jnp.bfloat16), "rows", scatter_dimension=0, tiled=True
        ).astype(jnp.float32),
        lax.psum_scatter(
            grad_down.astype(jnp.bfloat16), "rows", scatter_dimension=0, tiled=True
        ).astype(jnp.float32),
    )
    grad_up_bias, grad_mid_gain, grad_mid_bias = lax.psum(
        (stacked_own[0], stacked_own[1], stacked_own[2]), "rows"
    )
    result = jnp.where(valid_rows, mixed + ffn_part + down_bias, 0.0)
    grad_mixed_in, grad_ffn_gain, grad_ffn_bias = third_back(grad_second)
    grad_mixed = grad_result + grad_mixed_in
    grad_projected, grad_post_gain, grad_post_bias = second_back(grad_mixed)
    grad_projected_low = grad_projected.astype(jnp.bfloat16)
    grad_out_weight = contract_rows(scaled_low, grad_projected_low)
    grad_scaled = contract_cols(grad_projected_low, full_out).reshape(heads_shape)
    grad_head_scale = jnp.sum(grad_scaled * context, axis=(0, 2))
    grad_context = (grad_scaled * head_scale[None, :, None]).astype(jnp.bfloat16)
    grad_queries, grad_keys, grad_values = attend_backward(
        queries, key_rows, value_rows, grad_context, log_totals, length, block_rows
    )
    grad_query_low = grad_queries.reshape(seq_len, width).astype(jnp.bfloat16)
    grad_key_low = grad_keys.reshape(seq_len, width).astype(jnp.bfloat16)
    grad_value_low = grad_values.reshape(seq_len, width).astype(jnp.bfloat16)
    grad_query_weight = contract_rows(normed_low, grad_query_low)
    grad_key_weight = contract_rows(normed_low, grad_key_low)
    grad_value_weight = contract_rows(normed_low, grad_value_low)
    grad_normed = (
        contract_cols(grad_query_low, full_query)
        + contract_cols(grad_key_low, full_key)
        + contract_cols(grad_value_low, full_value)
    )
    grad_inputs, grad_ln_gain, grad_ln_bias = first_back(grad_normed)
    grad_tokens = grad_mixed + grad_inputs
    grad_query_weight, grad_key_weight, grad_value_weight, grad_out_weight = (
        lax.psum_scatter(grad_query_weight, ("rows", "ffn"), scatter_dimension=0, tiled=True),
        lax.psum_scatter(grad_key_weight, ("rows", "ffn"), scatter_dimension=0, tiled=True),
        lax.psum_scatter(grad_value_weight, ("rows", "ffn"), scatter_dimension=0, tiled=True),
        lax.psum_scatter(grad_out_weight, ("rows", "ffn"), scatter_dimension=0, tiled=True),
    )
    small_sums = lax.psum(
        (
            grad_ln_gain,
            grad_ln_bias,
            jnp.sum(grad_query_low.astype(jnp.float32), axis=0),
            jnp.sum(grad_value_low.astype(jnp.float32), axis=0),
            grad_head_scale,
            jnp.sum(grad_projected_low.astype(jnp.float32), axis=0),
            grad_post_gain,
            grad_post_bias,
            grad_ffn_gain,
            grad_ffn_bias,
            jnp.sum(grad_result_low.astype(jnp.float32), axis=0),
        ),
        ("rows", "ffn"),
    )
    (
        grad_ln_gain,
        grad_ln_bias,
        grad_query_bias,
        grad_value_bias,
        grad_head_scale,
        grad_out_bias,
        grad_post_gain,
        grad_post_bias,
        grad_ffn_gain,
        grad_ffn_bias,
        grad_down_bias,
    ) = small_sums
    return (
        result,
        grad_tokens,
        grad_ln_gain,
        grad_ln_bias,
        grad_query_weight,
        grad_query_bias,
        grad_key_weight,
        grad_value_weight,
        grad_value_bias,
        grad_head_scale,
        grad_out_weight,
        grad_out_bias,
        grad_post_gain,
        grad_post_bias,
        grad_ffn_gain,
        grad_ffn_bias,
        grad_up,
        grad_up_bias,
        grad_mid_gain,
        grad_mid_bias,
        grad_down,
        grad_down_bias,
    )


def solution(mesh):
    placed = (
        P(("rows", "ffn"), None),
        P(("rows", "ffn")),
        P(("rows", "ffn"), None),
        P(),
        P(),
        P(("rows", "ffn"), None),
        P(),
        P(("rows", "ffn"), None),
        P(("rows", "ffn"), None),
        P(),
        P(),
        P(("rows", "ffn"), None),
        P(),
        P(),
        P(),
        P(),
        P(),
        P("rows", "ffn"),
        P(),
        P(),
        P(),
        P("rows", "ffn"),
        P(),
    )
    return jax.shard_map(
        shards,
        mesh=mesh,
        in_specs=placed,
        out_specs=(
            P(("rows", "ffn"), None),
            P(("rows", "ffn"), None),
            P(),
            P(),
            P(("rows", "ffn"), None),
            P(),
            P(("rows", "ffn"), None),
            P(("rows", "ffn"), None),
            P(),
            P(),
            P(("rows", "ffn"), None),
            P(),
            P(),
            P(),
            P(),
            P(),
            P("rows", "ffn"),
            P("ffn"),
            P("ffn"),
            P("ffn"),
            P("rows", "ffn"),
            P(),
        ),
        check_vma=False,
    )
```

profile of v0, /device:TPU:0, one launch (start us, length us, event | category | flops | bytes accessed | tf_op | source)
XLA Modules:
  0.0 1731.7 jit_solution(4929488624384349497)
XLA Ops:
  11.2 28.0 %all-gather.17.cloned.1.call-done = bf16[1024,512]{1,0:T(8,128)(2,1)} async-done(((bf16[256,512]{1,0:T(8,128)(2,1)}), bf16[1024,512]{1,0:T(8,128)(2,1)}) %all-gather.17.cloned.1.call-update) | async-done | bytes 1048592 | tf_op jit(solution)/shard_map/all_gather | solution.py:162
  49.9 17.8 %all-gather.21.cloned.1.call-done = bf16[1024,512]{1,0:T(8,128)(2,1)} async-done(((bf16[256,512]{1,0:T(8,128)(2,1)}), bf16[1024,512]{1,0:T(8,128)(2,1)}) %all-gather.21.cloned.1.call-update) | async-done | bytes 1048592 | tf_op jit(solution)/shard_map/all_gather | solution.py:163
  67.8 59.4 %all-gather.11.cloned.1.call-done = bf16[1024,1024]{1,0:T(8,128)(2,1)} async-done(((bf16[32,1024]{1,0:T(8,128)(2,1)}), bf16[1024,1024]{1,0:T(8,128)(2,1)}) %all-gather.11.cloned.1.call-update) | async-done | bytes 2097168 | tf_op jit(solution)/shard_map/all_gather | solution.py:139
  132.2 53.3 %all-gather.13.cloned.1.call-done = bf16[1024,1024]{1,0:T(8,128)(2,1)} async-done(((bf16[32,1024]{1,0:T(8,128)(2,1)}), bf16[1024,1024]{1,0:T(8,128)(2,1)}) %all-gather.13.cloned.1.call-update) | async-done | bytes 2097168 | tf_op jit(solution)/shard_map/all_gather | solution.py:140
  191.7 52.0 %all-gather.9.cloned.1.call-done = bf16[1024,1024]{1,0:T(8,128)(2,1)} async-done(((bf16[32,1024]{1,0:T(8,128)(2,1)}), bf16[1024,1024]{1,0:T(8,128)(2,1)}) %all-gather.9.cloned.1.call-update) | async-done | bytes 2097168 | tf_op jit(solution)/shard_map/all_gather | solution.py:138
  249.9 188.4 %while.27 = (s32[]{:T(128)}, f32[2,512,16,64]{1,0,3,2:T(2,128)}, f32[2,16,512]{2,1,0:T(8,128)S(1)}, s32[2]{0:T(128)S(1)}, s32[]{:T(128)}, /*index=5*/bf16[1024,1...) while((s32[]{:T(128)}, f32[2,512,16,64]{1,0,3,2:T(2,128)}, ...), condition=%wide.region_5.6_spmd, body=%wide.region_2.5_spmd.sunk | while | flops 2249188864 | bytes 127146176 | solution.py:61
  305.7 38.2 %dynamic_update_slice.18 = f32[2,512,16,64]{1,0,3,2:T(2,128)} dynamic-update-slice(f32[2,512,16,64]{1,0,3,2:T(2,128)} %get-tuple-element.491, f32[1,512,16,64]{1,0,3,2:T(1,128)} %copy.137, s32[]{:T(128)} %get-tuple-element.490, s32[]{:T(128)} %constant.67.clone.1..sunk, s32[]{:T(128)} %constant.67.clone.1..sunk, s32[]{:T(128)} %constant.67.clone.1..sunk) | dynamic-update-slice | bytes 4194308 | tf_op jit(solution)/shard_map/while/body/jit(dynamic_update_index_in_dim)/dynamic_update_slice | solution.py:61
  399.7 38.2 %dynamic_update_slice.18 = f32[2,512,16,64]{1,0,3,2:T(2,128)} dynamic-update-slice(f32[2,512,16,64]{1,0,3,2:T(2,128)} %get-tuple-element.491, f32[1,512,16,64]{1,0,3,2:T(1,128)} %copy.137, s32[]{:T(128)} %get-tuple-element.490, s32[]{:T(128)} %constant.67.clone.1..sunk, s32[]{:T(128)} %constant.67.clone.1..sunk, s32[]{:T(128)} %constant.67.clone.1..sunk) | dynamic-update-slice | bytes 4194308 | tf_op jit(solution)/shard_map/while/body/jit(dynamic_update_index_in_dim)/dynamic_update_slice | solution.py:61
  459.0 51.2 %fusion.71 = (f32[1024]{0:T(1024)S(1)}, f32[1024]{0:T(1024)S(1)}, f32[1024,4096]{1,0:T(8,128)}, f32[1024,4096]{1,0:T(8,128)}, f32[1024,4096]{1,0:T(8,128)}) fusion(f32[4096]{0:T(1024)S(1)} %copy-done.52, bf16[1024,4096]{1,0:T(8,128)(2,1)} %all-gather.19.cloned.1.call-done, bf16[1024,1024]{0,1:T(8,128)(2,1)} %add_convert_fusion.7.clone.4), kind=kOutput, calls=%fused_computation.145 | convolution fusion | flops 8875145216 | bytes 60841984 | tf_op jit(solution)/shard_map/dot_general | solution.py:22
  510.2 22.7 %multiply_reduce_fusion.1 = (f32[4096]{0:T(1024)S(1)}, f32[1024]{0:T(1024)S(1)}, f32[1024]{0:T(1024)S(1)}, f32[4096]{0:T(1024)S(1)}, f32[1024,4096]{1,0:T(8,128)}) fusion(f32[1024,4096]{1,0:T(8,128)} %get-tuple-element.329, f32[1024]{0:T(1024)S(1)} %get-tuple-element.343, f32[1024]{0:T(1024)S(1)} %get-tuple-element.342, f32[4096]{0:T(1024)S(1)} %copy-done.53, ...), kind=kOutput, calls=%fused_computation.45 | convolution fusion | flops 8630818816 | bytes 44106752 | tf_op jit(solution)/shard_map/dot_general | solution.py:22
  532.9 30.2 %convert_reduce_fusion = (f32[4096]{0:T(1024)S(1)}, bf16[1024,4096]{1,0:T(8,128)(2,1)}, bf16[1024,4096]{1,0:T(8,128)(2,1)}) fusion(f32[1024,4096]{1,0:T(8,128)} %get-tuple-element.330, f32[1024]{0:T(1024)S(1)} %get-tuple-element.353, f32[1024]{0:T(1024)S(1)} %get-tuple-element.343, f32[1024,4096]{1,0:T(8,128)} %get-tuple-element.329, ...), kind=kLoop, calls=%fused_computation.46 | loop fusion | flops 113242112 | bytes 83968000 | tf_op jit(solution)/shard_map/reduce_sum | solution.py:191
  631.6 113.8 %reduce-scatter.20.cloned.1.call-done = f32[1024,512]{1,0:T(8,128)} async-done(((f32[1024,4096]{1,0:T(8,128)}), f32[1024,512]{1,0:T(8,128)}) %reduce-scatter.20.cloned.1.call-update) | async-done | bytes 2097168 | tf_op jit(solution)/shard_map/reduce_scatter | solution.py:197
  761.1 153.2 %reduce-scatter.24.cloned.1.call-done = f32[1024,512]{1,0:T(8,128)} async-done(((f32[1024,4096]{1,0:T(8,128)}), f32[1024,512]{1,0:T(8,128)}) %reduce-scatter.24.cloned.1.call-update) | async-done | bytes 2097168 | tf_op jit(solution)/shard_map/reduce_scatter | solution.py:198
  917.1 229.3 %while.28 = (s32[]{:T(128)}, f32[1024,16,64]{0,2,1:T(8,128)}, f32[1024,16,64]{0,2,1:T(8,128)}, bf16[2,512,16,64]{1,3,2,0:T(8,128)(2,1)}, s32[2]{0:T(128)S(1)}, /...) while((s32[]{:T(128)}, f32[1024,16,64]{0,2,1:T(8,128)}, ...), condition=%wide.region_20.21_spmd.clone, body=%wide.region_18.20_spmd.clone.sunk | while | flops 5501347328 | bytes 375626592 | solution.py:98
  939.0 25.7 %multiply_reduce_fusion.13 = (f32[16,512]{1,0:T(8,128)S(1)}, f32[16,512,1024]{2,1,0:T(8,128)}) fusion(f32[16,512,1024]{2,1,0:T(8,128)} %fusion.145, f32[16,512]{1,0:T(8,128)S(1)} %dynamic-slice_bitcast_fusion.2, pred[512,1024]{1,0:T(8,128)(4,1)S(1)} %fusion.146, bf16[1024,16,64]{0,2,1:T(8,128)(2,1)S(1)} %copy-done.8, ...), kind=kOutput, calls=%fused_computation.18.clone.1 | convolution fusion | flops 1115676672 | bytes 70844416 | tf_op jit(solution)/shard_map/while/body/eval_jaxpr/qhd,khd->hqk/dot_general | solution.py:74
  964.7 28.0 %multiply_convert_fusion.6 = bf16[16,512,1024]{2,1,0:T(8,128)(2,1)} fusion(f32[16,512,1024]{2,1,0:T(8,128)} %get-tuple-element.477, f32[16,512,1024]{2,1,0:T(8,128)} %fusion.145, f32[16,512]{1,0:T(8,128)S(1)} %get-tuple-element.478, f32[16,512]{1,0:T(8,128)S(1)} %dynamic-slice_bitcast_fusion.2, pred[512,1024]{1,0:T(8,128)(4,1)S(1)} %fusion.146), kind=kLoop, calls=%fused_computation.17.clone.1 | loop fusion | flops 50331648 | bytes 84475904 | tf_op jit(solution)/shard_map/while/body/eval_jaxpr/convert_element_type | solution.py:84
  1013.3 18.0 %bitcast_add_fusion.5 = f32[1024,16,64]{0,2,1:T(8,128)} fusion(f32[1024,16,64]{0,2,1:T(8,128)} %get-tuple-element.528, f32[16,512,1024]{2,1,0:T(8,128)} %fusion.145, f32[16,512]{1,0:T(8,128)S(1)} %dynamic-slice_bitcast_fusion.2, pred[512,1024]{1,0:T(8,128)(4,1)S(1)} %fusion.146, pred[]{:T(512)S(6)} %compare.3, ...), kind=kOutput, calls=%fused_computation.23.clone.1 | convolution fusion | flops 1109393408 | bytes 43548676 | tf_op jit(solution)/shard_map/while/body/eval_jaxpr/hqk,qhd->khd/dot_general | solution.py:77
  1052.6 25.6 %multiply_reduce_fusion.13 = (f32[16,512]{1,0:T(8,128)S(1)}, f32[16,512,1024]{2,1,0:T(8,128)}) fusion(f32[16,512,1024]{2,1,0:T(8,128)} %fusion.145, f32[16,512]{1,0:T(8,128)S(1)} %dynamic-slice_bitcast_fusion.2, pred[512,1024]{1,0:T(8,128)(4,1)S(1)} %fusion.146, bf16[1024,16,64]{0,2,1:T(8,128)(2,1)S(1)} %copy-done.8, ...), kind=kOutput, calls=%fused_computation.18.clone.1 | convolution fusion | flops 1115676672 | bytes 70844416 | tf_op jit(solution)/shard_map/while/body/eval_jaxpr/qhd,khd->hqk/dot_general | solution.py:74
  1078.2 27.8 %multiply_convert_fusion.6 = bf16[16,512,1024]{2,1,0:T(8,128)(2,1)} fusion(f32[16,512,1024]{2,1,0:T(8,128)} %get-tuple-element.477, f32[16,512,1024]{2,1,0:T(8,128)} %fusion.145, f32[16,512]{1,0:T(8,128)S(1)} %get-tuple-element.478, f32[16,512]{1,0:T(8,128)S(1)} %dynamic-slice_bitcast_fusion.2, pred[512,1024]{1,0:T(8,128)(4,1)S(1)} %fusion.146), kind=kLoop, calls=%fused_computation.17.clone.1 | loop fusion | flops 50331648 | bytes 84475904 | tf_op jit(solution)/shard_map/while/body/eval_jaxpr/convert_element_type | solution.py:84
  1126.9 19.1 %bitcast_add_fusion.5 = f32[1024,16,64]{0,2,1:T(8,128)} fusion(f32[1024,16,64]{0,2,1:T(8,128)} %get-tuple-element.528, f32[16,512,1024]{2,1,0:T(8,128)} %fusion.145, f32[16,512]{1,0:T(8,128)S(1)} %dynamic-slice_bitcast_fusion.2, pred[512,1024]{1,0:T(8,128)(4,1)S(1)} %fusion.146, pred[]{:T(512)S(6)} %compare.3, ...), kind=kOutput, calls=%fused_computation.23.clone.1 | convolution fusion | flops 1109393408 | bytes 43548676 | tf_op jit(solution)/shard_map/while/body/eval_jaxpr/hqk,qhd->khd/dot_general | solution.py:77
  1226.1 39.9 %all-reduce = (f32[1024]{0:T(1024)}, f32[1024]{0:T(1024)}, f32[1024]{0:T(1024)}, f32[1024]{0:T(1024)}, f32[16]{0:T(128)}, /*index=5*/f32[1024]{0:T(1024)}, f32[1...) all-reduce(f32[1024]{0:T(1024)S(1)} %get-tuple-element.263, ...), channel_id=1, replica_groups=mesh['rows'=4,'ffn'=8] {'rows','ffn'}, use_global_device_ids=true, to_apply=%region_24.25 | all-reduce | flops 10256 | bytes 82048 | tf_op jit(solution)/shard_map/psum | solution.py:243
  1298.3 142.2 %reduce-scatter.16.cloned.1.call-done = f32[32,1024]{1,0:T(8,128)} async-done(((f32[1024,1024]{1,0:T(8,128)}), f32[32,1024]{1,0:T(8,128)}) %reduce-scatter.16.cloned.1.call-update) | async-done | bytes 131088 | tf_op jit(solution)/shard_map/reduce_scatter | solution.py:240
  1440.5 142.0 %reduce-scatter.14.cloned.1.call-done = f32[32,1024]{1,0:T(8,128)} async-done(((f32[1024,1024]{1,0:T(8,128)}), f32[32,1024]{1,0:T(8,128)}) %reduce-scatter.14.cloned.1.call-update) | async-done | bytes 131088 | tf_op jit(solution)/shard_map/reduce_scatter | solution.py:239
  1582.5 142.5 %reduce-scatter.18.cloned.1.call-done = f32[32,1024]{1,0:T(8,128)} async-done(((f32[1024,1024]{1,0:T(8,128)}), f32[32,1024]{1,0:T(8,128)}) %reduce-scatter.18.cloned.1.call-update) | async-done | bytes 131088 | tf_op jit(solution)/shard_map/reduce_scatter | solution.py:241
  (328 shorter events, 437.8 us)
Async XLA Ops:
  7.2 32.0 %all-gather.17.cloned.1.call-start = ((), (), s32[]{:S(2)}) async-start(), calls=%async_computation.13 | async-start | bytes 1310720 | tf_op jit(solution)/shard_map/all_gather | solution.py:162
  7.9 59.8 %all-gather.21.cloned.1.call-start = ((), (), s32[]{:S(2)}) async-start(), calls=%async_computation.15 | async-start | bytes 1310720 | tf_op jit(solution)/shard_map/all_gather | solution.py:163
  8.7 118.6 %all-gather.11.cloned.1.call-start = ((), (), s32[]{:S(2)}) async-start(), calls=%async_computation.10 | async-start | bytes 2162688 | tf_op jit(solution)/shard_map/all_gather | solution.py:139
  9.4 176.0 %all-gather.13.cloned.1.call-start = ((), (), s32[]{:S(2)}) async-start(), calls=%async_computation.11 | async-start | bytes 2162688 | tf_op jit(solution)/shard_map/all_gather | solution.py:140
  10.0 233.6 %all-gather.9.cloned.1.call-start = ((), (), s32[]{:S(2)}) async-start(), calls=%async_computation.9 | async-start | bytes 2162688 | tf_op jit(solution)/shard_map/all_gather | solution.py:138
  10.6 433.8 %all-gather.15.cloned.1.call-start = ((), (), s32[]{:S(2)}) async-start(), calls=%async_computation.12 | async-start | bytes 2162688 | tf_op jit(solution)/shard_map/all_gather | solution.py:141
  11.2 447.8 %all-gather.19.cloned.1.call-start = ((), (), s32[]{:S(2)}) async-start(), calls=%async_computation.14 | async-start | bytes 9437184 | tf_op jit(solution)/shard_map/all_gather | solution.py:166
  39.3 470.9 %all-gather.23.cloned.1.call-start = ((), (), s32[]{:S(2)}) async-start(), calls=%async_computation.16 | async-start | bytes 9437184 | tf_op jit(solution)/shard_map/all_gather | solution.py:167
  48.7 195.0 %copy-start.37 = (f32[1024]{0:T(1024)}, f32[1024]{0:T(1024)S(1)}, u32[]{:S(2)}) copy-start(f32[1024]{0:T(1024)S(1)} %broadcast_multiply_fusion.5) | copy-start | bytes 12292
  49.9 193.8 %copy-start.43 = (f32[1024]{0:T(1024)}, f32[1024]{0:T(1024)S(1)}, u32[]{:S(2)}) copy-start(f32[1024]{0:T(1024)S(1)} %fusion.52) | copy-start | bytes 12292
  67.8 117.7 %copy-start.75 = (f32[1024]{0:T(1024)S(1)}, f32[1024]{0:T(1024)}, u32[]{:S(2)}) copy-start(f32[1024]{0:T(1024)} %param.36) | copy-start | bytes 12292
  67.8 677.7 %reduce-scatter.20.cloned.1.call-start = ((), (), s32[]{:S(2)}) async-start(), calls=%async_computation.21 | async-start | bytes 18874368 | tf_op jit(solution)/shard_map/reduce_scatter | solution.py:197
  132.2 111.5 %copy-start.76 = (f32[1024]{0:T(1024)S(1)}, f32[1024]{0:T(1024)}, u32[]{:S(2)}) copy-start(f32[1024]{0:T(1024)} %param.33) | copy-start | bytes 12292
  578.4 335.9 %reduce-scatter.24.cloned.1.call-start = ((), (), s32[]{:S(2)}) async-start(), calls=%async_computation.23 | async-start | bytes 18874368 | tf_op jit(solution)/shard_map/reduce_scatter | solution.py:198
  592.9 673.1 %reduce-scatter.28.cloned.1.call-start = ((), (), s32[]{:S(2)}) async-start(), calls=%async_computation.25 | async-start | bytes 2359296
  631.5 646.9 %reduce-scatter.22.cloned.1.call-start = ((), (), s32[]{:S(2)}) async-start(), calls=%async_computation.22 | async-start | bytes 1310720 | tf_op jit(solution)/shard_map/reduce_scatter | solution.py:202
  748.2 532.1 %reduce-scatter.26.cloned.1.call-start = ((), (), s32[]{:S(2)}) async-start(), calls=%async_computation.24 | async-start | bytes 1310720 | tf_op jit(solution)/shard_map/reduce_scatter | solution.py:205
  759.1 158.0 %copy-start.2 = (bf16[1024,16,64]{0,2,1:T(8,128)(2,1)S(1)}, bf16[1024,16,64]{0,2,1:T(8,128)(2,1)}, u32[]{:S(2)}) copy-start(bf16[1024,16,64]{0,2,1:T(8,128)(2,1)} %copy-done.1) | copy-start | bytes 6291460
  759.1 158.0 %copy-start.26 = (f32[2,16,512]{2,1,0:T(8,128)S(1)}, f32[2,16,512]{2,1,0:T(8,128)}, u32[]{:S(2)}) copy-start(f32[2,16,512]{2,1,0:T(8,128)} %copy-done.25) | copy-start | bytes 196612
  759.1 158.0 %copy-start.81 = (s32[2]{0:T(128)S(1)}, s32[2]{0:T(128)}, u32[]{:S(2)}) copy-start(s32[2]{0:T(128)} %copy-done.80) | copy-start | bytes 28
  917.0 381.2 %reduce-scatter.12.cloned.1.call-start = ((), (), s32[]{:S(2)}) async-start(), calls=%async_computation.17 | async-start | bytes 4325376 | tf_op jit(solution)/shard_map/reduce_scatter | solution.py:238
  1156.8 283.7 %reduce-scatter.16.cloned.1.call-start = ((), (), s32[]{:S(2)}) async-start(), calls=%async_computation.19 | async-start | bytes 4325376 | tf_op jit(solution)/shard_map/reduce_scatter | solution.py:240
  1165.2 417.3 %reduce-scatter.14.cloned.1.call-start = ((), (), s32[]{:S(2)}) async-start(), calls=%async_computation.18 | async-start | bytes 4325376 | tf_op jit(solution)/shard_map/reduce_scatter | solution.py:239
  1173.5 551.5 %reduce-scatter.18.cloned.1.call-start = ((), (), s32[]{:S(2)}) async-start(), calls=%async_computation.20 | async-start | bytes 4325376 | tf_op jit(solution)/shard_map/reduce_scatter | solution.py:241
  (80 other events, 926.2 us)
Sparse Core Ops, SparseCore 0:
  9.9 29.3 all-gather.16
  41.1 26.6 all-gather.20
  70.7 56.4 all-gather.10
  130.1 55.3 all-gather.12
  188.3 55.3 all-gather.8
  246.5 55.3 all-gather.14
  303.5 80.9 all-gather.18
  386.0 80.5 all-gather.22
  578.5 166.8 reduce-scatter.19
  747.6 166.6 reduce-scatter.23
  916.6 34.2 reduce-scatter.27
  953.6 26.3 reduce-scatter.21
  983.2 27.7 reduce-scatter.25
  1156.9 141.2 reduce-scatter.11
  1301.0 139.5 reduce-scatter.15
  1443.2 139.2 reduce-scatter.13
  1585.2 139.7 reduce-scatter.17
where the time goes:
time: 1750 us; the launch traced here: 1730 us
  waiting for transfers between devices  924 us (53%)
  matrix products  420 us (24%)
  other arithmetic  171 us (10%)
  local copies, waits for them, and re-layouts  140 us (8%)
  blocking collectives  50.6 us (3%)
    reduce_scatter x1, waiting for transfers between devices, shards(): lax.psum_scatter(grad_down_full, 'ffn', scatter_dimension=1, tiled=True)  153 us
    reduce_scatter x1, waiting for transfers between devices, shards(): lax.psum_scatter(grad_out_weight, ('rows', 'ffn'), scatter_dimension=0, t...  143 us
    reduce_scatter x1, waiting for transfers between devices, shards(): lax.psum_scatter(grad_value_weight, ('rows', 'ffn'), scatter_dimension=0,...  142 us
    reduce_scatter x1, waiting for transfers between devices, shards(): lax.psum_scatter(grad_key_weight, ('rows', 'ffn'), scatter_dimension=0, t...  142 us
    reduce_scatter x1, waiting for transfers between devices, shards(): lax.psum_scatter(grad_up_full, 'ffn', scatter_dimension=1, tiled=True)  114 us
    dot_general x6, matrix products, plain_dot(): return jnp.dot(left, right, preferred_element_type=jnp.float32)  96.6 us
    dynamic_update_slice x4, local copies, waits for them, and re-layouts, attend_forward(): context, log_totals = lax.map(one_block, firsts)  83.5 us
    dot_general x4, matrix products, block_scores(): jnp.einsum('qhd,khd->hqk', rows_here, key_rows, preferred_element_type=jn...  67.1 us
  transfers between devices with their start and end apart: 17, of which 11 were waited for; matrix products, arithmetic and copies ran while one was open for 37% of the time, Pallas kernels for 0%

commit v1 on v0

v1 whole, which is shorter than its diff:
```python
import functools
import math

import jax
import jax.numpy as jnp
from jax import lax
from jax.experimental import pallas as pl
from jax.experimental.pallas import tpu as pltpu
from jax.sharding import PartitionSpec as P

epsilon = 1e-05
masked_score = -1e30
F32 = jnp.float32
BF16 = jnp.bfloat16
MIB = 1 << 20
BOTH = ("rows", "ffn")


def dot_nn(left, right):
    return lax.dot_general(left, right, (((1,), (0,)), ((), ())), preferred_element_type=F32)


def dot_nt(left, right):
    return lax.dot_general(left, right, (((1,), (1,)), ((), ())), preferred_element_type=F32)


def dot_tn(left, right):
    return lax.dot_general(left, right, (((0,), (0,)), ((), ())), preferred_element_type=F32)


def params(limit=56 * MIB, **kw):
    return pltpu.CompilerParams(vmem_limit_bytes=limit, **kw)


def whole(shape):
    return pl.BlockSpec(shape, lambda *_: (0,) * len(shape), pipeline_mode=pl.Buffered(1))


def out_whole(shape):
    return pl.BlockSpec(shape, lambda *_: (0,) * len(shape))


def sds(shape, dtype):
    return jax.ShapeDtypeStruct(shape, dtype)


def norm_parts(values):
    center = jnp.mean(values, axis=-1, keepdims=True)
    centered = values - center
    spread = jnp.mean(centered * centered, axis=-1, keepdims=True)
    inverse = lax.rsqrt(spread + epsilon)
    return centered * inverse, inverse


def norm_back(grad_hat, hat, inverse):
    return (
        grad_hat
        - jnp.mean(grad_hat, axis=-1, keepdims=True)
        - hat * jnp.mean(grad_hat * hat, axis=-1, keepdims=True)
    ) * inverse


def col_sum(values):
    return jnp.sum(values, axis=0, keepdims=True)


def qkv_kernel(x_ref, gain_ref, bias_ref, wq_ref, qb_ref, wk_ref, wv_ref, vb_ref, h_ref, q_ref, k_ref, v_ref, *, factor):
    hat, _ = norm_parts(x_ref[...].astype(F32))
    h = (hat * gain_ref[...] + bias_ref[...]).astype(BF16)
    h_ref[...] = h
    queries = (dot_nn(h, wq_ref[...]) + qb_ref[...]).astype(BF16)
    q_ref[...] = (queries.astype(F32) * factor).astype(BF16)
    k_ref[...] = dot_nn(h, wk_ref[...]).astype(BF16)
    v_ref[...] = (dot_nn(h, wv_ref[...]) + vb_ref[...]).astype(BF16)


def project_qkv(x, gain, bias, wq, qb, wk, wv, vb, factor, block):
    seq, width = x.shape
    rows = pl.BlockSpec((block, width), lambda i: (i, 0))
    vec = whole((1, width))
    mat = whole((width, width))
    return pl.pallas_call(
        functools.partial(qkv_kernel, factor=factor),
        grid=(seq // block,),
        in_specs=[rows, vec, vec, mat, vec, mat, mat, vec],
        out_specs=[rows] * 4,
        out_shape=[sds((seq, width), BF16)] * 4,
        compiler_params=params(),
        cost_estimate=pl.CostEstimate(
            flops=6 * seq * width * width, bytes_accessed=16 * seq * width, transcendentals=0
        ),
        name="project_qkv",
    )(x, gain, bias, wq, qb, wk, wv, vb)


def attend_kernel(length_ref, scale_ref, q_ref, k_ref, v_ref, c_ref, lse_ref, *, block, head):
    pair = pl.program_id(0)
    seq, lanes = q_ref.shape
    length = length_ref[0]
    lane = lax.broadcasted_iota(jnp.int32, (block, lanes), 1)
    for i in range(seq // block):
        keys_here = (i + 1) * block
        rows = slice(i * block, (i + 1) * block)
        q = q_ref[rows, :]
        k = k_ref[:keys_here, :]
        v = v_ref[:keys_here, :]
        key_pos = lax.broadcasted_iota(jnp.int32, (block, keys_here), 1)
        row_pos = lax.broadcasted_iota(jnp.int32, (block, keys_here), 0) + i * block
        allowed = key_pos < jnp.minimum(row_pos + 1, length)
        ctx = None
        totals = []
        for n in range(2):
            mine = (lane < head) if n == 0 else (lane >= head)
            scores = dot_nt(jnp.where(mine, q, 0), k)
            scores = jnp.where(allowed, scores, masked_score)
            peak = jnp.max(scores, axis=-1, keepdims=True)
            weights = jnp.exp(scores - peak)
            total = jnp.sum(weights, axis=-1, keepdims=True)
            part = dot_nn(weights.astype(BF16), v) * (scale_ref[2 * pair + n] / total)
            ctx = part if n == 0 else jnp.where(lane < head, ctx, part)
            totals.append(peak + jnp.log(total))
        c_ref[rows, :] = ctx.astype(BF16)
        lse_ref[0, rows, :] = jnp.where(lane < head, totals[0], totals[1])


def attend_forward(length, scale, q, k, v, block, head):
    seq, width = q.shape
    lanes = 2 * head
    cols = pl.BlockSpec((seq, lanes), lambda p: (0, p))
    smem = pl.BlockSpec(memory_space=pltpu.SMEM)
    pairs = width // lanes
    return pl.pallas_call(
        functools.partial(attend_kernel, block=block, head=head),
        grid=(pairs,),
        in_specs=[smem, smem, cols, cols, cols],
        out_specs=[cols, pl.BlockSpec((1, seq, lanes), lambda p: (p, 0, 0))],
        out_shape=[sds((seq, width), BF16), sds((pairs, seq, lanes), F32)],
        compiler_params=params(),
        cost_estimate=pl.CostEstimate(
            flops=8 * seq * seq * width, bytes_accessed=12 * seq * width, transcendentals=seq * seq * 16
        ),
        name="attend_forward",
    )(length, scale, q, k, v)


def attend_back_kernel(
    length_ref, q_ref, k_ref, v_ref, g_ref, lse_ref, inner_ref, dq_ref, dk_ref, dv_ref, dq_s, *, block, head, factor
):
    seq, lanes = q_ref.shape
    length = length_ref[0]
    lane_q = lax.broadcasted_iota(jnp.int32, (seq, lanes), 1)
    dq_s[...] = jnp.zeros_like(dq_s)
    q_all = q_ref[...]
    g_all = g_ref[...]
    zero = jnp.zeros_like(q_all)
    q_heads = [jnp.where(lane_q < head, q_all, zero), jnp.where(lane_q >= head, q_all, zero)]
    g_heads = [jnp.where(lane_q < head, g_all, zero), jnp.where(lane_q >= head, g_all, zero)]
    for j in range(seq // block):
        start = j * block
        width = seq - start
        k = k_ref[start : start + block, :]
        v = v_ref[start : start + block, :]
        key_pos = lax.broadcasted_iota(jnp.int32, (block, width), 0) + start
        row_pos = lax.broadcasted_iota(jnp.int32, (block, width), 1) + start
        allowed = (key_pos <= row_pos) & (key_pos < length)
        dk = dv = None
        dqs = []
        for n in range(2):
            q = q_heads[n][start:, :]
            g = g_heads[n][start:, :]
            scores = dot_nt(k, q)
            probs = jnp.where(allowed, jnp.exp(scores - lse_ref[0, n : n + 1, start:]), 0.0)
            grad_probs = dot_nt(v, g)
            grad_scores = (probs * (grad_probs - inner_ref[0, n : n + 1, start:])).astype(BF16)
            dv_part = dot_nn(probs.astype(BF16), g)
            dk_part = dot_nn(grad_scores, q)
            dv = dv_part if n == 0 else dv + dv_part
            dk = dk_part if n == 0 else dk + dk_part
            dqs.append(dot_tn(grad_scores, k))
        dq_s[start:, :] += jnp.where(lane_q[start:, :] < head, dqs[0], dqs[1])
        dk_ref[start : start + block, :] = dk.astype(BF16)
        dv_ref[start : start + block, :] = dv.astype(BF16)
    dq_ref[...] = (dq_s[...] * factor).astype(BF16)


def attend_backward(length, q, k, v, g, lse_rows, inner_rows, block, head, factor):
    seq, width = q.shape
    lanes = 2 * head
    cols = pl.BlockSpec((seq, lanes), lambda p: (0, p))
    smem = pl.BlockSpec(memory_space=pltpu.SMEM)
    pairs = width // lanes
    rowspec = pl.BlockSpec((1, 2, seq), lambda p: (p, 0, 0))
    return pl.pallas_call(
        functools.partial(attend_back_kernel, block=block, head=head, factor=factor),
        grid=(pairs,),
        in_specs=[smem, cols, cols, cols, cols, rowspec, rowspec],
        out_specs=[cols] * 3,
        out_shape=[sds((seq, width), BF16)] * 3,
        scratch_shapes=[pltpu.VMEM((seq, lanes), F32)],
        compiler_params=params(),
        cost_estimate=pl.CostEstimate(
            flops=20 * seq * seq * width, bytes_accessed=16 * seq * width, transcendentals=seq * seq * 16
        ),
        name="attend_backward",
    )(length, q, k, v, g, lse_rows, inner_rows)


def out_kernel(c_ref, w_ref, ob_ref, x_ref, pg_ref, pb_ref, fg_ref, fb_ref, o_ref, x2_ref, h2_ref):
    o = dot_nn(c_ref[...], w_ref[...]) + ob_ref[...]
    o_ref[...] = o
    hat, _ = norm_parts(o)
    x2 = x_ref[...].astype(F32) + (hat * pg_ref[...] + pb_ref[...])
    x2_ref[...] = x2
    hat2, _ = norm_parts(x2)
    h2_ref[...] = (hat2 * fg_ref[...] + fb_ref[...]).astype(BF16)


def out_forward(c, w, ob, x, pg, pb, fg, fb, block):
    seq, width = c.shape
    rows = pl.BlockSpec((block, width), lambda i: (i, 0))
    vec = whole((1, width))
    return pl.pallas_call(
        out_kernel,
        grid=(seq // block,),
        in_specs=[rows, whole((width, width)), vec, rows, vec, vec, vec, vec],
        out_specs=[rows] * 3,
        out_shape=[sds((seq, width), F32), sds((seq, width), F32), sds((seq, width), BF16)],
        compiler_params=params(),
        cost_estimate=pl.CostEstimate(flops=2 * seq * width * width, bytes_accessed=16 * seq * width, transcendentals=0),
        name="out_forward",
    )(c, w, ob, x, pg, pb, fg, fb)


def ffn_kernel(
    length_ref, h2_ref, ct_ref, x2_ref, wup_ref, wdn_ref, ub_ref, mg_ref, mb_ref, db_ref,
    res_ref, dh2_ref, m_ref, du_ref, gub_ref, gmg_ref, gmb_ref, gdb_ref,
    e_s, gp_s, dm_s,
):
    step = pl.program_id(0)
    block, width = h2_ref.shape
    nb, _, hb = wup_ref.shape
    units = nb * hb
    row = lax.broadcasted_iota(jnp.int32, (block, width), 0) + step * block
    valid = row < length_ref[0]
    h2 = h2_ref[...]
    dfr = jnp.where(valid, ct_ref[...].astype(F32), 0.0).astype(BF16)

    @pl.when(step == 0)
    def _():
        gub_ref[...] = jnp.zeros_like(gub_ref)
        gmg_ref[...] = jnp.zeros_like(gmg_ref)
        gmb_ref[...] = jnp.zeros_like(gmb_ref)
        gdb_ref[...] = jnp.zeros_like(gdb_ref)

    gdb_ref[...] += col_sum(dfr.astype(F32))

    def first(j, sums):
        u = dot_nn(h2, wup_ref[j]) + ub_ref[j]
        dm = dot_nn(dfr, wdn_ref[j])
        cdf = 0.5 * (1.0 + lax.erf(u * math.sqrt(0.5)))
        e = u * cdf
        gp = cdf + u * (jnp.exp(u * u * -0.5) * (1.0 / math.sqrt(2.0 * math.pi)))
        dmh = dm * mg_ref[j]
        e_s[j] = e
        gp_s[j] = gp
        dm_s[j] = dm
        terms = (e, e * e, dmh, dmh * e)
        return tuple(s + jnp.sum(t, axis=-1, keepdims=True) for s, t in zip(sums, terms))

    zero = jnp.zeros((block, 1), F32)
    sum_e, sum_ee, sum_d, sum_de = lax.fori_loop(0, nb, first, (zero,) * 4)
    mu = sum_e / units
    inverse = lax.rsqrt(sum_ee / units - mu * mu + epsilon)
    mean_d = sum_d / units
    mean_dh = (sum_de - mu * sum_d) * inverse / units

    def second(j, sums):
        f, dh2 = sums
        ehat = (e_s[j] - mu) * inverse
        dm = dm_s[j]
        m = (ehat * mg_ref[j] + mb_ref[j]).astype(BF16)
        m_ref[j] = m
        f = f + dot_nt(m, wdn_ref[j])
        de = (dm * mg_ref[j] - mean_d - ehat * mean_dh) * inverse
        du = (de * gp_s[j]).astype(BF16)
        du_ref[j] = du
        dh2 = dh2 + dot_nt(du, wup_ref[j])
        gub_ref[j] += col_sum(du.astype(F32))
        gmg_ref[j] += col_sum(dm * ehat)
        gmb_ref[j] += col_sum(dm)
        return f, dh2

    zeros = jnp.zeros((block, width), F32)
    f, dh2 = lax.fori_loop(0, nb, second, (zeros, zeros))
    res_ref[...] = jnp.where(valid, x2_ref[...] + f + db_ref[...], 0.0)
    dh2_ref[...] = dh2


def feed_forward(length, h2, ct, x2, wup, wdn, ub, mg, mb, db, block):
    seq, width = h2.shape
    nb, _, hb = wup.shape
    rows = pl.BlockSpec((block, width), lambda i: (i, 0))
    smem = pl.BlockSpec(memory_space=pltpu.SMEM)
    units = whole((nb, 1, hb))
    blocks = pl.BlockSpec((nb, block, hb), lambda i: (0, i, 0))
    sums = out_whole((nb, 1, hb))
    return pl.pallas_call(
        ffn_kernel,
        grid=(seq // block,),
        in_specs=[
            smem, rows, rows, rows, whole((nb, width, hb)), whole((nb, width, hb)),
            units, units, units, whole((1, width)),
        ],
        out_specs=[rows, rows, blocks, blocks, sums, sums, sums, out_whole((1, width))],
        out_shape=[
            sds((seq, width), F32), sds((seq, width), F32), sds((nb, seq, hb), BF16), sds((nb, seq, hb), BF16),
            sds((nb, 1, hb), F32), sds((nb, 1, hb), F32), sds((nb, 1, hb), F32), sds((1, width), F32),
        ],
        scratch_shapes=[pltpu.VMEM((nb, block, hb), F32)] * 3,
        compiler_params=params(60 * MIB),
        cost_estimate=pl.CostEstimate(
            flops=16 * seq * width * nb * hb, bytes_accessed=60 * MIB, transcendentals=2 * seq * nb * hb
        ),
        name="feed_forward",
    )(length, h2, ct, x2, wup, wdn, ub, mg, mb, db)


def ffn_weights_kernel(length_ref, h2_ref, ct_ref, m_ref, du_ref, gup_ref, gdn_ref, h2t_s, dft_s):
    seq, width = h2_ref.shape

    @pl.when(pl.program_id(0) == 0)
    def _():
        row = lax.broadcasted_iota(jnp.int32, (seq, width), 0)
        dfr = jnp.where(row < length_ref[0], ct_ref[...], 0)
        h2t_s[...] = h2_ref[...].T
        dft_s[...] = dfr.T

    gdn_ref[0] = dot_nn(dft_s[...], m_ref[0]).astype(BF16)
    gup_ref[0] = dot_nn(h2t_s[...], du_ref[0]).astype(BF16)


def ffn_weight_grads(length, h2, ct, m, du):
    seq, width = h2.shape
    nb, _, hb = m.shape
    smem = pl.BlockSpec(memory_space=pltpu.SMEM)
    block = pl.BlockSpec((1, seq, hb), lambda j: (j, 0, 0))
    out = pl.BlockSpec((1, width, hb), lambda j: (j, 0, 0))
    return pl.pallas_call(
        ffn_weights_kernel,
        grid=(nb,),
        in_specs=[smem, whole((seq, width)), whole((seq, width)), block, block],
        out_specs=[out, out],
        out_shape=[sds((nb, width, hb), BF16)] * 2,
        scratch_shapes=[pltpu.VMEM((width, seq), BF16)] * 2,
        compiler_params=params(),
        cost_estimate=pl.CostEstimate(
            flops=4 * seq * width * nb * hb, bytes_accessed=36 * MIB, transcendentals=0
        ),
        name="ffn_weight_grads",
    )(length, h2, ct, m, du)


def out_back_kernel(
    length_ref, dh2_ref, ct_ref, x2_ref, o_ref, c_ref, w_ref, fg_ref, pg_ref, hs_ref,
    dx2_ref, dor_ref, g_ref, dcc_ref, gfg_ref, gfb_ref, gpg_ref, gpb_ref, gob_ref,
):
    step = pl.program_id(0)
    block, width = dh2_ref.shape
    row = lax.broadcasted_iota(jnp.int32, (block, width), 0) + step * block
    dy = jnp.where(row < length_ref[0], ct_ref[...].astype(F32), 0.0)

    @pl.when(step == 0)
    def _():
        for ref in (gfg_ref, gfb_ref, gpg_ref, gpb_ref, gob_ref):
            ref[...] = jnp.zeros_like(ref)

    dh2 = dh2_ref[...]
    hat2, inverse2 = norm_parts(x2_ref[...])
    gfg_ref[...] += col_sum(dh2 * hat2)
    gfb_ref[...] += col_sum(dh2)
    dx2 = dy + norm_back(dh2 * fg_ref[...], hat2, inverse2)
    dx2_ref[...] = dx2
    hat, inverse = norm_parts(o_ref[...])
    gpg_ref[...] += col_sum(dx2 * hat)
    gpb_ref[...] += col_sum(dx2)
    dor = norm_back(dx2 * pg_ref[...], hat, inverse).astype(BF16)
    dor_ref[...] = dor
    gob_ref[...] += col_sum(dor.astype(F32))
    dc = dot_nt(dor, w_ref[...])
    g_ref[...] = (dc * hs_ref[...]).astype(BF16)
    dcc_ref[...] = dc * c_ref[...].astype(F32)


def out_backward(length, dh2, ct, x2, o, c, w, fg, pg, hs, block):
    seq, width = dh2.shape
    rows = pl.BlockSpec((block, width), lambda i: (i, 0))
    smem = pl.BlockSpec(memory_space=pltpu.SMEM)
    vec = whole((1, width))
    ovec = out_whole((1, width))
    return pl.pallas_call(
        out_back_kernel,
        grid=(seq // block,),
        in_specs=[smem, rows, rows, rows, rows, rows, whole((width, width)), vec, vec, vec],
        out_specs=[rows] * 4 + [ovec] * 5,
        out_shape=[
            sds((seq, width), F32), sds((seq, width), BF16), sds((seq, width), BF16), sds((seq, width), F32),
        ] + [sds((1, width), F32)] * 5,
        compiler_params=params(),
        cost_estimate=pl.CostEstimate(flops=2 * seq * width * width, bytes_accessed=30 * seq * width, transcendentals=0),
        name="out_backward",
    )(length, dh2, ct, x2, o, c, w, fg, pg, hs)


def weights_kernel(left_ref, right_ref, out_ref, left_s):
    @pl.when(pl.program_id(0) == 0)
    def _():
        left_s[...] = left_ref[...].T

    out_ref[...] = dot_nn(left_s[...], right_ref[...]).astype(BF16)


def weight_grad(left, right, block):
    seq, width = left.shape
    cols = right.shape[1]
    return pl.pallas_call(
        weights_kernel,
        grid=(cols // block,),
        in_specs=[whole((seq, width)), pl.BlockSpec((seq, block), lambda j: (0, j))],
        out_specs=pl.BlockSpec((width, block), lambda j: (0, j)),
        out_shape=sds((width, cols), BF16),
        scratch_shapes=[pltpu.VMEM((width, seq), BF16)],
        compiler_params=params(),
        cost_estimate=pl.CostEstimate(flops=2 * seq * width * cols, bytes_accessed=6 * seq * cols, transcendentals=0),
        name="weight_grad",
    )(left, right)


def input_kernel(
    dq_ref, dk_ref, dv_ref, wq_ref, wk_ref, wv_ref, x_ref, dx2_ref, gain_ref,
    dx_ref, gg_ref, gb_ref, gqb_ref, gvb_ref,
):
    @pl.when(pl.program_id(0) == 0)
    def _():
        for ref in (gg_ref, gb_ref, gqb_ref, gvb_ref):
            ref[...] = jnp.zeros_like(ref)

    dq, dk, dv = dq_ref[...], dk_ref[...], dv_ref[...]
    dh = dot_nt(dq, wq_ref[...]) + dot_nt(dk, wk_ref[...]) + dot_nt(dv, wv_ref[...])
    hat, inverse = norm_parts(x_ref[...].astype(F32))
    gg_ref[...] += col_sum(dh * hat)
    gb_ref[...] += col_sum(dh)
    gqb_ref[...] += col_sum(dq.astype(F32))
    gvb_ref[...] += col_sum(dv.astype(F32))
    dx_ref[...] = dx2_ref[...] + norm_back(dh * gain_ref[...], hat, inverse)


def input_grad(dq, dk, dv, wq, wk, wv, x, dx2, gain, block):
    seq, width = dq.shape
    rows = pl.BlockSpec((block, width), lambda i: (i, 0))
    mat = whole((width, width))
    ovec = out_whole((1, width))
    return pl.pallas_call(
        input_kernel,
        grid=(seq // block,),
        in_specs=[rows, rows, rows, mat, mat, mat, rows, rows, whole((1, width))],
        out_specs=[rows] + [ovec] * 4,
        out_shape=[sds((seq, width), F32)] + [sds((1, width), F32)] * 4,
        compiler_params=params(),
        cost_estimate=pl.CostEstimate(flops=6 * seq * width * width, bytes_accessed=22 * seq * width, transcendentals=0),
        name="input_grad",
    )(dq, dk, dv, wq, wk, wv, x, dx2, gain)


def gather_rows(parts):
    n = len(parts)
    width = parts[0].shape[1]
    whole_rows = lax.all_gather(jnp.concatenate(parts, axis=1), BOTH, axis=0, tiled=True)
    return [whole_rows[:, i * width : (i + 1) * width] for i in range(n)]


def gather_blocks(shard):
    over_ffn = lax.all_gather(shard, "ffn", axis=0, tiled=False)
    return lax.all_gather(over_ffn, "rows", axis=1, tiled=True)


def widen(blocks, lanes):
    nb, rows, hb = blocks.shape
    group = max(1, lanes // hb)
    if group == 1:
        return blocks
    return blocks.reshape(nb // group, group, rows, hb).transpose(0, 2, 1, 3).reshape(nb // group, rows, group * hb)


def narrow(blocks, hb):
    nb, rows, lanes = blocks.shape
    group = lanes // hb
    if group == 1:
        return blocks
    return blocks.reshape(nb, rows, group, hb).transpose(0, 2, 1, 3).reshape(nb * group, rows, hb)


def scatter_blocks(grad):
    mine = lax.psum_scatter(grad, "rows", scatter_dimension=1, tiled=True)
    return lax.psum_scatter(mine, "ffn", scatter_dimension=0, tiled=False).astype(F32)


def rows_of(vector):
    return vector.reshape(1, -1)


def shards(
    tokens, lengths, cotangent, ln_attn_gain, ln_attn_bias, w_query, query_bias, w_key, w_value, value_bias,
    head_scale, w_out, out_bias, post_gain, post_bias, ffn_gain, ffn_bias, w_up, up_bias, mid_gain, mid_bias,
    w_down, down_bias,
):
    seq, width = tokens.shape
    heads = head_scale.shape[0]
    head = width // heads
    factor = head ** (-0.5)
    block = min(seq, 256)
    wq, wk, wv, wo = gather_rows([w_query, w_key, w_value, w_out])
    own_units = w_up.shape[1]
    wup = widen(gather_blocks(w_up), 512)
    wdn = widen(gather_blocks(w_down), 512)
    nb, _, hb = wup.shape
    h, q, k, v = project_qkv(
        tokens, rows_of(ln_attn_gain), rows_of(ln_attn_bias), wq, rows_of(query_bias), wk, wv, rows_of(value_bias),
        factor, block,
    )
    c, lse = attend_forward(lengths, head_scale, q, k, v, block, head)
    o, x2, h2 = out_forward(
        c, wo, rows_of(out_bias), tokens, rows_of(post_gain), rows_of(post_bias), rows_of(ffn_gain),
        rows_of(ffn_bias), block,
    )
    units = lambda vector: vector.reshape(nb, 1, hb)
    result, dh2, m, du, g_ub, g_mg, g_mb, g_db = feed_forward(
        lengths, h2, cotangent, x2, wup, wdn, units(up_bias), units(mid_gain), units(mid_bias), rows_of(down_bias),
        block,
    )
    g_up, g_dn = ffn_weight_grads(lengths, h2, cotangent, m, du)
    scale_cols = rows_of(jnp.repeat(head_scale, head))
    dx2, dor, g, dcc, g_fg, g_fb, g_pg, g_pb, g_ob = out_backward(
        lengths, dh2, cotangent, x2, o, c, wo, rows_of(ffn_gain), rows_of(post_gain), scale_cols, block
    )
    inner = jnp.sum(dcc.reshape(seq, heads, head), axis=-1)
    g_hs = jnp.sum(inner, axis=0) / head_scale
    inner_rows = inner.T.reshape(heads // 2, 2, seq)
    lse_rows = jnp.stack([lse[:, :, 0], lse[:, :, head]], axis=1)
    dq, dk, dv = attend_backward(lengths, q, k, v, g, lse_rows, inner_rows, block, head, factor)
    g_wo = weight_grad(c, dor, 512)
    g_wq, g_wk, g_wv = (weight_grad(h, part, 512) for part in (dq, dk, dv))
    dx, g_lg, g_lb, g_qb, g_vb = input_grad(dq, dk, dv, wq, wk, wv, tokens, dx2, rows_of(ln_attn_gain), block)
    grad_up = scatter_blocks(narrow(g_up, own_units))
    grad_down = scatter_blocks(narrow(g_dn, own_units))
    stacked = narrow(jnp.concatenate([g_ub, g_mg, g_mb], axis=1), own_units)
    stacked = lax.psum(lax.psum_scatter(stacked, "ffn", scatter_dimension=0, tiled=False), "rows")
    attn = lax.psum_scatter(
        jnp.concatenate([g_wq, g_wk, g_wv, g_wo], axis=1), BOTH, scatter_dimension=0, tiled=True
    ).astype(F32)
    small = jnp.concatenate(
        [g_lg, g_lb, g_qb, g_vb, g_ob, g_pg, g_pb, g_fg, g_fb, g_db, jnp.pad(rows_of(g_hs), ((0, 0), (0, width - heads)))],
        axis=0,
    )
    small = lax.psum(small, BOTH)
    return (
        result, dx, small[0], small[1], attn[:, :width], small[2], attn[:, width : 2 * width],
        attn[:, 2 * width : 3 * width], small[3], small[10, :heads], attn[:, 3 * width :], small[4], small[5],
        small[6], small[7], small[8], grad_up, stacked[0], stacked[1], stacked[2], grad_down, small[9],
    )


def solution(mesh):
    split = P(BOTH, None)
    tiles = P("rows", "ffn")
    one = P()
    return jax.shard_map(
        shards,
        mesh=mesh,
        in_specs=(
            split, P(BOTH), split, one, one, split, one, split, split, one, one, split, one, one, one, one, one,
            tiles, one, one, one, tiles, one,
        ),
        out_specs=(
            split, split, one, one, split, one, split, split, one, one, split, one, one, one, one, one,
            tiles, P("ffn"), P("ffn"), P("ffn"), tiles, one,
        ),
        check_vma=False,
    )
```

time: 1750 us -> 848 us (0.48)
  waiting for transfers between devices: 924 us -> 463 us
  matrix products: 420 us -> 0 us
  Pallas kernels: 0 us -> 249 us
  other arithmetic: 171 us -> 17.1 us
  local copies, waits for them, and re-layouts: 140 us -> 25.2 us
  blocking collectives: 50.6 us -> 77 us
    reduce_scatter x8 -> x5, waiting for transfers between devices: 710 us -> 202 us  [the longest x2 76 us: scatter_blocks(): mine = lax.psum_scatter(grad, 'rows', scatter_dimension=1, tiled=True)]
    dot_general x32 -> x0, matrix products: 420 us -> none  [the longest x6 96.6 us: plain_dot(): return jnp.dot(left, right, preferred_element_type=jnp.float32)]
    pallas_call x0 -> x12, Pallas kernels: none -> 249 us  [the longest x1 81.3 us: feed_forward(): pl.pallas_call(ffn_kernel, grid=(seq // block,), in_specs=[smem, rows, ro...]
    reduce_sum x18 -> x3, other arithmetic: 91 us -> 5.47 us  [the longest x1 2.88 us: shards(): inner = jnp.sum(dcc.reshape(seq, heads, head), axis=-1)]
    dynamic_update_slice x4 -> x0, local copies, waits for them, and re-layouts: 83.5 us -> none  [attend_forward(): context, log_totals = lax.map(one_block, firsts)]
    convert_element_type x8 -> x2, other arithmetic: 69.3 us -> 3.61 us  [scatter_blocks(): lax.psum_scatter(mine, 'ffn', scatter_dimension=0, tiled=False).astype(F32)]
    all_gather x8 -> x5, waiting for transfers between devices: 211 us -> 259 us  [the longest x2 118 us: gather_blocks(): return lax.all_gather(over_ffn, 'rows', axis=1, tiled=True)]
    unnamed x164 -> x29, local copies, waits for them, and re-layouts: 40.9 us -> 0.67 us
  transfers between devices with their start and end apart: 17 -> 10, of which waited for: 11 -> 9; matrix products, arithmetic and copies ran while one was open for 37% -> 5% of each run, Pallas kernels for 0% -> 17%
where the time goes in v1:
time: 848 us; the launch traced here: 847 us
  waiting for transfers between devices  463 us (55%)
  Pallas kernels  249 us (29%)
  blocking collectives  77 us (9%)
  local copies, waits for them, and re-layouts  25.2 us (3%)
  other arithmetic  17.1 us (2%)
  between operations  15.1 us (2%)
    all_gather x2, waiting for transfers between devices, gather_blocks(): return lax.all_gather(over_ffn, 'rows', axis=1, tiled=True)  118 us
    pallas_call x1, Pallas kernels, feed_forward(): pl.pallas_call(ffn_kernel, grid=(seq // block,), in_specs=[smem, rows, ro...  81.3 us
    all_gather x1, waiting for transfers between devices, gather_rows(): lax.all_gather(jnp.concatenate(parts, axis=1), BOTH, axis=0, tiled=True)  79.6 us
    reduce_scatter x2, waiting for transfers between devices, scatter_blocks(): mine = lax.psum_scatter(grad, 'rows', scatter_dimension=1, tiled=True)  76 us
    reduce_scatter x2, waiting for transfers between devices, scatter_blocks(): lax.psum_scatter(mine, 'ffn', scatter_dimension=0, tiled=False).astype(F32)  69.7 us
    all_gather x2, waiting for transfers between devices, gather_blocks(): over_ffn = lax.all_gather(shard, 'ffn', axis=0, tiled=False)  61.2 us
    reduce_scatter x1, waiting for transfers between devices, shards(): lax.psum_scatter(jnp.concatenate([g_wq, g_wk, g_wv, g_wo], axis=1), BOTH,...  55.8 us
    psum x1, blocking collectives, shards(): small = lax.psum(small, BOTH)  38.1 us
  transfers between devices with their start and end apart: 10, of which 9 were waited for; matrix products, arithmetic and copies ran while one was open for 5% of the time, Pallas kernels for 17%

profile of v1, /device:TPU:0, one launch (start us, length us, event | category | flops | bytes accessed | tf_op | source)
XLA Modules:
  0.0 847.1 jit_solution(10258411322052132413)
XLA Ops:
  10.5 31.0 %all-gather.14.cloned.1.call-done = bf16[2048,512]{1,0:T(8,128)(2,1)} async-done(((bf16[256,512]{1,0:T(8,128)(2,1)}), bf16[2048,512]{1,0:T(8,128)(2,1)}) %all-gather.14.cloned.1.call-update) | async-done | bytes 2097168 | tf_op jit(solution)/shard_map/all_gather | solution.py:482
  41.5 30.2 %all-gather.16.cloned.1.call-done = bf16[2048,512]{1,0:T(8,128)(2,1)} async-done(((bf16[256,512]{1,0:T(8,128)(2,1)}), bf16[2048,512]{1,0:T(8,128)(2,1)}) %all-gather.16.cloned.1.call-update) | async-done | bytes 2097168 | tf_op jit(solution)/shard_map/all_gather | solution.py:482
  72.4 79.6 %all-gather.8.cloned.1.call-done = bf16[1024,4096]{1,0:T(8,128)(2,1)} async-done(((bf16[32,4096]{1,0:T(8,128)(2,1)}), bf16[1024,4096]{1,0:T(8,128)(2,1)}) %all-gather.8.cloned.1.call-update) | async-done | bytes 8388624 | tf_op jit(solution)/shard_map/all_gather | solution.py:477
  152.0 6.1 fusion
  158.2 13.6 %project_qkv.1 = (bf16[1024,1024]{1,0:T(8,128)(2,1)}, bf16[1024,1024]{1,0:T(8,128)(2,1)}, bf16[1024,1024]{1,0:T(8,128)(2,1)}, bf16[1024,1024]{1,0:T(8,128)(2,1)}) custom-call(bf16[1024,1024]{1,0:T(8,128)(2,1)} %x_ref.5, f32[1,1024]{1,0:T(1,128)} %bitcast.78, f32[1,1024]{1,0:T(1,128)} %bitcast.71, bf16[1024,1024]{1,0:T(8,128)(2,1)} %get-tuple-element.97.wq_ref, ...), custom_call_target="tpu_custom_call" | custom-call | flops 6442450944 | bytes 16777216 | tf_op jit(solution)/shard_map/project_qkv/pallas_call | solution.py:82
  171.7 30.5 %attend_forward.1 = (bf16[1024,1024]{1,0:T(8,128)(2,1)}, f32[8,1024,128]{2,1,0:T(8,128)}) custom-call(s32[1]{0:T(128)S(6)} %copy.56.length_ref, f32[16]{0:T(128)} %scale_ref.1, bf16[1024,1024]{1,0:T(8,128)(2,1)} %get-tuple-element.58.q_ref, bf16[1024,1024]{1,0:T(8,128)(2,1)} %get-tuple-element.59.k_ref, bf16[1024,1024]{1,0:T(8,128)(2,1)} %get-tuple-element.60.v_ref), custom_call_target="tpu_custom_call" | custom-call | flops 8589934592 | bytes 12582912 | tf_op jit(solution)/shard_map/attend_forward/pallas_call | solution.py:132
  202.2 9.2 %out_forward.1 = (f32[1024,1024]{1,0:T(8,128)}, f32[1024,1024]{1,0:T(8,128)}, bf16[1024,1024]{1,0:T(8,128)(2,1)}) custom-call(bf16[1024,1024]{1,0:T(8,128)(2,1)} %get-tuple-element.61.c_ref.left_ref, bf16[1024,1024]{1,0:T(8,128)(2,1)} %get-tuple-element.94.w_ref, f32[1,1024]{1,0:T(1,128)} %bitcast.74, bf16[1024,1024]{1,0:T(8,128)(2,1)} %x_ref.5, ...), custom_call_target="tpu_custom_call" | custom-call | flops 2147483648 | bytes 16777216 | tf_op jit(solution)/shard_map/out_forward/pallas_call | solution.py:222
  211.5 28.5 %all-gather.10.cloned.1.call-done.wup_ref = bf16[8,1024,512]{2,1,0:T(8,128)(2,1)} async-done(((bf16[8,256,512]{2,1,0:T(8,128)(2,1)}), bf16[8,1024,512]{2,1,0:T(8,128)(2,1)}) %all-gather.10.cloned.1.call-update) | async-done | bytes 8388624 | tf_op jit(solution)/shard_map/all_gather | solution.py:483
  240.0 89.3 %all-gather.12.cloned.1.call-done.wdn_ref = bf16[8,1024,512]{2,1,0:T(8,128)(2,1)} async-done(((bf16[8,256,512]{2,1,0:T(8,128)(2,1)}), bf16[8,1024,512]{2,1,0:T(8,128)(2,1)}) %all-gather.12.cloned.1.call-update) | async-done | bytes 8388624 | tf_op jit(solution)/shard_map/all_gather | solution.py:483
  329.3 81.3 %feed_forward.1 = (f32[1024,1024]{1,0:T(8,128)}, f32[1024,1024]{1,0:T(8,128)}, bf16[8,1024,512]{2,1,0:T(8,128)(2,1)}, bf16[8,1024,512]{2,1,0:T(8,128)(2,1)}, f32...) custom-call(s32[1]{0:T(128)S(6)} %copy.56.length_ref, ...), custom_call_target="tpu_custom_call" | custom-call | flops 68719476736 | bytes 62914560 | tf_op jit(solution)/shard_map/feed_forward/pallas_call | solution.py:307
  410.6 24.0 %ffn_weight_grads.1 = (bf16[8,1024,512]{2,1,0:T(8,128)(2,1)}, bf16[8,1024,512]{2,1,0:T(8,128)(2,1)}) custom-call(s32[1]{0:T(128)S(6)} %copy.56.length_ref, bf16[1024,1024]{1,0:T(8,128)(2,1)} %get-tuple-element.62.h2_ref, bf16[1024,1024]{1,0:T(8,128)(2,1)} %ct_ref.5, bf16[8,1024,512]{2,1,0:T(8,128)(2,1)} %get-tuple-element.87.m_ref, ...), custom_call_target="tpu_custom_call" | custom-call | flops 17179869184 | bytes 37748736 | tf_op jit(solution)/shard_map/ffn_weight_grads/pallas_call | solution.py:348
  443.5 15.2 %out_backward.1 = (f32[1024,1024]{1,0:T(8,128)}, bf16[1024,1024]{1,0:T(8,128)(2,1)}, bf16[1024,1024]{1,0:T(8,128)(2,1)}, f32[1024,1024]{1,0:T(8,128)}, f32[1,102...) custom-call(s32[1]{0:T(128)S(6)} %copy.56.length_ref, ...), custom_call_target="tpu_custom_call" | custom-call | flops 2147483648 | bytes 31457280 | tf_op jit(solution)/shard_map/out_backward/pallas_call | solution.py:400
  473.9 35.9 %attend_backward.1 = (bf16[1024,1024]{1,0:T(8,128)(2,1)}, bf16[1024,1024]{1,0:T(8,128)(2,1)}, bf16[1024,1024]{1,0:T(8,128)(2,1)}) custom-call(s32[1]{0:T(128)S(6)} %copy.56.length_ref, bf16[1024,1024]{1,0:T(8,128)(2,1)} %get-tuple-element.58.q_ref, bf16[1024,1024]{1,0:T(8,128)(2,1)} %get-tuple-element.59.k_ref, bf16[1024,1024]{1,0:T(8,128)(2,1)} %get-tuple-element.60.v_ref, ...), custom_call_target="tpu_custom_call" | custom-call | flops 21474836480 | bytes 16777216 | tf_op jit(solution)/shard_map/attend_backward/pallas_call | solution.py:193
  509.8 6.2 weight_grad.6
  516.0 6.1 weight_grad.5
  522.1 6.5 weight_grad.4
  535.0 76.0 %reduce-scatter.8.cloned.1.call-done = bf16[8,256,512]{2,1,0:T(8,128)(2,1)} async-done(((bf16[8,1024,512]{2,1,0:T(8,128)(2,1)}), bf16[8,256,512]{2,1,0:T(8,128)(2,1)}) %reduce-scatter.8.cloned.1.call-update) | async-done | bytes 2097168 | tf_op jit(solution)/shard_map/reduce_scatter | solution.py:503
  614.4 14.6 %input_grad.1 = (f32[1024,1024]{1,0:T(8,128)}, f32[1,1024]{1,0:T(1,128)}, f32[1,1024]{1,0:T(1,128)}, f32[1,1024]{1,0:T(1,128)}, f32[1,1024]{1,0:T(1,128)}) custom-call(bf16[1024,1024]{1,0:T(8,128)(2,1)} %get-tuple-element.70.dq_ref.right_ref, bf16[1024,1024]{1,0:T(8,128)(2,1)} %get-tuple-element.71.dk_ref.right_ref, ...), custom_call_target="tpu_custom_call" | custom-call | flops 6442450944 | bytes 23068672 | tf_op jit(solution)/shard_map/input_grad/pallas_call | solution.py:462
  630.0 29.5 %all-reduce.1 = f32[8,3,512]{2,1,0:T(4,128)S(1)} all-reduce(f32[8,3,512]{2,1,0:T(4,128)S(1)} %pad_maximum_fusion.3), channel_id=7, replica_groups=mesh['rows'=4,'ffn'=8] {'ffn'}, use_global_device_ids=true, to_apply=%region_7.0.clone | all-reduce | flops 12288 | bytes 98304
  660.2 9.4 %psum.15 = f32[3,512]{1,0:T(4,128)S(1)} all-reduce(f32[3,512]{1,0:T(4,128)S(1)} %dynamic-slice_bitcast_fusion), channel_id=1, replica_groups=mesh['rows'=4,'ffn'=8] {'rows'}, use_global_device_ids=true, to_apply=%region_8.0 | all-reduce | flops 1536 | bytes 12288 | tf_op jit(solution)/shard_map/psum | solution.py:556
  669.6 38.1 %psum.14 = f32[11,1024]{1,0:T(8,128)S(1)} all-reduce(f32[11,1024]{1,0:T(8,128)S(1)} %concatenate.13), channel_id=1, replica_groups=mesh['rows'=4,'ffn'=8] {'rows','ffn'}, use_global_device_ids=true, to_apply=%region_3.0 | all-reduce | flops 11264 | bytes 90112 | tf_op jit(solution)/shard_map/psum | solution.py:564
  709.4 55.8 %reduce-scatter.6.cloned.1.call-done = bf16[32,4096]{1,0:T(8,128)(2,1)} async-done(((bf16[1024,4096]{1,0:T(8,128)(2,1)}), bf16[32,4096]{1,0:T(8,128)(2,1)}) %reduce-scatter.6.cloned.1.call-update) | async-done | bytes 262160 | tf_op jit(solution)/shard_map/reduce_scatter | solution.py:557
  767.0 34.8 %reduce-scatter.14.cloned.1.call-done = bf16[1,256,512]{2,1,0:T(8,128)(2,1)} async-done(((bf16[8,256,512]{2,1,0:T(8,128)(2,1)}), bf16[1,256,512]{2,1,0:T(8,128)(2,1)}) %reduce-scatter.14.cloned.1.call-update) | async-done | bytes 262160 | tf_op jit(solution)/shard_map/reduce_scatter | solution.py:504
  803.6 34.9 %reduce-scatter.10.cloned.1.call-done = bf16[1,256,512]{2,1,0:T(8,128)(2,1)} async-done(((bf16[8,256,512]{2,1,0:T(8,128)(2,1)}), bf16[1,256,512]{2,1,0:T(8,128)(2,1)}) %reduce-scatter.10.cloned.1.call-update) | async-done | bytes 262160 | tf_op jit(solution)/shard_map/reduce_scatter | solution.py:504
  (75 shorter events, 45.7 us)
Async XLA Ops:
  7.2 34.3 %all-gather.14.cloned.1.call-start = ((), (), s32[]{:S(2)}) async-start(), calls=%async_computation.13 | async-start | bytes 2359296 | tf_op jit(solution)/shard_map/all_gather | solution.py:482
  7.9 63.8 %all-gather.16.cloned.1.call-start = ((), (), s32[]{:S(2)}) async-start(), calls=%async_computation.14 | async-start | bytes 2359296 | tf_op jit(solution)/shard_map/all_gather | solution.py:482
  8.7 143.4 %all-gather.8.cloned.1.call-start = ((), (), s32[]{:S(2)}) async-start(), calls=%async_computation.5 | async-start | bytes 8650752 | tf_op jit(solution)/shard_map/all_gather | solution.py:477
  10.4 229.6 %all-gather.10.cloned.1.call-start = ((), (), s32[]{:S(2)}) async-start(), calls=%async_computation.6 | async-start | bytes 10485760 | tf_op jit(solution)/shard_map/all_gather | solution.py:483
  41.5 287.8 %all-gather.12.cloned.1.call-start = ((), (), s32[]{:S(2)}) async-start(), calls=%async_computation.7 | async-start | bytes 10485760 | tf_op jit(solution)/shard_map/all_gather | solution.py:483
  71.7 462.6 %reduce-scatter.12.cloned.1.call-start = ((), (), s32[]{:S(2)}) async-start(), calls=%async_computation.11 | async-start | bytes 10485760 | tf_op jit(solution)/shard_map/reduce_scatter | solution.py:503
  434.6 176.4 %reduce-scatter.8.cloned.1.call-start = ((), (), s32[]{:S(2)}) async-start(), calls=%async_computation.9 | async-start | bytes 10485760 | tf_op jit(solution)/shard_map/reduce_scatter | solution.py:503
  434.7 0.9 copy-start.12
  435.4 329.9 %reduce-scatter.6.cloned.1.call-start = ((), (), s32[]{:S(2)}) async-start(), calls=%async_computation.8 | async-start | bytes 8650752 | tf_op jit(solution)/shard_map/reduce_scatter | solution.py:557
  522.1 6.5 copy-start
  522.1 6.5 copy-start.1
  522.1 6.5 copy-start.2
  534.2 76.8 %copy-start.13 = (u32[32]{0:T(128)S(1)}, u32[32]{0:T(128)}, u32[]{:S(2)}) copy-start(u32[32]{0:T(128)} %constant.9) | copy-start | bytes 388
  534.2 267.6 %reduce-scatter.14.cloned.1.call-start = ((), (), s32[]{:S(2)}) async-start(), calls=%async_computation.12 | async-start | bytes 2359296 | tf_op jit(solution)/shard_map/reduce_scatter | solution.py:504
  535.0 303.5 %reduce-scatter.10.cloned.1.call-start = ((), (), s32[]{:S(2)}) async-start(), calls=%async_computation.10 | async-start | bytes 2359296 | tf_op jit(solution)/shard_map/reduce_scatter | solution.py:504
  614.3 14.7 %copy-start.6 = (f32[1,1024]{1,0:T(1,128)S(1)}, f32[1,1024]{1,0:T(1,128)}, u32[]{:S(2)}) copy-start(f32[1,1024]{1,0:T(1,128)} %get-tuple-element.84) | copy-start | bytes 12292
  614.3 14.7 %copy-start.7 = (f32[1,1024]{1,0:T(1,128)S(1)}, f32[1,1024]{1,0:T(1,128)}, u32[]{:S(2)}) copy-start(f32[1,1024]{1,0:T(1,128)} %get-tuple-element.82) | copy-start | bytes 12292
  614.3 14.7 %copy-start.8 = (f32[1,1024]{1,0:T(1,128)S(1)}, f32[1,1024]{1,0:T(1,128)}, u32[]{:S(2)}) copy-start(f32[1,1024]{1,0:T(1,128)} %get-tuple-element.83) | copy-start | bytes 12292
  614.4 14.7 %copy-start.9 = (f32[1,1024]{1,0:T(1,128)S(1)}, f32[1,1024]{1,0:T(1,128)}, u32[]{:S(2)}) copy-start(f32[1,1024]{1,0:T(1,128)} %get-tuple-element.80) | copy-start | bytes 12292
  614.4 14.7 %copy-start.10 = (f32[1,1024]{1,0:T(1,128)S(1)}, f32[1,1024]{1,0:T(1,128)}, u32[]{:S(2)}) copy-start(f32[1,1024]{1,0:T(1,128)} %get-tuple-element.81) | copy-start | bytes 12292
  614.4 14.7 %copy-start.11 = (f32[1,1024]{1,0:T(1,128)S(1)}, f32[1,1024]{1,0:T(1,128)}, u32[]{:S(2)}) copy-start(f32[1,1024]{1,0:T(1,128)} %get-tuple-element.79) | copy-start | bytes 12292
  614.4 15.5 %copy-start.3 = (f32[8,1,512]{2,1,0:T(1,128)S(1)}, f32[8,1,512]{2,1,0:T(1,128)}, u32[]{:S(2)}) copy-start(f32[8,1,512]{2,1,0:T(1,128)} %get-tuple-element.90) | copy-start | bytes 49156
  614.4 15.5 %copy-start.4 = (f32[8,1,512]{2,1,0:T(1,128)S(1)}, f32[8,1,512]{2,1,0:T(1,128)}, u32[]{:S(2)}) copy-start(f32[8,1,512]{2,1,0:T(1,128)} %get-tuple-element.91) | copy-start | bytes 49156
  614.4 15.5 %copy-start.5 = (f32[8,1,512]{2,1,0:T(1,128)S(1)}, f32[8,1,512]{2,1,0:T(1,128)}, u32[]{:S(2)}) copy-start(f32[8,1,512]{2,1,0:T(1,128)} %get-tuple-element.92) | copy-start | bytes 49156
Sparse Core Ops, SparseCore 0:
  9.6 31.7 all-gather.13
  43.1 28.5 all-gather.15
  75.3 76.7 all-gather.7
  153.7 86.1 all-gather.9
  241.7 87.5 all-gather.11
  434.7 86.4 reduce-scatter.11
  524.6 86.4 reduce-scatter.7
  613.3 151.8 reduce-scatter.5
  767.5 34.2 reduce-scatter.13
  803.9 34.5 reduce-scatter.9

commit v2 on v1

--- a/solution.py
+++ b/solution.py
@@ -471,16 +471,292 @@
     )(dq, dk, dv, wq, wk, wv, x, dx2, gain)
 
 
-def gather_rows(parts):
-    n = len(parts)
-    width = parts[0].shape[1]
-    whole_rows = lax.all_gather(jnp.concatenate(parts, axis=1), BOTH, axis=0, tiled=True)
-    return [whole_rows[:, i * width : (i + 1) * width] for i in range(n)]
-
-
-def gather_blocks(shard):
-    over_ffn = lax.all_gather(shard, "ffn", axis=0, tiled=False)
-    return lax.all_gather(over_ffn, "rows", axis=1, tiled=True)
+class Place:
+    def __init__(self, rows, ffn):
+        self.rows, self.ffn, self.depth = rows, ffn, ffn // 2
+        self.r = lax.axis_index("rows")
+        f = lax.axis_index("ffn")
+        self.z, self.c = f // 2, lax.rem(f, 2)
+
+    def row_flip(self, r, bit):
+        return r + 1 - 2 * lax.rem(r, 2) if bit == 0 else lax.rem(r + 2, 4)
+
+    def z_at(self, d):
+        return lax.rem(self.z + d + self.depth, self.depth)
+
+    def device(self, r, z, c):
+        return (r, 2 * z + c)
+
+
+def remote(src, dst, send, recv, device):
+    return pltpu.make_async_remote_copy(
+        src_ref=src, dst_ref=dst, send_sem=send, recv_sem=recv, device_id=device, device_id_type=pl.DeviceIdType.MESH
+    )
+
+
+class Gather:
+    def __init__(self, place, src, view, local, send, recv):
+        self.place, self.src, self.view, self.local, self.send, self.recv = place, src, view, local, send, recv
+
+    def piece(self, r, z, c):
+        return self.view(r, 2 * z + c)
+
+    def arrival(self, r, z, c):
+        return self.recv.at[r, 2 * z + c]
+
+    def copy(self, src, kind, d, r, z, c, device):
+        return remote(src, self.piece(r, z, c), self.send.at[kind, d], self.arrival(r, z, c), device)
+
+    def wait_piece(self, r, z, c):
+        there = self.piece(r, z, c)
+        pltpu.make_async_copy(there, there, self.arrival(r, z, c)).wait()
+
+    def begin(self):
+        p = self.place
+        self.own_copy().start()
+        for d in range(1, p.depth):
+            self.copy(self.src, 0, d, p.r, p.z, p.c, p.device(p.r, p.z_at(d), p.c)).start()
+        self.spread(0, self.src)
+
+    def own_copy(self):
+        p = self.place
+        return pltpu.make_async_copy(self.src, self.piece(p.r, p.z, p.c), self.local)
+
+    def bits(self, d):
+        return (0, 1) if d % 2 == 0 else (1, 0)
+
+    def spread(self, d, src=None):
+        p = self.place
+        z = p.z_at(-d)
+        first, second = self.bits(d)
+        src = self.piece(p.r, z, p.c) if src is None else src
+        self.copy(src, 1, d, p.r, z, p.c, p.device(p.row_flip(p.r, first), p.z, p.c)).start()
+        self.copy(src, 2, d, p.r, z, p.c, p.device(p.row_flip(p.r, second), p.z, p.c)).start()
+        self.hand_over(4, d, p.r, z, src)
+
+    def hand_over(self, kind, d, r, z, src=None):
+        p = self.place
+        src = self.piece(r, z, p.c) if src is None else src
+        self.copy(src, kind, d, r, z, p.c, p.device(p.r, p.z, 1 - p.c)).start()
+
+    def take_z(self, d):
+        p = self.place
+        self.wait_piece(p.r, p.z_at(-d), p.c)
+        self.spread(d)
+
+    def take_first(self, d):
+        p = self.place
+        z = p.z_at(-d)
+        first, second = self.bits(d)
+        r = p.row_flip(p.r, first)
+        self.wait_piece(r, z, p.c)
+        self.copy(
+            self.piece(r, z, p.c), 3, d, r, z, p.c, p.device(p.row_flip(p.r, second), p.z, p.c)
+        ).start()
+        self.hand_over(5, d, r, z)
+
+    def take_second(self, d):
+        p = self.place
+        r = p.row_flip(p.r, self.bits(d)[1])
+        z = p.z_at(-d)
+        self.wait_piece(r, z, p.c)
+        self.hand_over(6, d, r, z)
+
+    def take_both(self, d):
+        p = self.place
+        r = p.row_flip(p.row_flip(p.r, 0), 1)
+        z = p.z_at(-d)
+        self.wait_piece(r, z, p.c)
+        self.hand_over(7, d, r, z)
+
+    def finish(self):
+        p = self.place
+        self.own_copy().wait()
+        for d in range(p.depth):
+            for r in range(p.rows):
+                self.wait_piece(r, p.z_at(-d), 1 - p.c)
+        there = self.src
+        for d in range(p.depth):
+            for kind in range(8):
+                if kind > 0 or d > 0:
+                    pltpu.make_async_copy(there, there, self.send.at[kind, d]).wait()
+
+
+def gather_kernel(*refs, rows, ffn, views):
+    n = len(views)
+    src, dst = refs[:n], refs[n : 2 * n]
+    local, send, recv = refs[2 * n :]
+    place = Place(rows, ffn)
+    jobs = [
+        Gather(place, src[i], views[i](dst[i]), local.at[i], send.at[i], recv.at[i]) for i in range(n)
+    ]
+    for job in jobs:
+        job.begin()
+    for step in ("take_z", "take_first", "take_second", "take_both"):
+        for job in jobs:
+            for d in range(1 if step == "take_z" else 0, place.depth):
+                getattr(job, step)(d)
+    for job in jobs:
+        job.finish()
+
+
+def by_device(ref):
+    return lambda r, f: ref.at[r, f]
+
+
+def by_unit(ref):
+    return lambda r, f: ref.at[f, r]
+
+
+def gather_all(rows, ffn, by_rows, by_units):
+    src = list(by_rows) + list(by_units)
+    shapes = [(rows, ffn) + a.shape for a in by_rows] + [(ffn, rows) + a.shape for a in by_units]
+    views = (by_device,) * len(by_rows) + (by_unit,) * len(by_units)
+    n = len(src)
+    hbm = pl.BlockSpec(memory_space=pl.ANY)
+    return pl.pallas_call(
+        functools.partial(gather_kernel, rows=rows, ffn=ffn, views=views),
+        in_specs=[hbm] * n,
+        out_specs=[hbm] * n,
+        out_shape=[sds(s, BF16) for s in shapes],
+        scratch_shapes=[
+            pltpu.SemaphoreType.DMA((n,)),
+            pltpu.SemaphoreType.DMA((n, 8, ffn // 2)),
+            pltpu.SemaphoreType.DMA((n, rows, ffn)),
+        ],
+        compiler_params=pltpu.CompilerParams(has_side_effects=True),
+        name="gather_all",
+    )(*src)
+
+
+class Scatter:
+    def __init__(self, place, view, own, half, pair, last, far, sems):
+        self.place, self.view, self.own, self.half, self.pair, self.last, self.far = place, view, own, half, pair, last, far
+        self.load, self.send, self.recv = sems
+
+    def bits(self, d):
+        return (0, 1) if d % 2 == 0 else (1, 0)
+
+    def copy(self, src, dst, kind, d, device):
+        return remote(src, dst, self.send.at[kind, d], self.recv.at[kind, d], device)
+
+    def to_core(self, d, r):
+        p = self.place
+        z = p.z_at(d)
+        return self.copy(
+            self.view(r, 2 * z + 1 - p.c), self.half.at[d, r], r, d, p.device(p.r, p.z, 1 - p.c)
+        )
+
+    def fetch(self, d, r):
+        p = self.place
+        return pltpu.make_async_copy(self.view(r, 2 * p.z_at(d) + p.c), self.own.at[d, r], self.load.at[r, d])
+
+    def begin(self, d):
+        for r in range(4):
+            self.to_core(d, r).start()
+            self.fetch(d, r).start()
+
+    def exchange_one(self, d, k):
+        p = self.place
+        first, second = self.bits(d)
+        partner = p.row_flip(p.r, first)
+        r = partner if k == 0 else p.row_flip(partner, second)
+        return self.copy(self.own.at[d, r], self.pair.at[d, k], 4 + k, d, p.device(partner, p.z, p.c))
+
+    def exchange_two(self, d):
+        p = self.place
+        partner = p.row_flip(p.r, self.bits(d)[1])
+        return self.copy(self.own.at[d, partner], self.last.at[d], 6, d, p.device(partner, p.z, p.c))
+
+    def along(self, d):
+        p = self.place
+        return self.copy(self.own.at[d, p.r], self.far.at[d], 7, d, p.device(p.r, p.z_at(d), p.c))
+
+    def add_core(self, d, k):
+        p = self.place
+        first, second = self.bits(d)
+        base = p.row_flip(p.r, first) if k < 2 else p.r
+        r = base if k % 2 == 0 else p.row_flip(base, second)
+        pltpu.make_async_copy(self.own.at[d, r], self.own.at[d, r], self.load.at[r, d]).wait()
+        pltpu.make_async_copy(self.half.at[d, r], self.half.at[d, r], self.recv.at[r, d]).wait()
+        self.own[d, r] = self.own[d, r] + self.half[d, r]
+        if k < 2:
+            self.exchange_one(d, k).start()
+
+    def add_one(self, d, k):
+        p = self.place
+        r = p.r if k == 0 else p.row_flip(p.r, self.bits(d)[1])
+        self.exchange_one(d, k).wait_recv()
+        self.own[d, r] = self.own[d, r] + self.pair[d, k]
+        if k == 1:
+            self.exchange_two(d).start()
+
+    def add_two(self, d):
+        p = self.place
+        self.exchange_two(d).wait_recv()
+        self.own[d, p.r] = self.own[d, p.r] + self.last[d]
+        if d > 0:
+            self.along(d).start()
+
+    def total(self):
+        p = self.place
+        out = self.own[0, p.r].astype(F32)
+        for d in range(1, p.depth):
+            self.along(d).wait_recv()
+            out = out + self.far[d].astype(F32)
+        return out
+
+    def finish(self):
+        p = self.place
+        for d in range(p.depth):
+            for r in range(4):
+                self.to_core(d, r).wait_send()
+            for k in range(2):
+                self.exchange_one(d, k).wait_send()
+            self.exchange_two(d).wait_send()
+            if d > 0:
+                self.along(d).wait_send()
+
+
+def scatter_kernel(src, out, own, half, pair, last, far, load, send, recv, *, rows, ffn, view):
+    place = Place(rows, ffn)
+    job = Scatter(place, view(src), own, half, pair, last, far, (load, send, recv))
+    order = list(range(1, place.depth)) + [0]
+    for d in order:
+        job.begin(d)
+    for d in order:
+        for k in (0, 1, 3, 2):
+            job.add_core(d, k)
+    for d in order:
+        for k in (1, 0):
+            job.add_one(d, k)
+    for d in order:
+        job.add_two(d)
+    out[...] = job.total()
+    job.finish()
+
+
+def scatter_sum(rows, ffn, grad, view):
+    piece = grad.shape[2:]
+    depth = ffn // 2
+    return pl.pallas_call(
+        functools.partial(scatter_kernel, rows=rows, ffn=ffn, view=view),
+        in_specs=[pl.BlockSpec(memory_space=pl.ANY)],
+        out_specs=pl.BlockSpec(memory_space=pltpu.VMEM),
+        out_shape=sds(piece, F32),
+        scratch_shapes=[
+            pltpu.VMEM((depth, rows) + piece, BF16),
+            pltpu.VMEM((depth, rows) + piece, BF16),
+            pltpu.VMEM((depth, 2) + piece, BF16),
+            pltpu.VMEM((depth,) + piece, BF16),
+            pltpu.VMEM((depth,) + piece, BF16),
+            pltpu.SemaphoreType.DMA((4, depth)),
+            pltpu.SemaphoreType.DMA((8, depth)),
+            pltpu.SemaphoreType.DMA((8, depth)),
+        ],
+        compiler_params=params(has_side_effects=True),
+        name="scatter_sum",
+    )(grad)
 
 
 def widen(blocks, lanes):
@@ -497,11 +773,6 @@
     if group == 1:
         return blocks
     return blocks.reshape(nb, rows, group, hb).transpose(0, 2, 1, 3).reshape(nb * group, rows, hb)
-
-
-def scatter_blocks(grad):
-    mine = lax.psum_scatter(grad, "rows", scatter_dimension=1, tiled=True)
-    return lax.psum_scatter(mine, "ffn", scatter_dimension=0, tiled=False).astype(F32)
 
 
 def rows_of(vector):
@@ -518,10 +789,13 @@
     head = width // heads
     factor = head ** (-0.5)
     block = min(seq, 256)
-    wq, wk, wv, wo = gather_rows([w_query, w_key, w_value, w_out])
+    rows, ffn = lax.axis_size("rows"), lax.axis_size("ffn")
+    four = jnp.stack([w_query, w_key, w_value, w_out])
+    attn_all, up_all, down_all = gather_all(rows, ffn, [four], [w_up, w_down])
+    wq, wk, wv, wo = (attn_all[:, :, i].reshape(width, width) for i in range(4))
     own_units = w_up.shape[1]
-    wup = widen(gather_blocks(w_up), 512)
-    wdn = widen(gather_blocks(w_down), 512)
+    wup = widen(up_all.reshape(ffn, width, own_units), 512)
+    wdn = widen(down_all.reshape(ffn, width, own_units), 512)
     nb, _, hb = wup.shape
     h, q, k, v = project_qkv(
         tokens, rows_of(ln_attn_gain), rows_of(ln_attn_bias), wq, rows_of(query_bias), wk, wv, rows_of(value_bias),
@@ -550,21 +824,20 @@
     g_wo = weight_grad(c, dor, 512)
     g_wq, g_wk, g_wv = (weight_grad(h, part, 512) for part in (dq, dk, dv))
     dx, g_lg, g_lb, g_qb, g_vb = input_grad(dq, dk, dv, wq, wk, wv, tokens, dx2, rows_of(ln_attn_gain), block)
-    grad_up = scatter_blocks(narrow(g_up, own_units))
-    grad_down = scatter_blocks(narrow(g_dn, own_units))
+    grad_up, grad_down = (
+        scatter_sum(rows, ffn, narrow(part, own_units).reshape((ffn, rows) + w_up.shape), by_unit) for part in (g_up, g_dn)
+    )
     stacked = narrow(jnp.concatenate([g_ub, g_mg, g_mb], axis=1), own_units)
     stacked = lax.psum(lax.psum_scatter(stacked, "ffn", scatter_dimension=0, tiled=False), "rows")
-    attn = lax.psum_scatter(
-        jnp.concatenate([g_wq, g_wk, g_wv, g_wo], axis=1), BOTH, scatter_dimension=0, tiled=True
-    ).astype(F32)
+    attn = jnp.stack([part.reshape((rows, ffn) + w_query.shape) for part in (g_wq, g_wk, g_wv, g_wo)], axis=2)
+    attn = scatter_sum(rows, ffn, attn, by_device)
     small = jnp.concatenate(
         [g_lg, g_lb, g_qb, g_vb, g_ob, g_pg, g_pb, g_fg, g_fb, g_db, jnp.pad(rows_of(g_hs), ((0, 0), (0, width - heads)))],
         axis=0,
     )
     small = lax.psum(small, BOTH)
     return (
-        result, dx, small[0], small[1], attn[:, :width], small[2], attn[:, width : 2 * width],
-        attn[:, 2 * width : 3 * width], small[3], small[10, :heads], attn[:, 3 * width :], small[4], small[5],
+        result, dx, small[0], small[1], attn[0], small[2], attn[1], attn[2], small[3], small[10, :heads], attn[3], small[4], small[5],
         small[6], small[7], small[8], grad_up, stacked[0], stacked[1], stacked[2], grad_down, small[9],
     )
 

time: 848 us -> 696 us (0.82)
  waiting for transfers between devices: 463 us -> 0 us
  Pallas kernels: 249 us -> 565 us
  between operations: 15.1 us -> 1.58 us
  blocking collectives: 77 us -> 86.7 us
    pallas_call x0 -> x4, Pallas kernels: none -> 318 us  [the longest x3 188 us: scatter_sum(): pl.pallas_call(functools.partial(scatter_kernel, rows=rows, ffn=ffn, view...]
    all_gather x5 -> x0, waiting for transfers between devices: 259 us -> none  [the longest x2 118 us: gather_blocks(): return lax.all_gather(over_ffn, 'rows', axis=1, tiled=True)]
    reduce_scatter x5 -> x0, waiting for transfers between devices: 202 us -> none  [the longest x2 76 us: scatter_blocks(): mine = lax.psum_scatter(grad, 'rows', scatter_dimension=1, tiled=True)]
  transfers between devices with their start and end apart: 10 -> 0, of which waited for: 9 -> 0; matrix products, arithmetic and copies ran while one was open for 5% -> 0% of each run, Pallas kernels for 17% -> 0%
where the time goes in v2:
time: 696 us; the launch traced here: 695 us
  Pallas kernels  565 us (81%)
  blocking collectives  86.7 us (12%)
  local copies, waits for them, and re-layouts  27.5 us (4%)
  other arithmetic  14.2 us (2%)
    pallas_call x3, Pallas kernels, scatter_sum(): pl.pallas_call(functools.partial(scatter_kernel, rows=rows, ffn=ffn, view...  188 us
    pallas_call x1, Pallas kernels, gather_all(): pl.pallas_call(functools.partial(gather_kernel, rows=rows, ffn=ffn, views...  130 us
    pallas_call x1, Pallas kernels, feed_forward(): pl.pallas_call(ffn_kernel, grid=(seq // block,), in_specs=[smem, rows, ro...  81.2 us
    psum x1, blocking collectives, shards(): small = lax.psum(small, BOTH)  44.2 us
    pallas_call x1, Pallas kernels, attend_backward(): pl.pallas_call(functools.partial(attend_back_kernel, block=block, head=he...  35.8 us
    unnamed x1, blocking collectives  33.2 us
    pallas_call x1, Pallas kernels, attend_forward(): pl.pallas_call(functools.partial(attend_kernel, block=block, head=head),...  30.5 us
    pallas_call x4, Pallas kernels, weight_grad(): pl.pallas_call(weights_kernel, grid=(cols // block,), in_specs=[whole((se...  25.2 us

profile of v2, /device:TPU:0, one launch (start us, length us, event | category | flops | bytes accessed | tf_op | source)
XLA Modules:
  0.0 694.9 jit_solution(9731509857795457612)
XLA Ops:
  5.6 129.6 %gather_all.1 = (bf16[4,8,4,32,1024]{4,3,2,1,0:T(8,128)(2,1)}, bf16[8,4,256,512]{3,2,1,0:T(8,128)(2,1)}, bf16[8,4,256,512]{3,2,1,0:T(8,128)(2,1)}) custom-call(bf16[4,32,1024]{2,1,0:T(8,128)(2,1)} %pad_maximum_fusion.1.refs_0_, bf16[256,512]{1,0:T(8,128)(2,1)} %refs_1_.1, bf16[256,512]{1,0:T(8,128)(2,1)} %refs_2_.1), custom_call_target="tpu_custom_call" | custom-call | tf_op jit(solution)/shard_map/gather_all/pallas_call | solution.py:617
  135.2 6.2 fusion
  141.5 12.4 %project_qkv.1 = (bf16[1024,1024]{1,0:T(8,128)(2,1)}, bf16[1024,1024]{1,0:T(8,128)(2,1)}, bf16[1024,1024]{1,0:T(8,128)(2,1)}, bf16[1024,1024]{1,0:T(8,128)(2,1)}) custom-call(bf16[1024,1024]{1,0:T(8,128)(2,1)} %x_ref.5, f32[1,1024]{1,0:T(1,128)} %bitcast.112, f32[1,1024]{1,0:T(1,128)} %bitcast.105, bf16[1024,1024]{1,0:T(8,128)(2,1)} %bitcast.72, ...), custom_call_target="tpu_custom_call" | custom-call | flops 6442450944 | bytes 16777216 | tf_op jit(solution)/shard_map/project_qkv/pallas_call | solution.py:82
  153.8 30.5 %attend_forward.1 = (bf16[1024,1024]{1,0:T(8,128)(2,1)}, f32[8,1024,128]{2,1,0:T(8,128)}) custom-call(s32[1]{0:T(128)S(6)} %copy.58.length_ref, f32[16]{0:T(128)} %scale_ref.1, bf16[1024,1024]{1,0:T(8,128)(2,1)} %get-tuple-element.62.q_ref, bf16[1024,1024]{1,0:T(8,128)(2,1)} %get-tuple-element.63.k_ref, bf16[1024,1024]{1,0:T(8,128)(2,1)} %get-tuple-element.64.v_ref), custom_call_target="tpu_custom_call" | custom-call | flops 8589934592 | bytes 12582912 | tf_op jit(solution)/shard_map/attend_forward/pallas_call | solution.py:132
  184.3 5.3 copy.53
  191.4 9.2 %out_forward.1 = (f32[1024,1024]{1,0:T(8,128)}, f32[1024,1024]{1,0:T(8,128)}, bf16[1024,1024]{1,0:T(8,128)(2,1)}) custom-call(bf16[1024,1024]{1,0:T(8,128)(2,1)} %get-tuple-element.65.c_ref.left_ref, bf16[1024,1024]{1,0:T(8,128)(2,1)} %bitcast.66, f32[1,1024]{1,0:T(1,128)} %bitcast.108, bf16[1024,1024]{1,0:T(8,128)(2,1)} %x_ref.5, f32[1,1024]{1,0:T(1,128)} %bitcast.93, ...), custom_call_target="tpu_custom_call" | custom-call | flops 2147483648 | bytes 16777216 | tf_op jit(solution)/shard_map/out_forward/pallas_call | solution.py:222
  200.6 81.2 %feed_forward.1 = (f32[1024,1024]{1,0:T(8,128)}, f32[1024,1024]{1,0:T(8,128)}, bf16[8,1024,512]{2,1,0:T(8,128)(2,1)}, bf16[8,1024,512]{2,1,0:T(8,128)(2,1)}, f32...) custom-call(s32[1]{0:T(128)S(6)} %copy.58.length_ref, ...), custom_call_target="tpu_custom_call" | custom-call | flops 68719476736 | bytes 62914560 | tf_op jit(solution)/shard_map/feed_forward/pallas_call | solution.py:307
  282.6 33.2 %all-reduce.1 = f32[8,3,512]{2,1,0:T(4,128)S(1)} all-reduce(f32[8,3,512]{2,1,0:T(4,128)S(1)} %pad_maximum_fusion.3), channel_id=2, replica_groups=mesh['rows'=4,'ffn'=8] {'ffn'}, use_global_device_ids=true, to_apply=%region_4.5.clone | all-reduce | flops 12288 | bytes 98304
  316.5 9.3 %psum.15 = f32[3,512]{1,0:T(4,128)S(1)} all-reduce(f32[3,512]{1,0:T(4,128)S(1)} %dynamic-slice_bitcast_fusion), channel_id=1, replica_groups=mesh['rows'=4,'ffn'=8] {'rows'}, use_global_device_ids=true, to_apply=%region_5.6 | all-reduce | flops 1536 | bytes 12288 | tf_op jit(solution)/shard_map/psum | solution.py:831
  326.4 14.3 %out_backward.1 = (f32[1024,1024]{1,0:T(8,128)}, bf16[1024,1024]{1,0:T(8,128)(2,1)}, bf16[1024,1024]{1,0:T(8,128)(2,1)}, f32[1024,1024]{1,0:T(8,128)}, f32[1,102...) custom-call(s32[1]{0:T(128)S(6)} %copy.58.length_ref, ...), custom_call_target="tpu_custom_call" | custom-call | flops 2147483648 | bytes 31457280 | tf_op jit(solution)/shard_map/out_backward/pallas_call | solution.py:400
  340.7 23.9 %ffn_weight_grads.1 = (bf16[8,1024,512]{2,1,0:T(8,128)(2,1)}, bf16[8,1024,512]{2,1,0:T(8,128)(2,1)}) custom-call(s32[1]{0:T(128)S(6)} %copy.58.length_ref, bf16[1024,1024]{1,0:T(8,128)(2,1)} %get-tuple-element.66.h2_ref, bf16[1024,1024]{1,0:T(8,128)(2,1)} %ct_ref.5, bf16[8,1024,512]{2,1,0:T(8,128)(2,1)} %get-tuple-element.93.m_ref, ...), custom_call_target="tpu_custom_call" | custom-call | flops 17179869184 | bytes 37748736 | tf_op jit(solution)/shard_map/ffn_weight_grads/pallas_call | solution.py:348
  364.7 58.3 %scatter_sum.4 = f32[256,512]{1,0:T(8,128)} custom-call(bf16[8,4,256,512]{3,2,1,0:T(8,128)(2,1)} %bitcast.65), custom_call_target="tpu_custom_call" | custom-call | tf_op jit(solution)/shard_map/scatter_sum/pallas_call | solution.py:742
  423.0 64.9 %scatter_sum.5 = f32[256,512]{1,0:T(8,128)} custom-call(bf16[8,4,256,512]{3,2,1,0:T(8,128)(2,1)} %bitcast.64), custom_call_target="tpu_custom_call" | custom-call | tf_op jit(solution)/shard_map/scatter_sum/pallas_call | solution.py:742
  487.9 6.4 weight_grad.7
  496.8 5.3 copy.55
  502.1 2.7 bitcast_reduce_fusion
  505.5 35.8 %attend_backward.1 = (bf16[1024,1024]{1,0:T(8,128)(2,1)}, bf16[1024,1024]{1,0:T(8,128)(2,1)}, bf16[1024,1024]{1,0:T(8,128)(2,1)}) custom-call(s32[1]{0:T(128)S(6)} %copy.58.length_ref, bf16[1024,1024]{1,0:T(8,128)(2,1)} %get-tuple-element.62.q_ref, bf16[1024,1024]{1,0:T(8,128)(2,1)} %get-tuple-element.63.k_ref, bf16[1024,1024]{1,0:T(8,128)(2,1)} %get-tuple-element.64.v_ref, ...), custom_call_target="tpu_custom_call" | custom-call | flops 21474836480 | bytes 16777216 | tf_op jit(solution)/shard_map/attend_backward/pallas_call | solution.py:193
  541.3 14.6 %input_grad.1 = (f32[1024,1024]{1,0:T(8,128)}, f32[1,1024]{1,0:T(1,128)}, f32[1,1024]{1,0:T(1,128)}, f32[1,1024]{1,0:T(1,128)}, f32[1,1024]{1,0:T(1,128)}) custom-call(bf16[1024,1024]{1,0:T(8,128)(2,1)} %get-tuple-element.76.dq_ref.right_ref, bf16[1024,1024]{1,0:T(8,128)(2,1)} %get-tuple-element.77.dk_ref.right_ref, ...), custom_call_target="tpu_custom_call" | custom-call | flops 6442450944 | bytes 23068672 | tf_op jit(solution)/shard_map/input_grad/pallas_call | solution.py:462
  555.9 6.2 weight_grad.6
  562.1 6.1 weight_grad.5
  568.2 6.6 weight_grad.4
  574.8 5.7 pad_maximum_fusion.src
  580.6 64.9 %scatter_sum.3 = f32[4,32,1024]{2,1,0:T(8,128)} custom-call(bf16[4,8,4,32,1024]{4,3,2,1,0:T(8,128)(2,1)} %pad_maximum_fusion.src), custom_call_target="tpu_custom_call" | custom-call | tf_op jit(solution)/shard_map/scatter_sum/pallas_call | solution.py:742
  647.9 44.2 %psum.14 = f32[11,1024]{1,0:T(8,128)S(1)} all-reduce(f32[11,1024]{1,0:T(8,128)S(1)} %concatenate.6), channel_id=1, replica_groups=mesh['rows'=4,'ffn'=8] {'rows','ffn'}, use_global_device_ids=true, to_apply=%region_3.0 | all-reduce | flops 11264 | bytes 90112 | tf_op jit(solution)/shard_map/psum | solution.py:838
  (53 shorter events, 16.3 us)
Async XLA Ops:
  568.2 6.6 copy-start.2
  568.2 6.6 copy-start.3
  568.2 6.6 copy-start.4
  580.5 67.2 %copy-start.15 = (f32[16]{0:T(128)S(1)}, f32[16]{0:T(128)}, u32[]{:S(2)}) copy-start(f32[16]{0:T(128)} %scale_ref.1) | copy-start | bytes 196
  580.5 67.2 %copy-start.5 = (f32[1,1024]{1,0:T(1,128)S(1)}, f32[1,1024]{1,0:T(1,128)}, u32[]{:S(2)}) copy-start(f32[1,1024]{1,0:T(1,128)} %get-tuple-element.90) | copy-start | bytes 12292
  580.5 67.2 %copy-start.6 = (f32[1,1024]{1,0:T(1,128)S(1)}, f32[1,1024]{1,0:T(1,128)}, u32[]{:S(2)}) copy-start(f32[1,1024]{1,0:T(1,128)} %get-tuple-element.88) | copy-start | bytes 12292
  580.5 67.2 %copy-start.7 = (f32[1,1024]{1,0:T(1,128)S(1)}, f32[1,1024]{1,0:T(1,128)}, u32[]{:S(2)}) copy-start(f32[1,1024]{1,0:T(1,128)} %get-tuple-element.89) | copy-start | bytes 12292
  580.5 67.2 %copy-start.8 = (f32[1,1024]{1,0:T(1,128)S(1)}, f32[1,1024]{1,0:T(1,128)}, u32[]{:S(2)}) copy-start(f32[1,1024]{1,0:T(1,128)} %get-tuple-element.86) | copy-start | bytes 12292
  580.5 67.2 %copy-start.9 = (f32[1,1024]{1,0:T(1,128)S(1)}, f32[1,1024]{1,0:T(1,128)}, u32[]{:S(2)}) copy-start(f32[1,1024]{1,0:T(1,128)} %get-tuple-element.87) | copy-start | bytes 12292
  580.5 67.2 %copy-start.10 = (f32[1,1024]{1,0:T(1,128)S(1)}, f32[1,1024]{1,0:T(1,128)}, u32[]{:S(2)}) copy-start(f32[1,1024]{1,0:T(1,128)} %get-tuple-element.85) | copy-start | bytes 12292
  580.5 67.2 %copy-start.11 = (f32[1,1024]{1,0:T(1,128)S(1)}, f32[1,1024]{1,0:T(1,128)}, u32[]{:S(2)}) copy-start(f32[1,1024]{1,0:T(1,128)} %get-tuple-element.81) | copy-start | bytes 12292
  580.5 67.2 %copy-start.12 = (f32[1,1024]{1,0:T(1,128)S(1)}, f32[1,1024]{1,0:T(1,128)}, u32[]{:S(2)}) copy-start(f32[1,1024]{1,0:T(1,128)} %get-tuple-element.82) | copy-start | bytes 12292
  580.5 67.2 %copy-start.13 = (f32[1,1024]{1,0:T(1,128)S(1)}, f32[1,1024]{1,0:T(1,128)}, u32[]{:S(2)}) copy-start(f32[1,1024]{1,0:T(1,128)} %get-tuple-element.83) | copy-start | bytes 12292
  580.6 67.2 %copy-start.14 = (f32[1,1024]{1,0:T(1,128)S(1)}, f32[1,1024]{1,0:T(1,128)}, u32[]{:S(2)}) copy-start(f32[1,1024]{1,0:T(1,128)} %get-tuple-element.84) | copy-start | bytes 12292
  580.6 112.7 %copy-start = (f32[256,512]{1,0:T(8,128)S(1)}, f32[256,512]{1,0:T(8,128)}, u32[]{:S(2)}) copy-start(f32[256,512]{1,0:T(8,128)} %scatter_sum.4) | copy-start | bytes 1572868
  645.5 48.6 %copy-start.1 = (f32[256,512]{1,0:T(8,128)S(1)}, f32[256,512]{1,0:T(8,128)}, u32[]{:S(2)}) copy-start(f32[256,512]{1,0:T(8,128)} %scatter_sum.5) | copy-start | bytes 1572868

commit v3 on v1

v3 whole, which is shorter than its diff:
```python
import functools
import math

import jax
import jax.numpy as jnp
from jax import lax
from jax.experimental import pallas as pl
from jax.experimental.pallas import tpu as pltpu
from jax.sharding import PartitionSpec as P

epsilon = 1e-05
masked_score = -1e30
F32 = jnp.float32
BF16 = jnp.bfloat16
MIB = 1 << 20
BOTH = ("rows", "ffn")


def dot_nn(left, right):
    return lax.dot_general(left, right, (((1,), (0,)), ((), ())), preferred_element_type=F32)


def dot_nt(left, right):
    return lax.dot_general(left, right, (((1,), (1,)), ((), ())), preferred_element_type=F32)


def dot_tn(left, right):
    return lax.dot_general(left, right, (((0,), (0,)), ((), ())), preferred_element_type=F32)


def params(limit=56 * MIB, **kw):
    return pltpu.CompilerParams(vmem_limit_bytes=limit, **kw)


def whole(shape):
    return pl.BlockSpec(shape, lambda *_: (0,) * len(shape), pipeline_mode=pl.Buffered(1))


def out_whole(shape):
    return pl.BlockSpec(shape, lambda *_: (0,) * len(shape))


def sds(shape, dtype):
    return jax.ShapeDtypeStruct(shape, dtype)


def norm_parts(values):
    center = jnp.mean(values, axis=-1, keepdims=True)
    centered = values - center
    spread = jnp.mean(centered * centered, axis=-1, keepdims=True)
    inverse = lax.rsqrt(spread + epsilon)
    return centered * inverse, inverse


def norm_back(grad_hat, hat, inverse):
    return (
        grad_hat
        - jnp.mean(grad_hat, axis=-1, keepdims=True)
        - hat * jnp.mean(grad_hat * hat, axis=-1, keepdims=True)
    ) * inverse


def col_sum(values):
    return jnp.sum(values, axis=0, keepdims=True)


class Place:
    def __init__(self, rows, ffn):
        self.rows, self.ffn, self.depth = rows, ffn, ffn // 2
        self.r = lax.axis_index("rows")
        f = lax.axis_index("ffn")
        self.z, self.c = f // 2, lax.rem(f, 2)

    def row_flip(self, r, bit):
        return r + 1 - 2 * lax.rem(r, 2) if bit == 0 else lax.rem(r + 2, 4)

    def z_at(self, d):
        return lax.rem(self.z + d + self.depth, self.depth)

    def device(self, r, z, c):
        return (r, 2 * z + c)


def remote(src, dst, send, recv, device):
    return pltpu.make_async_remote_copy(
        src_ref=src, dst_ref=dst, send_sem=send, recv_sem=recv, device_id=device, device_id_type=pl.DeviceIdType.MESH
    )


class Gather:
    def __init__(self, place, src, view, local, send, recv):
        self.place, self.src, self.view, self.local, self.send, self.recv = place, src, view, local, send, recv

    def piece(self, r, z, c):
        return self.view(r, 2 * z + c)

    def arrival(self, r, z, c):
        return self.recv.at[r, 2 * z + c]

    def copy(self, src, kind, d, r, z, c, device):
        return remote(src, self.piece(r, z, c), self.send.at[kind, d], self.arrival(r, z, c), device)

    def wait_piece(self, r, z, c):
        there = self.piece(r, z, c)
        pltpu.make_async_copy(there, there, self.arrival(r, z, c)).wait()

    def begin(self):
        p = self.place
        self.own_copy().start()
        for d in range(1, p.depth):
            self.copy(self.src, 0, d, p.r, p.z, p.c, p.device(p.r, p.z_at(d), p.c)).start()
        self.spread(0, self.src)

    def own_copy(self):
        p = self.place
        return pltpu.make_async_copy(self.src, self.piece(p.r, p.z, p.c), self.local)

    def bits(self, d):
        return (0, 1) if d % 2 == 0 else (1, 0)

    def spread(self, d, src=None):
        p = self.place
        z = p.z_at(-d)
        first, second = self.bits(d)
        src = self.piece(p.r, z, p.c) if src is None else src
        self.copy(src, 1, d, p.r, z, p.c, p.device(p.row_flip(p.r, first), p.z, p.c)).start()
        self.copy(src, 2, d, p.r, z, p.c, p.device(p.row_flip(p.r, second), p.z, p.c)).start()
        self.hand_over(4, d, p.r, z, src)

    def hand_over(self, kind, d, r, z, src=None):
        p = self.place
        src = self.piece(r, z, p.c) if src is None else src
        self.copy(src, kind, d, r, z, p.c, p.device(p.r, p.z, 1 - p.c)).start()

    def take_z(self, d):
        p = self.place
        self.wait_piece(p.r, p.z_at(-d), p.c)
        self.spread(d)

    def take_first(self, d):
        p = self.place
        z = p.z_at(-d)
        first, second = self.bits(d)
        r = p.row_flip(p.r, first)
        self.wait_piece(r, z, p.c)
        self.copy(
            self.piece(r, z, p.c), 3, d, r, z, p.c, p.device(p.row_flip(p.r, second), p.z, p.c)
        ).start()
        self.hand_over(5, d, r, z)

    def take_second(self, d):
        p = self.place
        r = p.row_flip(p.r, self.bits(d)[1])
        z = p.z_at(-d)
        self.wait_piece(r, z, p.c)
        self.hand_over(6, d, r, z)

    def take_both(self, d):
        p = self.place
        r = p.row_flip(p.row_flip(p.r, 0), 1)
        z = p.z_at(-d)
        self.wait_piece(r, z, p.c)
        self.hand_over(7, d, r, z)

    def finish(self):
        p = self.place
        self.own_copy().wait()
        for d in range(p.depth):
            for r in range(p.rows):
                self.wait_piece(r, p.z_at(-d), 1 - p.c)
        there = self.src
        for d in range(p.depth):
            for kind in range(8):
                if kind > 0 or d > 0:
                    pltpu.make_async_copy(there, there, self.send.at[kind, d]).wait()


def gather_kernel(*refs, rows, ffn, views):
    n = len(views)
    src, dst = refs[:n], refs[n : 2 * n]
    local, send, recv = refs[2 * n :]
    place = Place(rows, ffn)
    jobs = [
        Gather(place, src[i], views[i](dst[i]), local.at[i], send.at[i], recv.at[i]) for i in range(n)
    ]
    for job in jobs:
        job.begin()
    for step in ("take_z", "take_first", "take_second", "take_both"):
        for job in jobs:
            for d in range(1 if step == "take_z" else 0, place.depth):
                getattr(job, step)(d)
    for job in jobs:
        job.finish()


def by_device(ref):
    return lambda r, f: ref.at[r, f]


def by_unit(ref):
    return lambda r, f: ref.at[f, r]


def gather_all(rows, ffn, by_rows, by_units):
    src = list(by_rows) + list(by_units)
    shapes = [(rows, ffn) + a.shape for a in by_rows] + [(ffn, rows) + a.shape for a in by_units]
    views = (by_device,) * len(by_rows) + (by_unit,) * len(by_units)
    n = len(src)
    hbm = pl.BlockSpec(memory_space=pl.ANY)
    return pl.pallas_call(
        functools.partial(gather_kernel, rows=rows, ffn=ffn, views=views),
        in_specs=[hbm] * n,
        out_specs=[hbm] * n,
        out_shape=[sds(s, BF16) for s in shapes],
        scratch_shapes=[
            pltpu.SemaphoreType.DMA((n,)),
            pltpu.SemaphoreType.DMA((n, 8, ffn // 2)),
            pltpu.SemaphoreType.DMA((n, rows, ffn)),
        ],
        compiler_params=pltpu.CompilerParams(has_side_effects=True),
        name="gather_all",
    )(*src)


class Scatter:
    def __init__(self, place, view, own, half, pair, last, far, sems):
        self.place, self.view, self.own, self.half, self.pair, self.last, self.far = place, view, own, half, pair, last, far
        self.load, self.send, self.recv = sems

    def bits(self, d):
        return (0, 1) if d % 2 == 0 else (1, 0)

    def copy(self, src, dst, kind, d, device):
        return remote(src, dst, self.send.at[kind, d], self.recv.at[kind, d], device)

    def to_core(self, d, r):
        p = self.place
        z = p.z_at(d)
        return self.copy(
            self.view(r, 2 * z + 1 - p.c), self.half.at[d, r], r, d, p.device(p.r, p.z, 1 - p.c)
        )

    def fetch(self, d, r):
        p = self.place
        return pltpu.make_async_copy(self.view(r, 2 * p.z_at(d) + p.c), self.own.at[d, r], self.load.at[r, d])

    def begin(self, d):
        for r in range(4):
            self.to_core(d, r).start()
            self.fetch(d, r).start()

    def exchange_one(self, d, k):
        p = self.place
        first, second = self.bits(d)
        partner = p.row_flip(p.r, first)
        r = partner if k == 0 else p.row_flip(partner, second)
        return self.copy(self.own.at[d, r], self.pair.at[d, k], 4 + k, d, p.device(partner, p.z, p.c))

    def exchange_two(self, d):
        p = self.place
        partner = p.row_flip(p.r, self.bits(d)[1])
        return self.copy(self.own.at[d, partner], self.last.at[d], 6, d, p.device(partner, p.z, p.c))

    def along(self, d):
        p = self.place
        return self.copy(self.own.at[d, p.r], self.far.at[d], 7, d, p.device(p.r, p.z_at(d), p.c))

    def add_core(self, d, k):
        p = self.place
        first, second = self.bits(d)
        base = p.row_flip(p.r, first) if k < 2 else p.r
        r = base if k % 2 == 0 else p.row_flip(base, second)
        pltpu.make_async_copy(self.own.at[d, r], self.own.at[d, r], self.load.at[r, d]).wait()
        pltpu.make_async_copy(self.half.at[d, r], self.half.at[d, r], self.recv.at[r, d]).wait()
        self.own[d, r] = self.own[d, r] + self.half[d, r]
        if k < 2:
            self.exchange_one(d, k).start()

    def add_one(self, d, k):
        p = self.place
        r = p.r if k == 0 else p.row_flip(p.r, self.bits(d)[1])
        self.exchange_one(d, k).wait_recv()
        self.own[d, r] = self.own[d, r] + self.pair[d, k]
        if k == 1:
            self.exchange_two(d).start()

    def add_two(self, d):
        p = self.place
        self.exchange_two(d).wait_recv()
        self.own[d, p.r] = self.own[d, p.r] + self.last[d]
        if d > 0:
            self.along(d).start()

    def total(self):
        p = self.place
        out = self.own[0, p.r].astype(F32)
        for d in range(1, p.depth):
            self.along(d).wait_recv()
            out = out + self.far[d].astype(F32)
        return out

    def finish(self):
        p = self.place
        for d in range(p.depth):
            for r in range(4):
                self.to_core(d, r).wait_send()
            for k in range(2):
                self.exchange_one(d, k).wait_send()
            self.exchange_two(d).wait_send()
            if d > 0:
                self.along(d).wait_send()


def scatter_kernel(src, out, own, half, pair, last, far, load, send, recv, *, rows, ffn, view):
    place = Place(rows, ffn)
    job = Scatter(place, view(src), own, half, pair, last, far, (load, send, recv))
    order = list(range(1, place.depth)) + [0]
    for d in order:
        job.begin(d)
    for d in order:
        for k in (0, 1, 3, 2):
            job.add_core(d, k)
    for d in order:
        for k in (1, 0):
            job.add_one(d, k)
    for d in order:
        job.add_two(d)
    out[...] = job.total()
    job.finish()


def scatter_sum(rows, ffn, grad, view):
    piece = grad.shape[2:]
    depth = ffn // 2
    return pl.pallas_call(
        functools.partial(scatter_kernel, rows=rows, ffn=ffn, view=view),
        in_specs=[pl.BlockSpec(memory_space=pl.ANY)],
        out_specs=pl.BlockSpec(memory_space=pltpu.VMEM),
        out_shape=sds(piece, F32),
        scratch_shapes=[
            pltpu.VMEM((depth, rows) + piece, BF16),
            pltpu.VMEM((depth, rows) + piece, BF16),
            pltpu.VMEM((depth, 2) + piece, BF16),
            pltpu.VMEM((depth,) + piece, BF16),
            pltpu.VMEM((depth,) + piece, BF16),
            pltpu.SemaphoreType.DMA((4, depth)),
            pltpu.SemaphoreType.DMA((8, depth)),
            pltpu.SemaphoreType.DMA((8, depth)),
        ],
        compiler_params=params(has_side_effects=True),
        name="scatter_sum",
    )(grad)


def clip(step, low, count):
    return jnp.minimum(jnp.maximum(step - low, 0), count - 1)


def at_steps(step, plan):
    for when, actions in plan.items():

        @pl.when(step == when)
        def _(actions=actions):
            for action in actions:
                action()


def attend_pair(length, scales, q_of, k, v, seq, block, head, store):
    lanes = 2 * head
    lane = lax.broadcasted_iota(jnp.int32, (block, lanes), 1)
    for i in range(seq // block):
        keys_here = (i + 1) * block
        q = q_of(i)
        key_pos = lax.broadcasted_iota(jnp.int32, (block, keys_here), 1)
        row_pos = lax.broadcasted_iota(jnp.int32, (block, keys_here), 0) + i * block
        allowed = key_pos < jnp.minimum(row_pos + 1, length)
        ctx = None
        logs = []
        for n in range(2):
            mine = (lane < head) if n == 0 else (lane >= head)
            scores = dot_nt(jnp.where(mine, q, 0), k[:keys_here, :])
            scores = jnp.where(allowed, scores, masked_score)
            peak = jnp.max(scores, axis=-1, keepdims=True)
            weights = jnp.exp(scores - peak)
            total = jnp.sum(weights, axis=-1, keepdims=True)
            part = dot_nn(weights.astype(BF16), v[:keys_here, :]) * (scales[n] / total)
            ctx = part if n == 0 else jnp.where(lane < head, ctx, part)
            logs.append(peak + jnp.log(total))
        store(i, ctx.astype(BF16), jnp.where(lane < head, logs[0], logs[1]).T)


def front_kernel(*refs, rows, ffn, block, head, factor, fused):
    n_in = 14 if fused else 12
    (length_ref, scale_ref, x_ref, lg_ref, lb_ref, qb_ref, vb_ref, ob_ref, pg_ref, pb_ref, fg_ref) = refs[:11]
    fb_ref = refs[11]
    comm_in = refs[12 : 15 if fused else 13]
    refs = refs[15 if fused else 13 :]
    h_ref, q_ref, k_ref, v_ref, c_ref, lse_ref, o_ref, x2_ref, h2_ref = refs[:9]
    comm_out = refs[9:12] if fused else ()
    refs = refs[12 if fused else 9 :]
    w_s, q_s, k_s, v_s, c_s, load = refs[:6]
    step = pl.program_id(0)
    seq, width = q_s.shape
    nb = seq // block
    pairs = width // (2 * head)
    last = 2 * nb + pairs - 1

    def load_weights(source):
        copies = [pltpu.make_async_copy(source(i), w_s.at[i], load.at[i]) for i in range(4)]
        for copy in copies:
            copy.start()
        for copy in copies:
            copy.wait()

    late = {}
    if fused:
        local, send, recv = refs[6:9]
        place = Place(rows, ffn)
        views = (by_device, by_unit, by_unit)
        four, down, up = (
            Gather(place, comm_in[i], views[i](comm_out[i]), local.at[i], send.at[i], recv.at[i]) for i in range(3)
        )
        depth = place.depth
        every = range(depth)

        @pl.when(step == 0)
        def _():
            four.begin()
            for d in range(1, depth):
                four.take_z(d)
            down.begin()
            for d in every:
                four.take_first(d)
            for d in every:
                four.take_second(d)
            for d in every:
                four.take_both(d)
            up.begin()
            four.finish()
            load_weights(lambda i: comm_out[0].at[:, :, i])

        def do(job, name, *ds):
            return [functools.partial(getattr(job, name), d) for d in ds if d < depth]

        late = {
            1: do(down, "take_z", 1) + do(down, "take_first", 0),
            2: do(down, "take_z", 2) + do(down, "take_first", 1),
            3: do(down, "take_z", 3) + do(down, "take_second", 0),
            4: do(down, "take_first", 2) + do(up, "take_z", 1),
            5: do(down, "take_first", 3) + do(down, "take_second", 1) + do(up, "take_z", 2),
            6: do(down, "take_both", 0, 1) + do(down, "take_second", 2) + do(up, "take_z", 3),
            7: do(down, "take_second", 3) + do(up, "take_first", 0),
            8: do(down, "take_both", 2, 3) + do(up, "take_first", 1),
            9: do(up, "take_first", 2) + do(up, "take_second", 0),
            10: do(up, "take_first", 3) + do(up, "take_second", 1),
            11: do(up, "take_second", 2),
            12: do(up, "take_second", 3) + do(up, "take_both", 0),
            13: do(up, "take_both", 1),
        }
        at_steps(step, late)
    else:

        @pl.when(step == 0)
        def _():
            load_weights(lambda i: comm_in[0].at[i])

    def weight(i):
        return w_s[i].reshape(width, width)

    @pl.when(step < nb)
    def _():
        here = pl.ds(pl.multiple_of(step * block, block), block)
        hat, _ = norm_parts(x_ref[...].astype(F32))
        h = (hat * lg_ref[...] + lb_ref[...]).astype(BF16)
        h_ref[...] = h
        q = ((dot_nn(h, weight(0)) + qb_ref[...]).astype(BF16).astype(F32) * factor).astype(BF16)
        k = dot_nn(h, weight(1)).astype(BF16)
        v = (dot_nn(h, weight(2)) + vb_ref[...]).astype(BF16)
        for ref, scratch, value in ((q_ref, q_s, q), (k_ref, k_s, k), (v_ref, v_s, v)):
            ref[...] = value
            scratch[here, :] = value

    @pl.when((step >= nb) & (step < nb + pairs))
    def _():
        pair = step - nb
        cols = pl.ds(pl.multiple_of(pair * (2 * head), 2 * head), 2 * head)

        def store(i, ctx, logs):
            c_s[i * block : (i + 1) * block, cols] = ctx
            for n in range(2):
                lse_ref[0, n : n + 1, i * block : (i + 1) * block] = logs[n * head : n * head + 1, :]

        attend_pair(
            length_ref[0], [scale_ref[2 * pair + n] for n in range(2)],
            lambda i: q_s[i * block : (i + 1) * block, cols], k_s[:, cols], v_s[:, cols], seq, block, head, store,
        )

    @pl.when(step >= nb + pairs)
    def _():
        here = pl.ds(pl.multiple_of((step - nb - pairs) * block, block), block)
        c = c_s[here, :]
        c_ref[...] = c
        o = dot_nn(c, weight(3)) + ob_ref[...]
        o_ref[...] = o
        hat, _ = norm_parts(o)
        x2 = x_ref[...].astype(F32) + (hat * pg_ref[...] + pb_ref[...])
        x2_ref[...] = x2
        hat2, _ = norm_parts(x2)
        h2_ref[...] = (hat2 * fg_ref[...] + fb_ref[...]).astype(BF16)

    if fused:

        @pl.when(step == last)
        def _():
            for d in (2, 3):
                if d < depth:
                    up.take_both(d)
            down.finish()
            up.finish()


def front(length, scale, x, vectors, weights, rows, ffn, block, head, factor, fused):
    seq, width = x.shape
    nb, pairs = seq // block, width // (2 * head)
    steps = 2 * nb + pairs
    x_rows = pl.BlockSpec((block, width), lambda i: (jnp.where(i < nb + pairs, jnp.minimum(i, nb - 1), i - nb - pairs), 0))
    first = pl.BlockSpec((block, width), lambda i: (clip(i, 0, nb), 0))
    final = pl.BlockSpec((block, width), lambda i: (clip(i, nb + pairs, nb), 0))
    smem = pl.BlockSpec(memory_space=pltpu.SMEM)
    hbm = pl.BlockSpec(memory_space=pl.ANY)
    out_specs = [first] * 4 + [final, pl.BlockSpec((1, 2, seq), lambda i: (clip(i, nb, pairs), 0, 0))] + [final] * 3
    out_shape = [sds((seq, width), BF16)] * 5 + [sds((pairs, 2, seq), F32)] + [sds((seq, width), F32)] * 2
    out_shape += [sds((seq, width), BF16)]
    scratch = [pltpu.VMEM((seq, width), BF16)] * 4 + [pltpu.SemaphoreType.DMA((4,))]
    if fused:
        four, down, up = weights
        out_shape += [sds((rows, ffn) + four.shape, BF16)] + [sds((ffn, rows) + a.shape, BF16) for a in (down, up)]
        out_specs += [hbm] * 3
        scratch = [pltpu.VMEM((4, rows, ffn) + four.shape[1:], BF16)] + scratch + [
            pltpu.SemaphoreType.DMA((3,)),
            pltpu.SemaphoreType.DMA((3, 8, ffn // 2)),
            pltpu.SemaphoreType.DMA((3, rows, ffn)),
        ]
    else:
        scratch = [pltpu.VMEM((4, width, width), BF16)] + scratch
    return pl.pallas_call(
        functools.partial(front_kernel, rows=rows, ffn=ffn, block=block, head=head, factor=factor, fused=fused),
        grid=(steps,),
        in_specs=[smem, smem, x_rows] + [whole((1, width))] * 9 + [hbm] * len(weights),
        out_specs=out_specs,
        out_shape=out_shape,
        scratch_shapes=scratch,
        compiler_params=params(60 * MIB, has_side_effects=fused),
        name="forward_attention",
    )(length, scale, x, *vectors, *weights)


def ffn_kernel(
    length_ref, h2_ref, ct_ref, x2_ref, wup_ref, wdn_ref, ub_ref, mg_ref, mb_ref, db_ref,
    res_ref, dh2_ref, m_ref, du_ref, gub_ref, gmg_ref, gmb_ref, gdb_ref,
    e_s, gp_s, dm_s,
):
    step = pl.program_id(0)
    block, width = h2_ref.shape
    nb, _, hb = wup_ref.shape
    units = nb * hb
    row = lax.broadcasted_iota(jnp.int32, (block, width), 0) + step * block
    valid = row < length_ref[0]
    h2 = h2_ref[...]
    dfr = jnp.where(valid, ct_ref[...].astype(F32), 0.0).astype(BF16)

    @pl.when(step == 0)
    def _():
        gub_ref[...] = jnp.zeros_like(gub_ref)
        gmg_ref[...] = jnp.zeros_like(gmg_ref)
        gmb_ref[...] = jnp.zeros_like(gmb_ref)
        gdb_ref[...] = jnp.zeros_like(gdb_ref)

    gdb_ref[...] += col_sum(dfr.astype(F32))

    def first(j, sums):
        u = dot_nn(h2, wup_ref[j]) + ub_ref[j]
        dm = dot_nn(dfr, wdn_ref[j])
        cdf = 0.5 * (1.0 + lax.erf(u * math.sqrt(0.5)))
        e = u * cdf
        gp = cdf + u * (jnp.exp(u * u * -0.5) * (1.0 / math.sqrt(2.0 * math.pi)))
        dmh = dm * mg_ref[j]
        e_s[j] = e
        gp_s[j] = gp
        dm_s[j] = dm
        terms = (e, e * e, dmh, dmh * e)
        return tuple(s + jnp.sum(t, axis=-1, keepdims=True) for s, t in zip(sums, terms))

    zero = jnp.zeros((block, 1), F32)
    sum_e, sum_ee, sum_d, sum_de = lax.fori_loop(0, nb, first, (zero,) * 4)
    mu = sum_e / units
    inverse = lax.rsqrt(sum_ee / units - mu * mu + epsilon)
    mean_d = sum_d / units
    mean_dh = (sum_de - mu * sum_d) * inverse / units

    def second(j, sums):
        f, dh2 = sums
        ehat = (e_s[j] - mu) * inverse
        dm = dm_s[j]
        m = (ehat * mg_ref[j] + mb_ref[j]).astype(BF16)
        m_ref[j] = m
        f = f + dot_nt(m, wdn_ref[j])
        de = (dm * mg_ref[j] - mean_d - ehat * mean_dh) * inverse
        du = (de * gp_s[j]).astype(BF16)
        du_ref[j] = du
        dh2 = dh2 + dot_nt(du, wup_ref[j])
        gub_ref[j] += col_sum(du.astype(F32))
        gmg_ref[j] += col_sum(dm * ehat)
        gmb_ref[j] += col_sum(dm)
        return f, dh2

    zeros = jnp.zeros((block, width), F32)
    f, dh2 = lax.fori_loop(0, nb, second, (zeros, zeros))
    res_ref[...] = jnp.where(valid, x2_ref[...] + f + db_ref[...], 0.0)
    dh2_ref[...] = dh2


def feed_forward(length, h2, ct, x2, wup, wdn, ub, mg, mb, db, block):
    seq, width = h2.shape
    nb, _, hb = wup.shape
    rows = pl.BlockSpec((block, width), lambda i: (i, 0))
    smem = pl.BlockSpec(memory_space=pltpu.SMEM)
    units = whole((nb, 1, hb))
    blocks = pl.BlockSpec((nb, block, hb), lambda i: (0, i, 0))
    sums = out_whole((nb, 1, hb))
    return pl.pallas_call(
        ffn_kernel,
        grid=(seq // block,),
        in_specs=[
            smem, rows, rows, rows, whole((nb, width, hb)), whole((nb, width, hb)),
            units, units, units, whole((1, width)),
        ],
        out_specs=[rows, rows, blocks, blocks, sums, sums, sums, out_whole((1, width))],
        out_shape=[
            sds((seq, width), F32), sds((seq, width), F32), sds((nb, seq, hb), BF16), sds((nb, seq, hb), BF16),
            sds((nb, 1, hb), F32), sds((nb, 1, hb), F32), sds((nb, 1, hb), F32), sds((1, width), F32),
        ],
        scratch_shapes=[pltpu.VMEM((nb, block, hb), F32)] * 3,
        compiler_params=params(60 * MIB),
        cost_estimate=pl.CostEstimate(
            flops=16 * seq * width * nb * hb, bytes_accessed=60 * MIB, transcendentals=2 * seq * nb * hb
        ),
        name="feed_forward",
    )(length, h2, ct, x2, wup, wdn, ub, mg, mb, db)


def ffn_weights_kernel(length_ref, h2_ref, ct_ref, m_ref, du_ref, gup_ref, gdn_ref, h2t_s, dft_s):
    seq, width = h2_ref.shape

    @pl.when(pl.program_id(0) == 0)
    def _():
        row = lax.broadcasted_iota(jnp.int32, (seq, width), 0)
        dfr = jnp.where(row < length_ref[0], ct_ref[...], 0)
        h2t_s[...] = h2_ref[...].T
        dft_s[...] = dfr.T

    gdn_ref[0] = dot_nn(dft_s[...], m_ref[0]).astype(BF16)
    gup_ref[0] = dot_nn(h2t_s[...], du_ref[0]).astype(BF16)


def ffn_weight_grads(length, h2, ct, m, du):
    seq, width = h2.shape
    nb, _, hb = m.shape
    smem = pl.BlockSpec(memory_space=pltpu.SMEM)
    block = pl.BlockSpec((1, seq, hb), lambda j: (j, 0, 0))
    out = pl.BlockSpec((1, width, hb), lambda j: (j, 0, 0))
    return pl.pallas_call(
        ffn_weights_kernel,
        grid=(nb,),
        in_specs=[smem, whole((seq, width)), whole((seq, width)), block, block],
        out_specs=[out, out],
        out_shape=[sds((nb, width, hb), BF16)] * 2,
        scratch_shapes=[pltpu.VMEM((width, seq), BF16)] * 2,
        compiler_params=params(),
        cost_estimate=pl.CostEstimate(
            flops=4 * seq * width * nb * hb, bytes_accessed=36 * MIB, transcendentals=0
        ),
        name="ffn_weight_grads",
    )(length, h2, ct, m, du)


def attend_back_pair(length, q_all, k_of, v_of, g_all, lse_ref, inner_row, dq_s, store, seq, block, head):
    lanes = 2 * head
    lane = lax.broadcasted_iota(jnp.int32, (seq, lanes), 1)
    dq_s[...] = jnp.zeros_like(dq_s)
    zero = jnp.zeros_like(q_all)
    q_heads = [jnp.where(lane < head, q_all, zero), jnp.where(lane >= head, q_all, zero)]
    g_heads = [jnp.where(lane < head, g_all, zero), jnp.where(lane >= head, g_all, zero)]
    for j in range(seq // block):
        start = j * block
        width = seq - start
        k, v = k_of(j), v_of(j)
        key_pos = lax.broadcasted_iota(jnp.int32, (block, width), 0) + start
        row_pos = lax.broadcasted_iota(jnp.int32, (block, width), 1) + start
        allowed = (key_pos <= row_pos) & (key_pos < length)
        dk = dv = None
        dqs = []
        for n in range(2):
            q = q_heads[n][start:, :]
            g = g_heads[n][start:, :]
            scores = dot_nt(k, q)
            probs = jnp.where(allowed, jnp.exp(scores - lse_ref[0, n : n + 1, start:]), 0.0)
            grad_probs = dot_nt(v, g)
            grad_scores = (probs * (grad_probs - inner_row(n)[:, start:])).astype(BF16)
            dv_part = dot_nn(probs.astype(BF16), g)
            dk_part = dot_nn(grad_scores, q)
            dv = dv_part if n == 0 else dv + dv_part
            dk = dk_part if n == 0 else dk + dk_part
            dqs.append(dot_tn(grad_scores, k))
        dq_s[start:, :] += jnp.where(lane[start:, :] < head, dqs[0], dqs[1])
        store(j, dk.astype(BF16), dv.astype(BF16))


def back_kernel(*refs, rows, ffn, block, head, factor, fused):
    (
        length_ref, dh2_ref, ct_ref, x2_ref, o_ref, c_ref, w_ref, fg_ref, pg_ref, hs_ref, q_ref, k_ref, v_ref, lse_ref,
    ) = refs[:14]
    comm_in = refs[14:16] if fused else ()
    refs = refs[16 if fused else 14 :]
    (
        dx2_ref, dor_ref, dq_ref, dk_ref, dv_ref, ghs_ref, gfg_ref, gfb_ref, gpg_ref, gpb_ref, gob_ref,
    ) = refs[:11]
    comm_out = refs[11:13] if fused else ()
    refs = refs[13 if fused else 11 :]
    g_s, inner_s, dq_s = refs[:3]
    step = pl.program_id(0)
    seq, width = g_s.shape
    nb = seq // block
    pairs = width // (2 * head)
    heads = width // head
    last = nb + pairs - 1

    if fused:
        place = Place(rows, ffn)
        depth = place.depth
        jobs = []
        for n in range(2):
            bufs = refs[3 + 8 * n : 11 + 8 * n]
            jobs.append(Scatter(place, by_unit(comm_in[n]), *bufs[:5], bufs[5:]))
        one, two = jobs
        order = [d for d in (1, 2, 3) if d < depth] + [0]

        @pl.when(step == 0)
        def _():
            for job in jobs:
                for d in order:
                    job.begin(d)

        def core(job, *ds):
            return [functools.partial(job.add_core, d, k) for d in ds if d < depth for k in (0, 1, 3, 2)]

        def first(job, *ds):
            return [functools.partial(job.add_one, d, k) for d in ds if d < depth for k in (1, 0)]

        def second(job, *ds):
            return [functools.partial(job.add_two, d) for d in ds if d < depth]

        at_steps(step, {
            2: core(one, 1, 2),
            3: core(one, 3, 0),
            4: core(two, 1, 2),
            5: core(two, 3, 0),
            6: first(one, 1, 2),
            7: first(one, 3, 0),
            8: second(one, 1, 2, 3),
            10: first(two, 1, 2) + second(one, 0),
        })

    @pl.when(step < nb)
    def _():
        row = lax.broadcasted_iota(jnp.int32, (block, width), 0) + step * block
        dy = jnp.where(row < length_ref[0], ct_ref[...].astype(F32), 0.0)

        @pl.when(step == 0)
        def _():
            for ref in (gfg_ref, gfb_ref, gpg_ref, gpb_ref, gob_ref, ghs_ref):
                ref[...] = jnp.zeros_like(ref)

        dh2 = dh2_ref[...]
        hat2, inverse2 = norm_parts(x2_ref[...])
        gfg_ref[...] += col_sum(dh2 * hat2)
        gfb_ref[...] += col_sum(dh2)
        dx2 = dy + norm_back(dh2 * fg_ref[...], hat2, inverse2)
        dx2_ref[...] = dx2
        hat, inverse = norm_parts(o_ref[...])
        gpg_ref[...] += col_sum(dx2 * hat)
        gpb_ref[...] += col_sum(dx2)
        dor = norm_back(dx2 * pg_ref[...], hat, inverse).astype(BF16)
        dor_ref[...] = dor
        gob_ref[...] += col_sum(dor.astype(F32))
        dc = dot_nt(dor, w_ref[...].reshape(width, width))
        here = pl.ds(pl.multiple_of(step * block, block), block)
        g_s[here, :] = (dc * hs_ref[...]).astype(BF16)
        product = dc * c_ref[...].astype(F32)
        high = product.astype(BF16)
        low = (product - high.astype(F32)).astype(BF16)
        owner = lax.broadcasted_iota(jnp.int32, (heads, width), 1) // head
        pick = (owner == lax.broadcasted_iota(jnp.int32, (heads, width), 0)).astype(BF16)
        inner = dot_nt(pick, high) + dot_nt(pick, low)
        inner_s[step] = inner
        ghs_ref[...] += jnp.broadcast_to(jnp.sum(inner, axis=-1, keepdims=True), ghs_ref.shape)

    @pl.when(step >= nb)
    def _():
        pair = step - nb
        cols = pl.ds(pl.multiple_of(pair * (2 * head), 2 * head), 2 * head)
        inner_rows = [
            jnp.concatenate([inner_s[i, pl.ds(2 * pair + n, 1), :] for i in range(nb)], axis=1) for n in range(2)
        ]

        def store(j, dk, dv):
            dk_ref[j * block : (j + 1) * block, :] = dk
            dv_ref[j * block : (j + 1) * block, :] = dv

        attend_back_pair(
            length_ref[0], q_ref[...], lambda j: k_ref[j * block : (j + 1) * block, :],
            lambda j: v_ref[j * block : (j + 1) * block, :], g_s[:, cols], lse_ref, lambda n: inner_rows[n], dq_s, store,
            seq, block, head,
        )
        dq_ref[...] = (dq_s[...] * factor).astype(BF16)

    if fused:

        @pl.when(step == last)
        def _():
            for action in first(two, 3, 0) + second(two, 1, 2, 3, 0):
                action()
            for job, out in zip(jobs, comm_out):
                out[...] = job.total()
                job.finish()


def scatter_scratch(piece, rows, depth):
    return [
        pltpu.VMEM((depth, rows) + piece, BF16),
        pltpu.VMEM((depth, rows) + piece, BF16),
        pltpu.VMEM((depth, 2) + piece, BF16),
        pltpu.VMEM((depth,) + piece, BF16),
        pltpu.VMEM((depth,) + piece, BF16),
        pltpu.SemaphoreType.DMA((4, depth)),
        pltpu.SemaphoreType.DMA((8, depth)),
        pltpu.SemaphoreType.DMA((8, depth)),
    ]


def back(length, dh2, ct, x2, o, c, w, w_spec, fg, pg, hs, q, k, v, lse, grads, rows, ffn, block, head, factor, fused):
    seq, width = dh2.shape
    nb, pairs, heads = seq // block, width // (2 * head), width // head
    part = pl.BlockSpec((block, width), lambda i: (clip(i, 0, nb), 0))
    cols = pl.BlockSpec((seq, 2 * head), lambda i: (0, clip(i, nb, pairs)))
    smem = pl.BlockSpec(memory_space=pltpu.SMEM)
    hbm = pl.BlockSpec(memory_space=pl.ANY)
    vec, ovec = whole((1, width)), out_whole((1, width))
    out_specs = [part] * 2 + [cols] * 3 + [out_whole((heads, 128))] + [ovec] * 5
    out_shape = [sds((seq, width), F32), sds((seq, width), BF16)] + [sds((seq, width), BF16)] * 3
    out_shape += [sds((heads, 128), F32)] + [sds((1, width), F32)] * 5
    scratch = [
        pltpu.VMEM((seq, width), BF16), pltpu.VMEM((nb, heads, block), F32), pltpu.VMEM((seq, 2 * head), F32),
    ]
    if fused:
        piece = grads[0].shape[2:]
        out_specs += [pl.BlockSpec(memory_space=pltpu.VMEM)] * 2
        out_shape += [sds(piece, F32)] * 2
        scratch += scatter_scratch(piece, rows, ffn // 2) * 2
    else:
        grads = ()
    return pl.pallas_call(
        functools.partial(back_kernel, rows=rows, ffn=ffn, block=block, head=head, factor=factor, fused=fused),
        grid=(nb + pairs,),
        in_specs=[smem] + [part] * 5 + [w_spec] + [vec] * 3 + [cols] * 3
        + [pl.BlockSpec((1, 2, seq), lambda i: (clip(i, nb, pairs), 0, 0))] + [hbm] * len(grads),
        out_specs=out_specs,
        out_shape=out_shape,
        scratch_shapes=scratch,
        compiler_params=params(60 * MIB, has_side_effects=fused),
        name="backward_attention",
    )(length, dh2, ct, x2, o, c, w, fg, pg, hs, q, k, v, lse, *grads)


class AllSum:
    def __init__(self, place, stages, far, send, recv):
        self.place, self.stages, self.far, self.send, self.recv = place, stages, far, send, recv

    def copy(self, k):
        p = self.place
        device = (
            p.device(p.r, p.z, 1 - p.c), p.device(p.row_flip(p.r, 0), p.z, p.c), p.device(p.row_flip(p.r, 1), p.z, p.c)
        )[k]
        return remote(self.stages.at[k], self.stages.at[3 + k], self.send.at[k], self.recv.at[k], device)

    def along(self, d):
        p = self.place
        return remote(
            self.far.at[p.z], self.far.at[p.z], self.send.at[2 + d], self.recv.at[2 + d], p.device(p.r, p.z_at(d), p.c)
        )

    def begin(self):
        self.copy(0).start()

    def add(self, k):
        self.copy(k).wait_recv()
        total = self.stages[k] + self.stages[3 + k]
        if k < 2:
            self.stages[k + 1] = total
            self.copy(k + 1).start()
        else:
            self.far[self.place.z] = total
            for d in range(1, self.place.depth):
                self.along(d).start()

    def total(self):
        p = self.place
        for d in range(1, p.depth):
            there = self.far.at[p.z_at(-d)]
            pltpu.make_async_copy(there, there, self.recv.at[2 + d]).wait()
        out = self.far[0]
        for z in range(1, p.depth):
            out = out + self.far[z]
        return out

    def finish(self):
        for k in range(3):
            self.copy(k).wait_send()
        for d in range(1, self.place.depth):
            self.along(d).wait_send()


def last_kernel(*refs, rows, ffn, block, fused):
    (
        dq_ref, dk_ref, dv_ref, dor_ref, h_ref, c_ref, wq_ref, wk_ref, wv_ref, x_ref, dx2_ref, gain_ref, small_ref,
    ) = refs[:13]
    refs = refs[13:]
    dx_ref, small_out = refs[:2]
    refs = refs[2:]
    grad_refs = refs[:4]
    refs = refs[4:]
    if fused:
        grads = refs[:4]
        left_s, sums_s = refs[4:6]
        refs = refs[6:]
    else:
        grads = grad_refs
        left_s, sums_s = refs[:2]
    step = pl.program_id(0)
    seq, width = dq_ref.shape
    nb = seq // block
    last = 4 + nb - 1

    if fused:
        place = Place(rows, ffn)
        depth = place.depth
        jobs = []
        for n in range(4):
            bufs = refs[8 * n : 8 * n + 8]
            jobs.append(Scatter(place, by_device(grads[n]), *bufs[:5], bufs[5:]))
        small = AllSum(place, *refs[32:36])
        order = [d for d in (1, 2, 3) if d < depth] + [0]

        def core(job):
            for d in order:
                for k in (0, 1, 3, 2):
                    job.add_core(d, k)

        def first(job):
            for d in order:
                for k in (1, 0):
                    job.add_one(d, k)

        def second(job):
            for d in order:
                job.add_two(d)

    for n, right in enumerate((dor_ref, dv_ref, dk_ref, dq_ref)):

        @pl.when(step == n)
        def _(n=n, right=right):
            if n == 0:
                left_s[...] = c_ref[...].T
            if n == 1:
                left_s[...] = h_ref[...].T
            half = width // 2
            for part in range(2):
                cols = slice(part * half, (part + 1) * half)
                value = dot_nn(left_s[...], right[:, cols]).astype(BF16)
                if fused:
                    grads[n][..., cols] = value.reshape(grads[n].shape[:-1] + (half,))
                else:
                    grads[n][:, cols] = value
            if fused:
                for d in order:
                    jobs[n].begin(d)
                if n > 0:
                    core(jobs[n - 1])

    @pl.when(step >= 4)
    def _():
        here = pl.ds(pl.multiple_of((step - 4) * block, block), block)
        dq, dk, dv = dq_ref[here, :], dk_ref[here, :], dv_ref[here, :]

        @pl.when(step == 4)
        def _():
            sums_s[...] = jnp.zeros_like(sums_s)

        dh = (
            dot_nt(dq, wq_ref[...].reshape(width, width))
            + dot_nt(dk, wk_ref[...].reshape(width, width))
            + dot_nt(dv, wv_ref[...].reshape(width, width))
        )
        hat, inverse = norm_parts(x_ref[...].astype(F32))
        sums_s[0:1, :] += col_sum(dh * hat)
        sums_s[1:2, :] += col_sum(dh)
        sums_s[2:3, :] += col_sum(dq.astype(F32))
        sums_s[3:4, :] += col_sum(dv.astype(F32))
        dx_ref[...] = dx2_ref[...] + norm_back(dh * gain_ref[...], hat, inverse)

    if fused:
        at_steps(step, {
            4: [functools.partial(core, jobs[3]), functools.partial(first, jobs[0])],
            5: [functools.partial(first, jobs[1])],
            6: [functools.partial(first, jobs[2]), functools.partial(second, jobs[0])],
            7: [functools.partial(first, jobs[3]), functools.partial(second, jobs[1])],
        })

    @pl.when(step == last)
    def _():
        if fused:
            stages = refs[32]
            stages[0] = small_ref[...]
            stages[0, 0:4, :] = sums_s[0:4, :]
            small.begin()
            second(jobs[2])
            small.add(0)
            second(jobs[3])
            small.add(1)
            small.add(2)
            for job, out in zip(jobs, grad_refs):
                out[...] = job.total()
            small_out[...] = small.total()
            small.finish()
            for job in jobs:
                job.finish()
        else:
            small_out[...] = small_ref[...]
            small_out[0:4, :] = sums_s[0:4, :]


def last_stage(dq, dk, dv, dor, h, c, w, w_specs, x, dx2, gain, small, rows, ffn, block, fused):
    seq, width = dq.shape
    nb = seq // block
    part = pl.BlockSpec((block, width), lambda i: (clip(i, 4, nb), 0))
    full = whole((seq, width))
    piece = (width // (rows * ffn), width)
    depth = ffn // 2
    scratch = [pltpu.VMEM((width, seq), BF16), pltpu.VMEM((8, width), F32)]
    out_specs = [part, out_whole(small.shape)]
    out_shape = [sds((seq, width), F32), sds(small.shape, F32)]
    if fused:
        scratch = [pltpu.VMEM((rows, ffn) + piece, BF16)] * 4 + scratch + scatter_scratch(piece, rows, depth) * 4 + [
            pltpu.VMEM((6,) + small.shape, F32),
            pltpu.VMEM((depth,) + small.shape, F32),
            pltpu.SemaphoreType.DMA((2 + depth,)),
            pltpu.SemaphoreType.DMA((2 + depth,)),
        ]
        out_specs += [pl.BlockSpec(memory_space=pltpu.VMEM)] * 4
        out_shape += [sds(piece, F32)] * 4
    else:
        out_specs += [out_whole((width, width))] * 4
        out_shape += [sds((width, width), BF16)] * 4
    return pl.pallas_call(
        functools.partial(last_kernel, rows=rows, ffn=ffn, block=block, fused=fused),
        grid=(4 + nb,),
        in_specs=[full] * 6 + list(w_specs) + [part, part, whole((1, width)), whole(small.shape)],
        out_specs=out_specs,
        out_shape=out_shape,
        scratch_shapes=scratch,
        compiler_params=params(60 * MIB, has_side_effects=fused),
        name="input_and_weights",
    )(dq, dk, dv, dor, h, c, *[w] * 3, x, dx2, gain, small)


def widen(blocks, lanes):
    nb, rows, hb = blocks.shape
    group = max(1, lanes // hb)
    if group == 1:
        return blocks
    return blocks.reshape(nb // group, group, rows, hb).transpose(0, 2, 1, 3).reshape(nb // group, rows, group * hb)


def narrow(blocks, hb):
    nb, rows, lanes = blocks.shape
    group = lanes // hb
    if group == 1:
        return blocks
    return blocks.reshape(nb, rows, group, hb).transpose(0, 2, 1, 3).reshape(nb * group, rows, hb)


def rows_of(vector):
    return vector.reshape(1, -1)


def shards(
    tokens, lengths, cotangent, ln_attn_gain, ln_attn_bias, w_query, query_bias, w_key, w_value, value_bias,
    head_scale, w_out, out_bias, post_gain, post_bias, ffn_gain, ffn_bias, w_up, up_bias, mid_gain, mid_bias,
    w_down, down_bias,
):
    seq, width = tokens.shape
    heads = head_scale.shape[0]
    head = width // heads
    factor = head ** (-0.5)
    block = min(seq, 256)
    rows, ffn = lax.axis_size("rows"), lax.axis_size("ffn")
    own_units = w_up.shape[1]
    hidden = own_units * ffn
    fused = w_query.shape[0] % 16 == 0 and own_units % 128 == 0
    four = jnp.stack([w_query, w_key, w_value, w_out])
    vectors = [
        rows_of(v)
        for v in (
            ln_attn_gain, ln_attn_bias, query_bias, value_bias, out_bias, post_gain, post_bias, ffn_gain, ffn_bias,
        )
    ]
    if fused:
        weights = (four, w_down, w_up)
    else:
        attn, down_all, up_all = gather_all(rows, ffn, [four], [w_down, w_up])
        attn = attn.transpose(2, 0, 1, 3, 4).reshape(4, width, width)
        weights = (attn,)
    h, q, k, v, c, lse, o, x2, h2, *gathered = front(
        lengths, head_scale, tokens, vectors, weights, rows, ffn, block, head, factor, fused
    )
    if fused:
        attn, down_all, up_all = gathered

        def w_spec(i):
            return pl.BlockSpec(
                (rows, ffn, None) + four.shape[1:], lambda *_: (0, 0, i, 0, 0), pipeline_mode=pl.Buffered(1)
            )

    else:

        def w_spec(i):
            return pl.BlockSpec((None, width, width), lambda *_: (i, 0, 0), pipeline_mode=pl.Buffered(1))

    wup = widen(up_all.reshape(ffn, width, own_units), 512)
    wdn = widen(down_all.reshape(ffn, width, own_units), 512)
    nb, _, hb = wup.shape
    units = lambda vector: vector.reshape(nb, 1, hb)
    result, dh2, m, du, g_ub, g_mg, g_mb, g_db = feed_forward(
        lengths, h2, cotangent, x2, wup, wdn, units(up_bias), units(mid_gain), units(mid_bias), rows_of(down_bias),
        block,
    )
    g_up, g_dn = ffn_weight_grads(lengths, h2, cotangent, m, du)
    g_up, g_dn = (narrow(part, own_units).reshape((ffn, rows) + w_up.shape) for part in (g_up, g_dn))
    scale_cols = rows_of(jnp.repeat(head_scale, head))
    dx2, dor, dq, dk, dv, g_hs, g_fg, g_fb, g_pg, g_pb, g_ob, *summed = back(
        lengths, dh2, cotangent, x2, o, c, attn, w_spec(3), rows_of(ffn_gain), rows_of(post_gain), scale_cols, q, k, v,
        lse, (g_dn, g_up), rows, ffn, block, head, factor, fused,
    )
    if fused:
        grad_down, grad_up = summed
    else:
        grad_down, grad_up = (scatter_sum(rows, ffn, part, by_unit) for part in (g_dn, g_up))
    g_hs = jnp.pad(rows_of(g_hs[:, 0] / head_scale), ((0, 0), (0, width - heads)))
    wide = [part.reshape(-1, width) for part in (g_ub, g_mg, g_mb)]
    small = jnp.concatenate([jnp.zeros((4, width), F32), g_ob, g_pg, g_pb, g_fg, g_fb, g_db, g_hs] + wide, axis=0)
    small = jnp.pad(small, ((0, -small.shape[0] % 8), (0, 0)))
    dx, small, *attn_grads = last_stage(
        dq, dk, dv, dor, h, c, attn, [w_spec(i) for i in range(3)], tokens, dx2, rows_of(ln_attn_gain), small, rows, ffn,
        block, fused,
    )
    if not fused:
        small = lax.psum(small, BOTH)
        attn_grads = [
            scatter_sum(rows, ffn, part.reshape((rows, ffn) + w_query.shape), by_device) for part in attn_grads
        ]
    g_wo, g_wv, g_wk, g_wq = attn_grads
    n = hidden // width
    mine = lax.axis_index("ffn") * own_units
    g_ub, g_mg, g_mb = (
        lax.dynamic_slice(small[11 + i * n : 11 + (i + 1) * n].reshape(hidden), (mine,), (own_units,)) for i in range(3)
    )
    return (
        result, dx, small[0], small[1], g_wq, small[2], g_wk, g_wv, small[3], small[10, :heads], g_wo, small[4],
        small[5], small[6], small[7], small[8], grad_up, g_ub, g_mg, g_mb, grad_down, small[9],
    )


def solution(mesh):
    split = P(BOTH, None)
    tiles = P("rows", "ffn")
    one = P()
    return jax.shard_map(
        shards,
        mesh=mesh,
        in_specs=(
            split, P(BOTH), split, one, one, split, one, split, split, one, one, split, one, one, one, one, one,
            tiles, one, one, one, tiles, one,
        ),
        out_specs=(
            split, split, one, one, split, one, split, split, one, one, split, one, one, one, one, one,
            tiles, P("ffn"), P("ffn"), P("ffn"), tiles, one,
        ),
        check_vma=False,
    )
```

time: 848 us -> 469 us (0.55)
  waiting for transfers between devices: 463 us -> 0 us
  Pallas kernels: 249 us -> 446 us
  blocking collectives: 77 us -> 0 us
  other arithmetic: 17.1 us -> 1.8 us
  between operations: 15.1 us -> 1.48 us
    all_gather x5 -> x0, waiting for transfers between devices: 259 us -> none  [the longest x2 118 us: gather_blocks(): return lax.all_gather(over_ffn, 'rows', axis=1, tiled=True)]
    reduce_scatter x5 -> x0, waiting for transfers between devices: 202 us -> none  [the longest x2 76 us: scatter_blocks(): mine = lax.psum_scatter(grad, 'rows', scatter_dimension=1, tiled=True)]
    pallas_call x10 -> x3, Pallas kernels: 144 us -> 341 us  [the longest x1 136 us: front(): pl.pallas_call(functools.partial(front_kernel, rows=rows, ffn=ffn, block=...]
    psum x2 -> x0, blocking collectives: 47.5 us -> none  [the longest x1 38.1 us: shards(): small = lax.psum(small, BOTH)]
    unnamed x1 -> x0, blocking collectives: 29.5 us -> none
    pallas_call x2 -> x0, local copies, waits for them, and re-layouts: 11 us -> none  [the longest x1 5.61 us: out_backward(): pl.pallas_call(out_back_kernel, grid=(seq // block,), in_specs=[smem, row...]
    unnamed x29 -> x31, local copies, waits for them, and re-layouts: 0.67 us -> 10 us
  transfers between devices with their start and end apart: 10 -> 0, of which waited for: 9 -> 0; matrix products, arithmetic and copies ran while one was open for 5% -> 0% of each run, Pallas kernels for 17% -> 0%
where the time goes in v3:
time: 469 us; the launch traced here: 468 us
  Pallas kernels  446 us (95%)
  local copies, waits for them, and re-layouts  18.7 us (4%)
    pallas_call x1, Pallas kernels, front(): pl.pallas_call(functools.partial(front_kernel, rows=rows, ffn=ffn, block=...  136 us
    pallas_call x1, Pallas kernels, back(): pl.pallas_call(functools.partial(back_kernel, rows=rows, ffn=ffn, block=b...  119 us
    pallas_call x1, Pallas kernels, last_stage(): pl.pallas_call(functools.partial(last_kernel, rows=rows, ffn=ffn, block=b...  85.7 us
    pallas_call x1, Pallas kernels, feed_forward(): pl.pallas_call(ffn_kernel, grid=(seq // block,), in_specs=[smem, rows, ro...  81.2 us
    pallas_call x1, Pallas kernels, ffn_weight_grads(): pl.pallas_call(ffn_weights_kernel, grid=(nb,), in_specs=[smem, whole((seq...  24.1 us
    unnamed x31, local copies, waits for them, and re-layouts  10 us

profile of v3, /device:TPU:0, one launch (start us, length us, event | category | flops | bytes accessed | tf_op | source)
XLA Modules:
  0.0 468.2 jit_solution(15644735666710207111)
XLA Ops:
  1.3 1.7 pad_maximum_fusion.refs_12_
  3.0 135.7 %forward_attention.1 = (bf16[1024,1024]{1,0:T(8,128)(2,1)}, bf16[1024,1024]{1,0:T(8,128)(2,1)}, bf16[1024,1024]{1,0:T(8,128)(2,1)}, bf16[1024,1024]{1,0:T(8,128)...) custom-call(s32[1]{0:T(128)S(6)} %copy.59.refs_0_.length_ref, ...), custom_call_target="tpu_custom_call" | custom-call | tf_op jit(solution)/shard_map/forward_attention/pallas_call | solution.py:546
  138.7 81.2 %feed_forward.1 = (f32[1024,1024]{1,0:T(8,128)}, f32[1024,1024]{1,0:T(8,128)}, bf16[8,1024,512]{2,1,0:T(8,128)(2,1)}, bf16[8,1024,512]{2,1,0:T(8,128)(2,1)}, f32...) custom-call(s32[1]{0:T(128)S(6)} %copy.59.refs_0_.length_ref, ...), custom_call_target="tpu_custom_call" | custom-call | flops 68719476736 | bytes 62914560 | tf_op jit(solution)/shard_map/feed_forward/pallas_call | solution.py:631
  219.9 24.1 %ffn_weight_grads.1 = (bf16[8,1024,512]{2,1,0:T(8,128)(2,1)}, bf16[8,1024,512]{2,1,0:T(8,128)(2,1)}) custom-call(s32[1]{0:T(128)S(6)} %copy.59.refs_0_.length_ref, bf16[1024,1024]{1,0:T(8,128)(2,1)} %get-tuple-element.63.h2_ref, bf16[1024,1024]{1,0:T(8,128)(2,1)} %refs_2_.3, bf16[8,1024,512]{2,1,0:T(8,128)(2,1)} %get-tuple-element.76.m_ref, ...), custom_call_target="tpu_custom_call" | custom-call | flops 17179869184 | bytes 37748736 | tf_op jit(solution)/shard_map/ffn_weight_grads/pallas_call | solution.py:672
  244.1 0.1 broadcast_in_dim.6
  244.1 0.7 reshape_reshape.3.refs_9_
  244.8 119.4 %backward_attention.1 = (f32[1024,1024]{1,0:T(8,128)}, bf16[1024,1024]{1,0:T(8,128)(2,1)}, bf16[1024,1024]{1,0:T(8,128)(2,1)}, bf16[1024,1024]{1,0:T(8,128)(2,1)...) custom-call(s32[1]{0:T(128)S(6)} %copy.59.refs_0_.length_ref, ...), custom_call_target="tpu_custom_call" | custom-call | tf_op jit(solution)/shard_map/backward_attention/pallas_call | solution.py:872
  364.2 0.8 slice_reduce_fusion
  365.3 1.6 concatenate.3
  366.9 0.7 pad.9.refs_12_
  367.5 85.7 %input_and_weights.1 = (f32[1024,1024]{1,0:T(8,128)}, f32[24,1024]{1,0:T(8,128)}, f32[32,1024]{1,0:T(8,128)}, f32[32,1024]{1,0:T(8,128)}, f32[32,1024]{1,0:T(8,128)}, /*index=5*/f32[32,1024]{1,0:T(8,128)}) custom-call(bf16[1024,1024]{1,0:T(8,128)(2,1)} %get-tuple-element.80.refs_0_, bf16[1024,1024]{1,0:T(8,128)(2,1)} %get-tuple-element.81.refs_1_, ...), custom_call_target="tpu_custom_call" | custom-call | tf_op jit(solution)/shard_map/input_and_weights/pallas_call | solution.py:1074
  453.3 0.9 slice_bitcast_fusion
  454.2 0.7 dynamic_slice.11
  454.8 0.7 dynamic_slice.10
  455.5 0.7 dynamic_slice.9
  456.1 1.7 fusion
  457.8 1.2 slice_bitcast_fusion.3
  459.0 4.9 %copy.60 = f32[1024,1024]{1,0:T(8,128)} copy(f32[1024,1024]{1,0:T(8,128)} %get-tuple-element.142) | data formatting | bytes 8388608
  464.0 0.7 copy.61
  464.6 0.7 copy.62
  465.3 0.7 copy.63
  465.9 0.7 copy.64
  466.6 0.8 copy.65
  467.4 0.8 copy.66
  (33 shorter events, 0.2 us)
Async XLA Ops:
  219.9 24.1 %copy-start.10 = (f32[16]{0:T(128)S(1)}, f32[16]{0:T(128)}, u32[]{:S(2)}) copy-start(f32[16]{0:T(128)} %refs_1_.1) | copy-start | bytes 196
  244.8 120.2 %copy-start.8 = (f32[8,1,512]{2,1,0:T(1,128)S(1)}, f32[8,1,512]{2,1,0:T(1,128)}, u32[]{:S(2)}) copy-start(f32[8,1,512]{2,1,0:T(1,128)} %get-tuple-element.93) | copy-start | bytes 49156
  244.8 120.3 %copy-start.7 = (f32[8,1,512]{2,1,0:T(1,128)S(1)}, f32[8,1,512]{2,1,0:T(1,128)}, u32[]{:S(2)}) copy-start(f32[8,1,512]{2,1,0:T(1,128)} %get-tuple-element.94) | copy-start | bytes 49156
  244.8 120.4 %copy-start.6 = (f32[8,1,512]{2,1,0:T(1,128)S(1)}, f32[8,1,512]{2,1,0:T(1,128)}, u32[]{:S(2)}) copy-start(f32[8,1,512]{2,1,0:T(1,128)} %get-tuple-element.95) | copy-start | bytes 49156
  244.8 120.5 %copy-start.9 = (f32[1,1024]{1,0:T(1,128)S(1)}, f32[1,1024]{1,0:T(1,128)}, u32[]{:S(2)}) copy-start(f32[1,1024]{1,0:T(1,128)} %get-tuple-element.91) | copy-start | bytes 12292
  459.0 4.9 %copy-start.5 = (f32[32,1024]{1,0:T(8,128)S(1)}, f32[32,1024]{1,0:T(8,128)}, u32[]{:S(2)}) copy-start(f32[32,1024]{1,0:T(8,128)} %get-tuple-element.145) | copy-start | bytes 393220
  459.0 5.6 %copy-start.4 = (f32[32,1024]{1,0:T(8,128)S(1)}, f32[32,1024]{1,0:T(8,128)}, u32[]{:S(2)}) copy-start(f32[32,1024]{1,0:T(8,128)} %get-tuple-element.147) | copy-start | bytes 393220
  459.0 6.3 %copy-start.3 = (f32[32,1024]{1,0:T(8,128)S(1)}, f32[32,1024]{1,0:T(8,128)}, u32[]{:S(2)}) copy-start(f32[32,1024]{1,0:T(8,128)} %get-tuple-element.148) | copy-start | bytes 393220
  459.0 6.9 %copy-start.2 = (f32[32,1024]{1,0:T(8,128)S(1)}, f32[32,1024]{1,0:T(8,128)}, u32[]{:S(2)}) copy-start(f32[32,1024]{1,0:T(8,128)} %get-tuple-element.151) | copy-start | bytes 393220
  459.0 7.6 %copy-start.1 = (f32[256,512]{1,0:T(8,128)S(1)}, f32[256,512]{1,0:T(8,128)}, u32[]{:S(2)}) copy-start(f32[256,512]{1,0:T(8,128)} %get-tuple-element.157) | copy-start | bytes 1572868
  459.0 8.3 %copy-start = (f32[256,512]{1,0:T(8,128)S(1)}, f32[256,512]{1,0:T(8,128)}, u32[]{:S(2)}) copy-start(f32[256,512]{1,0:T(8,128)} %get-tuple-element.161) | copy-start | bytes 1572868

commit v4 on v3

--- a/solution.py
+++ b/solution.py
@@ -32,6 +32,10 @@
     return pltpu.CompilerParams(vmem_limit_bytes=limit, **kw)
 
 
+def comm_params(fused, number):
+    return dict(has_side_effects=True, collective_id=number) if fused else {}
+
+
 def whole(shape):
     return pl.BlockSpec(shape, lambda *_: (0,) * len(shape), pipeline_mode=pl.Buffered(1))
 
@@ -77,8 +81,29 @@
     def z_at(self, d):
         return lax.rem(self.z + d + self.depth, self.depth)
 
+    def near(self, k):
+        if self.depth != 4:
+            return self.z_at(k)
+        inward = 1 - 2 * (self.z // 2)
+        inner = lax.rem(self.z, 3) // 1
+        inner = inner - (inner // 2)
+        if k == 0:
+            return self.z
+        if k == 1:
+            return self.z + inward * (1 - 2 * inner)
+        return self.z + inward * (k - inner)
+
     def device(self, r, z, c):
         return (r, 2 * z + c)
+
+    def enter(self):
+        barrier = pltpu.get_barrier_semaphore()
+        partners = [self.device(self.r, self.z, 1 - self.c)]
+        partners += [self.device(self.row_flip(self.r, bit), self.z, self.c) for bit in range(2)]
+        partners += [self.device(self.r, self.z_at(d), self.c) for d in range(1, self.depth)]
+        for partner in partners:
+            pl.semaphore_signal(barrier, inc=1, device_id=partner, device_id_type=pl.DeviceIdType.MESH)
+        pl.semaphore_wait(barrier, len(partners))
 
 
 def remote(src, dst, send, recv, device):
@@ -88,138 +113,167 @@
 
 
 class Gather:
-    def __init__(self, place, src, view, local, send, recv):
-        self.place, self.src, self.view, self.local, self.send, self.recv = place, src, view, local, send, recv
-
-    def piece(self, r, z, c):
-        return self.view(r, 2 * z + c)
-
-    def arrival(self, r, z, c):
-        return self.recv.at[r, 2 * z + c]
-
-    def copy(self, src, kind, d, r, z, c, device):
-        return remote(src, self.piece(r, z, c), self.send.at[kind, d], self.arrival(r, z, c), device)
-
-    def wait_piece(self, r, z, c):
-        there = self.piece(r, z, c)
-        pltpu.make_async_copy(there, there, self.arrival(r, z, c)).wait()
-
-    def begin(self):
-        p = self.place
-        self.own_copy().start()
-        for d in range(1, p.depth):
-            self.copy(self.src, 0, d, p.r, p.z, p.c, p.device(p.r, p.z_at(d), p.c)).start()
-        self.spread(0, self.src)
-
-    def own_copy(self):
-        p = self.place
-        return pltpu.make_async_copy(self.src, self.piece(p.r, p.z, p.c), self.local)
+    def __init__(self, place, src, view, many, sems):
+        self.place, self.src, self.view, self.many = place, src, view, many
+        self.local, self.send, self.recv, self.core = sems
+
+    def copy(self, src, kind, r, z, c, device, arrival):
+        return remote(src, self.view(r, z, c), self.send.at[kind], arrival, device)
+
+    def to_near(self, src, kind, r, z, device):
+        self.copy(src, kind, r, z, self.place.c, device, self.recv.at[r, z]).start()
+
+    def wait_piece(self, r, z):
+        there = self.view(r, z, self.place.c)
+        pltpu.make_async_copy(there, there, self.recv.at[r, z]).wait()
 
     def bits(self, d):
         return (0, 1) if d % 2 == 0 else (1, 0)
 
+    def begin_z(self, d=0):
+        p = self.place
+        for k in range(1, p.depth):
+            self.to_near(self.src, 0, p.r, p.z, p.device(p.r, p.near(k), p.c))
+
+    def begin_rows(self, d=0):
+        p = self.place
+        pltpu.make_async_copy(self.src, self.view(p.r, p.z, p.c), self.local).start()
+        self.spread(0, self.src)
+
     def spread(self, d, src=None):
         p = self.place
-        z = p.z_at(-d)
-        first, second = self.bits(d)
-        src = self.piece(p.r, z, p.c) if src is None else src
-        self.copy(src, 1, d, p.r, z, p.c, p.device(p.row_flip(p.r, first), p.z, p.c)).start()
-        self.copy(src, 2, d, p.r, z, p.c, p.device(p.row_flip(p.r, second), p.z, p.c)).start()
-        self.hand_over(4, d, p.r, z, src)
-
-    def hand_over(self, kind, d, r, z, src=None):
-        p = self.place
-        src = self.piece(r, z, p.c) if src is None else src
-        self.copy(src, kind, d, r, z, p.c, p.device(p.r, p.z, 1 - p.c)).start()
+        z = p.near(d)
+        src = self.view(p.r, z, p.c) if src is None else src
+        for bit in self.bits(d):
+            self.to_near(src, 1, p.r, z, p.device(p.row_flip(p.r, bit), p.z, p.c))
+        self.hand_over(p.r, z, src)
+
+    def hand_over(self, r, z, src=None):
+        p = self.place
+        src = self.view(r, z, p.c) if src is None else src
+        self.copy(src, 2, r, z, p.c, p.device(p.r, p.z, 1 - p.c), self.core).start()
 
     def take_z(self, d):
         p = self.place
-        self.wait_piece(p.r, p.z_at(-d), p.c)
+        self.wait_piece(p.r, p.near(d))
         self.spread(d)
 
     def take_first(self, d):
         p = self.place
-        z = p.z_at(-d)
+        z = p.near(d)
         first, second = self.bits(d)
         r = p.row_flip(p.r, first)
-        self.wait_piece(r, z, p.c)
-        self.copy(
-            self.piece(r, z, p.c), 3, d, r, z, p.c, p.device(p.row_flip(p.r, second), p.z, p.c)
-        ).start()
-        self.hand_over(5, d, r, z)
-
-    def take_second(self, d):
-        p = self.place
-        r = p.row_flip(p.r, self.bits(d)[1])
-        z = p.z_at(-d)
-        self.wait_piece(r, z, p.c)
-        self.hand_over(6, d, r, z)
-
-    def take_both(self, d):
-        p = self.place
-        r = p.row_flip(p.row_flip(p.r, 0), 1)
-        z = p.z_at(-d)
-        self.wait_piece(r, z, p.c)
-        self.hand_over(7, d, r, z)
+        self.wait_piece(r, z)
+        self.to_near(self.view(r, z, p.c), 1, r, z, p.device(p.row_flip(p.r, second), p.z, p.c))
+        self.hand_over(r, z)
+
+    def take_rest(self, d):
+        p = self.place
+        z = p.near(d)
+        for r in (p.row_flip(p.r, self.bits(d)[1]), p.row_flip(p.row_flip(p.r, 0), 1)):
+            self.wait_piece(r, z)
+            self.hand_over(r, z)
 
     def finish(self):
         p = self.place
-        self.own_copy().wait()
-        for d in range(p.depth):
-            for r in range(p.rows):
-                self.wait_piece(r, p.z_at(-d), 1 - p.c)
-        there = self.src
-        for d in range(p.depth):
-            for kind in range(8):
-                if kind > 0 or d > 0:
-                    pltpu.make_async_copy(there, there, self.send.at[kind, d]).wait()
-
-
-def gather_kernel(*refs, rows, ffn, views):
-    n = len(views)
-    src, dst = refs[:n], refs[n : 2 * n]
-    local, send, recv = refs[2 * n :]
+        pltpu.make_async_copy(self.src, self.view(p.r, p.z, p.c), self.local).wait()
+        half = self.many(slice(None), slice(None), p.c)
+        pltpu.make_async_copy(half, half, self.core).wait()
+        pltpu.make_async_copy(half, half, self.send.at[2]).wait()
+        part = self.many(slice(0, 3), slice(None), p.c)
+        pltpu.make_async_copy(part, part, self.send.at[1]).wait()
+        part = self.many(0, slice(0, p.depth - 1), p.c)
+        pltpu.make_async_copy(part, part, self.send.at[0]).wait()
+
+
+def gather_sems(jobs, rows, depth):
+    dma = pltpu.SemaphoreType.DMA
+    return [dma((jobs,)), dma((jobs, 3)), dma((jobs, rows, depth)), dma((jobs,))]
+
+
+def gather_jobs(place, four, four_all, down, down_all, up, up_all, sems):
+    local, send, recv, core = sems
+    jobs = []
+
+    def add(src, many):
+        n = len(jobs)
+        jobs.append(Gather(place, src, many, many, (local.at[n], send.at[n], recv.at[n], core.at[n])))
+
+    for i in range(4):
+        add(four.at[i], lambda r, z, c, i=i: four_all.at[r, z, c, i])
+    half = down.shape[0] // 2
+    for src, out in ((down, down_all), (up, up_all)):
+        for i in range(2):
+            part = pl.ds(i * half, half)
+            add(src.at[part], lambda r, z, c, out=out, part=part: out.at[z, c, r, part])
+    return jobs
+
+
+def gather_kernel(four, down, up, four_all, down_all, up_all, *sems, rows, ffn):
     place = Place(rows, ffn)
-    jobs = [
-        Gather(place, src[i], views[i](dst[i]), local.at[i], send.at[i], recv.at[i]) for i in range(n)
-    ]
+    jobs = gather_jobs(place, four, four_all, down, down_all, up, up_all, sems)
+    place.enter()
     for job in jobs:
-        job.begin()
-    for step in ("take_z", "take_first", "take_second", "take_both"):
-        for job in jobs:
-            for d in range(1 if step == "take_z" else 0, place.depth):
-                getattr(job, step)(d)
+        job.begin_z()
+        job.begin_rows()
     for job in jobs:
+        for d in range(1, place.depth):
+            job.take_z(d)
+    for job in jobs:
+        for d in range(place.depth):
+            job.take_first(d)
+    for job in jobs:
+        for d in range(place.depth):
+            job.take_rest(d)
         job.finish()
 
 
-def by_device(ref):
-    return lambda r, f: ref.at[r, f]
-
-
-def by_unit(ref):
-    return lambda r, f: ref.at[f, r]
-
-
-def gather_all(rows, ffn, by_rows, by_units):
-    src = list(by_rows) + list(by_units)
-    shapes = [(rows, ffn) + a.shape for a in by_rows] + [(ffn, rows) + a.shape for a in by_units]
-    views = (by_device,) * len(by_rows) + (by_unit,) * len(by_units)
-    n = len(src)
+def gathered_shapes(rows, ffn, four, down, up):
+    depth = ffn // 2
+    return [sds((rows, depth, 2) + four.shape, BF16)] + [sds((depth, 2, rows) + a.shape, BF16) for a in (down, up)]
+
+
+def gather_all(rows, ffn, four, down, up):
     hbm = pl.BlockSpec(memory_space=pl.ANY)
     return pl.pallas_call(
-        functools.partial(gather_kernel, rows=rows, ffn=ffn, views=views),
-        in_specs=[hbm] * n,
-        out_specs=[hbm] * n,
-        out_shape=[sds(s, BF16) for s in shapes],
-        scratch_shapes=[
-            pltpu.SemaphoreType.DMA((n,)),
-            pltpu.SemaphoreType.DMA((n, 8, ffn // 2)),
-            pltpu.SemaphoreType.DMA((n, rows, ffn)),
-        ],
-        compiler_params=pltpu.CompilerParams(has_side_effects=True),
+        functools.partial(gather_kernel, rows=rows, ffn=ffn),
+        in_specs=[hbm] * 3,
+        out_specs=[hbm] * 3,
+        out_shape=gathered_shapes(rows, ffn, four, down, up),
+        scratch_shapes=gather_sems(8, rows, ffn // 2),
+        compiler_params=pltpu.CompilerParams(has_side_effects=True, collective_id=3),
         name="gather_all",
-    )(*src)
+    )(four, down, up)
+
+
+ROWS_FIRST = 8
+STRIDE = 6
+BACK_FROM = 0
+BACK_STRIDE = 4
+LAST_ONE = 2
+LAST_TWO = 4
+LAST_ORDER = ("leave", "add_one", "add_two", "stay")
+
+
+def gather_rounds(jobs, depth, rows_first):
+    rounds = [[(n, "begin_rows", 0) for n in range(rows_first)]]
+    for t in range(jobs + 2):
+        todo = []
+        if t < jobs:
+            todo += [(t, "begin_rows", 0)] if t >= rows_first else []
+            todo += [(t, "take_z", d) for d in range(1, depth)]
+        rounds.append(todo)
+        rounds.append([(t - 1, "take_first", d) for d in range(depth)] if 0 <= t - 1 < jobs else [])
+        rounds.append([(t - 2, "take_rest", d) for d in range(depth)] if 0 <= t - 2 < jobs else [])
+    return rounds
+
+
+def by_device(ref):
+    return lambda r, z, c: ref.at[r, z, c]
+
+
+def by_unit(ref, part=slice(None)):
+    return lambda r, z, c: ref.at[z, c, r, part]
 
 
 class Scatter:
@@ -230,124 +284,129 @@
     def bits(self, d):
         return (0, 1) if d % 2 == 0 else (1, 0)
 
-    def copy(self, src, dst, kind, d, device):
-        return remote(src, dst, self.send.at[kind, d], self.recv.at[kind, d], device)
-
-    def to_core(self, d, r):
-        p = self.place
-        z = p.z_at(d)
-        return self.copy(
-            self.view(r, 2 * z + 1 - p.c), self.half.at[d, r], r, d, p.device(p.r, p.z, 1 - p.c)
-        )
+    def sum_at(self, d, r):
+        if self.own is None:
+            return self.view(r, self.place.z_at(d), self.place.c)
+        return self.own.at[d, r]
+
+    def copy(self, src, dst, kind, arrival, d, device):
+        return remote(src, dst, self.send.at[kind], self.recv.at[arrival, d], device)
 
     def fetch(self, d, r):
         p = self.place
-        return pltpu.make_async_copy(self.view(r, 2 * p.z_at(d) + p.c), self.own.at[d, r], self.load.at[r, d])
+        return pltpu.make_async_copy(self.view(r, p.z_at(d), p.c), self.own.at[d, r], self.load.at[r, d])
 
     def begin(self, d):
-        for r in range(4):
-            self.to_core(d, r).start()
-            self.fetch(d, r).start()
-
-    def exchange_one(self, d, k):
+        p = self.place
+        first, _ = self.bits(d)
+        leaving = p.row_flip(p.r, first)
+        for base in (leaving, p.r):
+            for r in (base, p.row_flip(base, 1 - first)):
+                self.copy(
+                    self.view(r, p.z_at(d), 1 - p.c), self.half.at[d, r], 0, r, d, p.device(p.r, p.z, 1 - p.c)
+                ).start()
+                if self.own is not None:
+                    self.fetch(d, r).start()
+
+    def arrived(self, ref, arrival, d):
+        pltpu.make_async_copy(ref, ref, self.recv.at[arrival, d]).wait()
+
+    def add(self, d, r, ref):
+        here = self.sum_at(d, r)
+        here[...] = here[...] + ref[...]
+
+    def add_half(self, d, r):
+        if self.own is not None:
+            self.fetch(d, r).wait()
+        self.arrived(self.half.at[d, r], r, d)
+        self.add(d, r, self.half.at[d, r])
+
+    def leave(self, d):
         p = self.place
         first, second = self.bits(d)
         partner = p.row_flip(p.r, first)
-        r = partner if k == 0 else p.row_flip(partner, second)
-        return self.copy(self.own.at[d, r], self.pair.at[d, k], 4 + k, d, p.device(partner, p.z, p.c))
-
-    def exchange_two(self, d):
+        for k, r in enumerate((partner, p.row_flip(partner, second))):
+            self.add_half(d, r)
+            self.copy(self.sum_at(d, r), self.pair.at[d, k], 1, 4 + k, d, p.device(partner, p.z, p.c)).start()
+
+    def stay(self, d):
+        p = self.place
+        for r in (p.row_flip(p.r, self.bits(d)[1]), p.r):
+            self.add_half(d, r)
+
+    def add_one(self, d):
         p = self.place
         partner = p.row_flip(p.r, self.bits(d)[1])
-        return self.copy(self.own.at[d, partner], self.last.at[d], 6, d, p.device(partner, p.z, p.c))
-
-    def along(self, d):
-        p = self.place
-        return self.copy(self.own.at[d, p.r], self.far.at[d], 7, d, p.device(p.r, p.z_at(d), p.c))
-
-    def add_core(self, d, k):
-        p = self.place
-        first, second = self.bits(d)
-        base = p.row_flip(p.r, first) if k < 2 else p.r
-        r = base if k % 2 == 0 else p.row_flip(base, second)
-        pltpu.make_async_copy(self.own.at[d, r], self.own.at[d, r], self.load.at[r, d]).wait()
-        pltpu.make_async_copy(self.half.at[d, r], self.half.at[d, r], self.recv.at[r, d]).wait()
-        self.own[d, r] = self.own[d, r] + self.half[d, r]
-        if k < 2:
-            self.exchange_one(d, k).start()
-
-    def add_one(self, d, k):
-        p = self.place
-        r = p.r if k == 0 else p.row_flip(p.r, self.bits(d)[1])
-        self.exchange_one(d, k).wait_recv()
-        self.own[d, r] = self.own[d, r] + self.pair[d, k]
-        if k == 1:
-            self.exchange_two(d).start()
+        for k, r in ((1, partner), (0, p.r)):
+            self.arrived(self.pair.at[d, k], 4 + k, d)
+            self.add(d, r, self.pair.at[d, k])
+            if k == 1:
+                self.copy(self.sum_at(d, r), self.last.at[d], 2, 6, d, p.device(partner, p.z, p.c)).start()
 
     def add_two(self, d):
         p = self.place
-        self.exchange_two(d).wait_recv()
-        self.own[d, p.r] = self.own[d, p.r] + self.last[d]
+        self.arrived(self.last.at[d], 6, d)
+        self.add(d, p.r, self.last.at[d])
         if d > 0:
-            self.along(d).start()
+            self.copy(self.sum_at(d, p.r), self.far.at[d], 3, 7, d, p.device(p.r, p.z_at(d), p.c)).start()
 
     def total(self):
         p = self.place
-        out = self.own[0, p.r].astype(F32)
+        out = self.sum_at(0, p.r)[...].astype(F32)
         for d in range(1, p.depth):
-            self.along(d).wait_recv()
+            self.arrived(self.far.at[d], 7, d)
             out = out + self.far[d].astype(F32)
         return out
 
     def finish(self):
-        p = self.place
-        for d in range(p.depth):
-            for r in range(4):
-                self.to_core(d, r).wait_send()
-            for k in range(2):
-                self.exchange_one(d, k).wait_send()
-            self.exchange_two(d).wait_send()
-            if d > 0:
-                self.along(d).wait_send()
+        for kind, ref in enumerate((self.half, self.pair, self.last, self.far.at[pl.ds(1, self.place.depth - 1)])):
+            pltpu.make_async_copy(ref, ref, self.send.at[kind]).wait()
+
+
+def scatter_rounds(jobs, depth):
+    order = list(range(1, depth)) + [0]
+    rounds = []
+    for t in range(jobs + 2):
+        rounds.append([(t, "leave", d) for d in order] if t < jobs else [])
+        rounds.append([(t - 1, "add_one", d) for d in order] if 0 <= t - 1 < jobs else [])
+        rounds.append([(t - 2, "add_two", d) for d in order] if 0 <= t - 2 < jobs else [])
+        rounds.append([(t, "stay", d) for d in order] if t < jobs else [])
+    return rounds
 
 
 def scatter_kernel(src, out, own, half, pair, last, far, load, send, recv, *, rows, ffn, view):
     place = Place(rows, ffn)
     job = Scatter(place, view(src), own, half, pair, last, far, (load, send, recv))
     order = list(range(1, place.depth)) + [0]
-    for d in order:
-        job.begin(d)
-    for d in order:
-        for k in (0, 1, 3, 2):
-            job.add_core(d, k)
-    for d in order:
-        for k in (1, 0):
-            job.add_one(d, k)
-    for d in order:
-        job.add_two(d)
+    place.enter()
+    for name in ("begin", "leave", "stay", "add_one", "add_two"):
+        for d in order:
+            getattr(job, name)(d)
     out[...] = job.total()
     job.finish()
 
 
+def scatter_scratch(piece, rows, depth, own):
+    return ([pltpu.VMEM((depth, rows) + piece, BF16)] if own else []) + [
+        pltpu.VMEM((depth, rows) + piece, BF16),
+        pltpu.VMEM((depth, 2) + piece, BF16),
+        pltpu.VMEM((depth,) + piece, BF16),
+        pltpu.VMEM((depth,) + piece, BF16),
+        pltpu.SemaphoreType.DMA((4, depth)),
+        pltpu.SemaphoreType.DMA((4,)),
+        pltpu.SemaphoreType.DMA((8, depth)),
+    ]
+
+
 def scatter_sum(rows, ffn, grad, view):
-    piece = grad.shape[2:]
-    depth = ffn // 2
+    piece = grad.shape[3:]
     return pl.pallas_call(
         functools.partial(scatter_kernel, rows=rows, ffn=ffn, view=view),
         in_specs=[pl.BlockSpec(memory_space=pl.ANY)],
         out_specs=pl.BlockSpec(memory_space=pltpu.VMEM),
         out_shape=sds(piece, F32),
-        scratch_shapes=[
-            pltpu.VMEM((depth, rows) + piece, BF16),
-            pltpu.VMEM((depth, rows) + piece, BF16),
-            pltpu.VMEM((depth, 2) + piece, BF16),
-            pltpu.VMEM((depth,) + piece, BF16),
-            pltpu.VMEM((depth,) + piece, BF16),
-            pltpu.SemaphoreType.DMA((4, depth)),
-            pltpu.SemaphoreType.DMA((8, depth)),
-            pltpu.SemaphoreType.DMA((8, depth)),
-        ],
-        compiler_params=params(has_side_effects=True),
+        scratch_shapes=scatter_scratch(piece, rows, ffn // 2, True),
+        compiler_params=params(has_side_effects=True, collective_id=4),
         name="scatter_sum",
     )(grad)
 
@@ -357,7 +416,7 @@
 
 
 def at_steps(step, plan):
-    for when, actions in plan.items():
+    for when, actions in sorted(plan.items()):
 
         @pl.when(step == when)
         def _(actions=actions):
@@ -414,49 +473,35 @@
 
     late = {}
     if fused:
-        local, send, recv = refs[6:9]
         place = Place(rows, ffn)
-        views = (by_device, by_unit, by_unit)
-        four, down, up = (
-            Gather(place, comm_in[i], views[i](comm_out[i]), local.at[i], send.at[i], recv.at[i]) for i in range(3)
+        jobs = gather_jobs(
+            place, comm_in[0], comm_out[0], comm_in[1], comm_out[1], comm_in[2], comm_out[2], refs[6:10]
         )
-        depth = place.depth
-        every = range(depth)
+        rounds = gather_rounds(len(jobs), place.depth, ROWS_FIRST)
+        cut = 1 + 3 * 6
+        opening = sum(rounds[:cut], [])
+        table = {}
+        for k, keys in enumerate(rounds[cut:]):
+            table.setdefault(min(1 + k * STRIDE // 4, last), []).extend(keys)
+
+        def actions(keys):
+            return [functools.partial(getattr(jobs[n], name), d) for n, name, d in keys]
 
         @pl.when(step == 0)
         def _():
-            four.begin()
-            for d in range(1, depth):
-                four.take_z(d)
-            down.begin()
-            for d in every:
-                four.take_first(d)
-            for d in every:
-                four.take_second(d)
-            for d in every:
-                four.take_both(d)
-            up.begin()
-            four.finish()
-            load_weights(lambda i: comm_out[0].at[:, :, i])
-
-        def do(job, name, *ds):
-            return [functools.partial(getattr(job, name), d) for d in ds if d < depth]
-
-        late = {
-            1: do(down, "take_z", 1) + do(down, "take_first", 0),
-            2: do(down, "take_z", 2) + do(down, "take_first", 1),
-            3: do(down, "take_z", 3) + do(down, "take_second", 0),
-            4: do(down, "take_first", 2) + do(up, "take_z", 1),
-            5: do(down, "take_first", 3) + do(down, "take_second", 1) + do(up, "take_z", 2),
-            6: do(down, "take_both", 0, 1) + do(down, "take_second", 2) + do(up, "take_z", 3),
-            7: do(down, "take_second", 3) + do(up, "take_first", 0),
-            8: do(down, "take_both", 2, 3) + do(up, "take_first", 1),
-            9: do(up, "take_first", 2) + do(up, "take_second", 0),
-            10: do(up, "take_first", 3) + do(up, "take_second", 1),
-            11: do(up, "take_second", 2),
-            12: do(up, "take_second", 3) + do(up, "take_both", 0),
-            13: do(up, "take_both", 1),
-        }
+            place.enter()
+            for job in jobs:
+                job.begin_z()
+            for action in actions(opening):
+                action()
+            copies = [pltpu.make_async_copy(comm_out[0].at[:, :, :, i], w_s.at[i], load.at[i]) for i in range(4)]
+            for job, copy in zip(jobs, copies):
+                job.finish()
+                copy.start()
+            for copy in copies:
+                copy.wait()
+
+        late = {i: actions(keys) for i, keys in table.items() if keys and i < last}
         at_steps(step, late)
     else:
 
@@ -512,11 +557,10 @@
 
         @pl.when(step == last)
         def _():
-            for d in (2, 3):
-                if d < depth:
-                    up.take_both(d)
-            down.finish()
-            up.finish()
+            for action in actions(table.get(last, [])):
+                action()
+            for job in jobs[4:]:
+                job.finish()
 
 
 def front(length, scale, x, vectors, weights, rows, ffn, block, head, factor, fused):
@@ -534,13 +578,10 @@
     scratch = [pltpu.VMEM((seq, width), BF16)] * 4 + [pltpu.SemaphoreType.DMA((4,))]
     if fused:
         four, down, up = weights
-        out_shape += [sds((rows, ffn) + four.shape, BF16)] + [sds((ffn, rows) + a.shape, BF16) for a in (down, up)]
+        out_shape += gathered_shapes(rows, ffn, four, down, up)
         out_specs += [hbm] * 3
-        scratch = [pltpu.VMEM((4, rows, ffn) + four.shape[1:], BF16)] + scratch + [
-            pltpu.SemaphoreType.DMA((3,)),
-            pltpu.SemaphoreType.DMA((3, 8, ffn // 2)),
-            pltpu.SemaphoreType.DMA((3, rows, ffn)),
-        ]
+        scratch = [pltpu.VMEM((4, rows, ffn // 2, 2) + four.shape[1:], BF16)] + scratch
+        scratch += gather_sems(8, rows, ffn // 2)
     else:
         scratch = [pltpu.VMEM((4, width, width), BF16)] + scratch
     return pl.pallas_call(
@@ -550,7 +591,7 @@
         out_specs=out_specs,
         out_shape=out_shape,
         scratch_shapes=scratch,
-        compiler_params=params(60 * MIB, has_side_effects=fused),
+        compiler_params=params(60 * MIB, **comm_params(fused, 0)),
         name="forward_attention",
     )(length, scale, x, *vectors, *weights)
 
@@ -592,7 +633,7 @@
         return tuple(s + jnp.sum(t, axis=-1, keepdims=True) for s, t in zip(sums, terms))
 
     zero = jnp.zeros((block, 1), F32)
-    sum_e, sum_ee, sum_d, sum_de = lax.fori_loop(0, nb, first, (zero,) * 4)
+    sum_e, sum_ee, sum_d, sum_de = lax.fori_loop(0, nb, first, (zero,) * 4, unroll=2)
     mu = sum_e / units
     inverse = lax.rsqrt(sum_ee / units - mu * mu + epsilon)
     mean_d = sum_d / units
@@ -615,7 +656,7 @@
         return f, dh2
 
     zeros = jnp.zeros((block, width), F32)
-    f, dh2 = lax.fori_loop(0, nb, second, (zeros, zeros))
+    f, dh2 = lax.fori_loop(0, nb, second, (zeros, zeros), unroll=2)
     res_ref[...] = jnp.where(valid, x2_ref[...] + f + db_ref[...], 0.0)
     dh2_ref[...] = dh2
 
@@ -739,37 +780,24 @@
         place = Place(rows, ffn)
         depth = place.depth
         jobs = []
-        for n in range(2):
+        half = comm_out[0].shape[0] // 2
+        for n in range(4):
             bufs = refs[3 + 8 * n : 11 + 8 * n]
-            jobs.append(Scatter(place, by_unit(comm_in[n]), *bufs[:5], bufs[5:]))
-        one, two = jobs
-        order = [d for d in (1, 2, 3) if d < depth] + [0]
-
-        @pl.when(step == 0)
-        def _():
-            for job in jobs:
-                for d in order:
-                    job.begin(d)
-
-        def core(job, *ds):
-            return [functools.partial(job.add_core, d, k) for d in ds if d < depth for k in (0, 1, 3, 2)]
-
-        def first(job, *ds):
-            return [functools.partial(job.add_one, d, k) for d in ds if d < depth for k in (1, 0)]
-
-        def second(job, *ds):
-            return [functools.partial(job.add_two, d) for d in ds if d < depth]
-
-        at_steps(step, {
-            2: core(one, 1, 2),
-            3: core(one, 3, 0),
-            4: core(two, 1, 2),
-            5: core(two, 3, 0),
-            6: first(one, 1, 2),
-            7: first(one, 3, 0),
-            8: second(one, 1, 2, 3),
-            10: first(two, 1, 2) + second(one, 0),
-        })
+            part = pl.ds(n % 2 * half, half)
+            jobs.append(Scatter(place, by_unit(comm_in[n // 2], part), *bufs[:5], bufs[5:]))
+        rounds = scatter_rounds(4, depth)
+        table = {}
+        for k, keys in enumerate(rounds):
+            table.setdefault(min(max(0, k - BACK_FROM) * BACK_STRIDE // 8, last), []).extend(keys)
+
+        def actions(keys):
+            return [functools.partial(getattr(jobs[n], name), d) for n, name, d in keys]
+
+        order = list(range(1, depth)) + [0]
+        begin = [functools.partial(job.begin, d) for job in jobs for d in order]
+        plan = {i: actions(keys) for i, keys in table.items() if i < last}
+        plan[0] = [place.enter] + begin + plan[0]
+        at_steps(step, {i: todo for i, todo in plan.items() if todo})
 
     @pl.when(step < nb)
     def _():
@@ -828,24 +856,11 @@
 
         @pl.when(step == last)
         def _():
-            for action in first(two, 3, 0) + second(two, 1, 2, 3, 0):
+            for action in actions(table.get(last, [])):
                 action()
-            for job, out in zip(jobs, comm_out):
-                out[...] = job.total()
+            for n, job in enumerate(jobs):
+                comm_out[n // 2][n % 2 * half : (n % 2 + 1) * half, :] = job.total()
                 job.finish()
-
-
-def scatter_scratch(piece, rows, depth):
-    return [
-        pltpu.VMEM((depth, rows) + piece, BF16),
-        pltpu.VMEM((depth, rows) + piece, BF16),
-        pltpu.VMEM((depth, 2) + piece, BF16),
-        pltpu.VMEM((depth,) + piece, BF16),
-        pltpu.VMEM((depth,) + piece, BF16),
-        pltpu.SemaphoreType.DMA((4, depth)),
-        pltpu.SemaphoreType.DMA((8, depth)),
-        pltpu.SemaphoreType.DMA((8, depth)),
-    ]
 
 
 def back(length, dh2, ct, x2, o, c, w, w_spec, fg, pg, hs, q, k, v, lse, grads, rows, ffn, block, head, factor, fused):
@@ -863,10 +878,10 @@
         pltpu.VMEM((seq, width), BF16), pltpu.VMEM((nb, heads, block), F32), pltpu.VMEM((seq, 2 * head), F32),
     ]
     if fused:
-        piece = grads[0].shape[2:]
+        piece = grads[0].shape[3:]
         out_specs += [pl.BlockSpec(memory_space=pltpu.VMEM)] * 2
         out_shape += [sds(piece, F32)] * 2
-        scratch += scatter_scratch(piece, rows, ffn // 2) * 2
+        scratch += scatter_scratch((piece[0] // 2, piece[1]), rows, ffn // 2, True) * 4
     else:
         grads = ()
     return pl.pallas_call(
@@ -877,7 +892,7 @@
         out_specs=out_specs,
         out_shape=out_shape,
         scratch_shapes=scratch,
-        compiler_params=params(60 * MIB, has_side_effects=fused),
+        compiler_params=params(60 * MIB, **comm_params(fused, 1)),
         name="backward_attention",
     )(length, dh2, ct, x2, o, c, w, fg, pg, hs, q, k, v, lse, *grads)
 
@@ -956,24 +971,23 @@
         depth = place.depth
         jobs = []
         for n in range(4):
-            bufs = refs[8 * n : 8 * n + 8]
-            jobs.append(Scatter(place, by_device(grads[n]), *bufs[:5], bufs[5:]))
-        small = AllSum(place, *refs[32:36])
-        order = [d for d in (1, 2, 3) if d < depth] + [0]
-
-        def core(job):
-            for d in order:
-                for k in (0, 1, 3, 2):
-                    job.add_core(d, k)
-
-        def first(job):
-            for d in order:
-                for k in (1, 0):
-                    job.add_one(d, k)
-
-        def second(job):
-            for d in order:
-                job.add_two(d)
+            bufs = refs[7 * n : 7 * n + 7]
+            jobs.append(Scatter(place, by_device(grads[n]), None, *bufs[:4], bufs[4:]))
+        small = AllSum(place, *refs[28:32])
+        table = {}
+        for n in range(4):
+            for k, (name, when) in enumerate((("leave", 1), ("stay", 1), ("add_one", 1 + LAST_ONE), ("add_two", 1 + LAST_TWO))):
+                table.setdefault(min(n + when, last + 1), []).extend((n, name, d) for d in list(range(1, depth)) + [0])
+
+        def actions(keys):
+            return [functools.partial(getattr(jobs[n], name), d) for n, name, d in keys]
+
+        order = list(range(1, depth)) + [0]
+        plan = {i: actions(sorted(keys, key=lambda key: LAST_ORDER.index(key[1]))) for i, keys in table.items() if i <= last}
+        rest = table.get(last + 1, [])
+        plan[0] = []
+        plan[0] = [place.enter] + plan[0]
+        at_steps(step, {i: todo for i, todo in plan.items() if todo})
 
     for n, right in enumerate((dor_ref, dv_ref, dk_ref, dq_ref)):
 
@@ -994,8 +1008,6 @@
             if fused:
                 for d in order:
                     jobs[n].begin(d)
-                if n > 0:
-                    core(jobs[n - 1])
 
     @pl.when(step >= 4)
     def _():
@@ -1018,24 +1030,19 @@
         sums_s[3:4, :] += col_sum(dv.astype(F32))
         dx_ref[...] = dx2_ref[...] + norm_back(dh * gain_ref[...], hat, inverse)
 
-    if fused:
-        at_steps(step, {
-            4: [functools.partial(core, jobs[3]), functools.partial(first, jobs[0])],
-            5: [functools.partial(first, jobs[1])],
-            6: [functools.partial(first, jobs[2]), functools.partial(second, jobs[0])],
-            7: [functools.partial(first, jobs[3]), functools.partial(second, jobs[1])],
-        })
-
     @pl.when(step == last)
     def _():
         if fused:
-            stages = refs[32]
+            stages = refs[28]
             stages[0] = small_ref[...]
             stages[0, 0:4, :] = sums_s[0:4, :]
             small.begin()
-            second(jobs[2])
+            half = len(rest) // 2
+            for action in actions(rest[:half]):
+                action()
             small.add(0)
-            second(jobs[3])
+            for action in actions(rest[half:]):
+                action()
             small.add(1)
             small.add(2)
             for job, out in zip(jobs, grad_refs):
@@ -1060,7 +1067,8 @@
     out_specs = [part, out_whole(small.shape)]
     out_shape = [sds((seq, width), F32), sds(small.shape, F32)]
     if fused:
-        scratch = [pltpu.VMEM((rows, ffn) + piece, BF16)] * 4 + scratch + scatter_scratch(piece, rows, depth) * 4 + [
+        scratch = [pltpu.VMEM((rows, depth, 2) + piece, BF16)] * 4 + scratch
+        scratch += scatter_scratch(piece, rows, depth, False) * 4 + [
             pltpu.VMEM((6,) + small.shape, F32),
             pltpu.VMEM((depth,) + small.shape, F32),
             pltpu.SemaphoreType.DMA((2 + depth,)),
@@ -1078,7 +1086,7 @@
         out_specs=out_specs,
         out_shape=out_shape,
         scratch_shapes=scratch,
-        compiler_params=params(60 * MIB, has_side_effects=fused),
+        compiler_params=params(60 * MIB, **comm_params(fused, 2)),
         name="input_and_weights",
     )(dq, dk, dv, dor, h, c, *[w] * 3, x, dx2, gain, small)
 
@@ -1127,8 +1135,8 @@
     if fused:
         weights = (four, w_down, w_up)
     else:
-        attn, down_all, up_all = gather_all(rows, ffn, [four], [w_down, w_up])
-        attn = attn.transpose(2, 0, 1, 3, 4).reshape(4, width, width)
+        attn, down_all, up_all = gather_all(rows, ffn, four, w_down, w_up)
+        attn = attn.transpose(3, 0, 1, 2, 4, 5).reshape(4, width, width)
         weights = (attn,)
     h, q, k, v, c, lse, o, x2, h2, *gathered = front(
         lengths, head_scale, tokens, vectors, weights, rows, ffn, block, head, factor, fused
@@ -1138,7 +1146,7 @@
 
         def w_spec(i):
             return pl.BlockSpec(
-                (rows, ffn, None) + four.shape[1:], lambda *_: (0, 0, i, 0, 0), pipeline_mode=pl.Buffered(1)
+                (rows, ffn // 2, 2, None) + four.shape[1:], lambda *_: (0, 0, 0, i, 0, 0), pipeline_mode=pl.Buffered(1)
             )
 
     else:
@@ -1155,7 +1163,7 @@
         block,
     )
     g_up, g_dn = ffn_weight_grads(lengths, h2, cotangent, m, du)
-    g_up, g_dn = (narrow(part, own_units).reshape((ffn, rows) + w_up.shape) for part in (g_up, g_dn))
+    g_up, g_dn = (narrow(part, own_units).reshape((ffn // 2, 2, rows) + w_up.shape) for part in (g_up, g_dn))
     scale_cols = rows_of(jnp.repeat(head_scale, head))
     dx2, dor, dq, dk, dv, g_hs, g_fg, g_fb, g_pg, g_pb, g_ob, *summed = back(
         lengths, dh2, cotangent, x2, o, c, attn, w_spec(3), rows_of(ffn_gain), rows_of(post_gain), scale_cols, q, k, v,
@@ -1176,7 +1184,7 @@
     if not fused:
         small = lax.psum(small, BOTH)
         attn_grads = [
-            scatter_sum(rows, ffn, part.reshape((rows, ffn) + w_query.shape), by_device) for part in attn_grads
+            scatter_sum(rows, ffn, part.reshape((rows, ffn // 2, 2) + w_query.shape), by_device) for part in attn_grads
         ]
     g_wo, g_wv, g_wk, g_wq = attn_grads
     n = hidden // width

time: 469 us -> 420 us (0.90); the launches traced: 468 us -> 412 us
  Pallas kernels: 446 us -> 390 us
    pallas_call x1, Pallas kernels: 119 us -> 100 us  [back(): pl.pallas_call(functools.partial(back_kernel, rows=rows, ffn=ffn, block=b...]
    pallas_call x1, Pallas kernels: 85.7 us -> 71.3 us  [last_stage(): pl.pallas_call(functools.partial(last_kernel, rows=rows, ffn=ffn, block=b...]
    pallas_call x1, Pallas kernels: 81.2 us -> 68.5 us  [feed_forward(): pl.pallas_call(ffn_kernel, grid=(seq // block,), in_specs=[smem, rows, ro...]
    pallas_call x1, Pallas kernels: 136 us -> 126 us  [front(): pl.pallas_call(functools.partial(front_kernel, rows=rows, ffn=ffn, block=...]
where the time goes in v4:
time: 420 us; the launch traced here: 412 us
  Pallas kernels  390 us (93%)
  local copies, waits for them, and re-layouts  18.7 us (4%)
    pallas_call x1, Pallas kernels, front(): pl.pallas_call(functools.partial(front_kernel, rows=rows, ffn=ffn, block=...  126 us
    pallas_call x1, Pallas kernels, back(): pl.pallas_call(functools.partial(back_kernel, rows=rows, ffn=ffn, block=b...  100 us
    pallas_call x1, Pallas kernels, last_stage(): pl.pallas_call(functools.partial(last_kernel, rows=rows, ffn=ffn, block=b...  71.3 us
    pallas_call x1, Pallas kernels, feed_forward(): pl.pallas_call(ffn_kernel, grid=(seq // block,), in_specs=[smem, rows, ro...  68.5 us
    pallas_call x1, Pallas kernels, ffn_weight_grads(): pl.pallas_call(ffn_weights_kernel, grid=(nb,), in_specs=[smem, whole((seq...  23.9 us
    unnamed x31, local copies, waits for them, and re-layouts  10 us

profile of v4, /device:TPU:0, one launch (start us, length us, event | category | flops | bytes accessed | tf_op | source)
XLA Modules:
  0.0 412.4 jit_solution(2301522731722495033)
XLA Ops:
  1.3 1.7 pad_maximum_fusion.refs_12_
  3.0 126.2 %forward_attention.1 = (bf16[1024,1024]{1,0:T(8,128)(2,1)}, bf16[1024,1024]{1,0:T(8,128)(2,1)}, bf16[1024,1024]{1,0:T(8,128)(2,1)}, bf16[1024,1024]{1,0:T(8,128)...) custom-call(s32[1]{0:T(128)S(6)} %copy.59.refs_0_.length_ref, ...), custom_call_target="tpu_custom_call" | custom-call | tf_op jit(solution)/shard_map/forward_attention/pallas_call | solution.py:587
  129.2 68.5 %feed_forward.1 = (f32[1024,1024]{1,0:T(8,128)}, f32[1024,1024]{1,0:T(8,128)}, bf16[8,1024,512]{2,1,0:T(8,128)(2,1)}, bf16[8,1024,512]{2,1,0:T(8,128)(2,1)}, f32...) custom-call(s32[1]{0:T(128)S(6)} %copy.59.refs_0_.length_ref, ...), custom_call_target="tpu_custom_call" | custom-call | flops 68719476736 | bytes 62914560 | tf_op jit(solution)/shard_map/feed_forward/pallas_call | solution.py:672
  197.8 23.9 %ffn_weight_grads.1 = (bf16[8,1024,512]{2,1,0:T(8,128)(2,1)}, bf16[8,1024,512]{2,1,0:T(8,128)(2,1)}) custom-call(s32[1]{0:T(128)S(6)} %copy.59.refs_0_.length_ref, bf16[1024,1024]{1,0:T(8,128)(2,1)} %get-tuple-element.63.h2_ref, bf16[1024,1024]{1,0:T(8,128)(2,1)} %refs_2_.3, bf16[8,1024,512]{2,1,0:T(8,128)(2,1)} %get-tuple-element.76.m_ref, ...), custom_call_target="tpu_custom_call" | custom-call | flops 17179869184 | bytes 37748736 | tf_op jit(solution)/shard_map/ffn_weight_grads/pallas_call | solution.py:713
  221.7 0.1 broadcast_in_dim.6
  221.8 0.7 reshape_reshape.3.refs_9_
  222.5 100.1 %backward_attention.1 = (f32[1024,1024]{1,0:T(8,128)}, bf16[1024,1024]{1,0:T(8,128)(2,1)}, bf16[1024,1024]{1,0:T(8,128)(2,1)}, bf16[1024,1024]{1,0:T(8,128)(2,1)...) custom-call(s32[1]{0:T(128)S(6)} %copy.59.refs_0_.length_ref, ...), custom_call_target="tpu_custom_call" | custom-call | tf_op jit(solution)/shard_map/backward_attention/pallas_call | solution.py:887
  322.5 0.8 slice_reduce_fusion
  323.6 1.6 concatenate.3
  325.2 0.7 pad.9.refs_12_
  325.9 71.3 %input_and_weights.1 = (f32[1024,1024]{1,0:T(8,128)}, f32[24,1024]{1,0:T(8,128)}, f32[32,1024]{1,0:T(8,128)}, f32[32,1024]{1,0:T(8,128)}, f32[32,1024]{1,0:T(8,128)}, /*index=5*/f32[32,1024]{1,0:T(8,128)}) custom-call(bf16[1024,1024]{1,0:T(8,128)(2,1)} %get-tuple-element.80.refs_0_, bf16[1024,1024]{1,0:T(8,128)(2,1)} %get-tuple-element.81.refs_1_, ...), custom_call_target="tpu_custom_call" | custom-call | tf_op jit(solution)/shard_map/input_and_weights/pallas_call | solution.py:1082
  397.1 0.9 slice_bitcast_fusion
  398.0 0.7 dynamic_slice.11
  398.7 0.7 dynamic_slice.10
  399.3 0.7 dynamic_slice.9
  400.0 1.7 fusion
  401.7 1.2 slice_bitcast_fusion.3
  402.9 4.9 %copy.60 = f32[1024,1024]{1,0:T(8,128)} copy(f32[1024,1024]{1,0:T(8,128)} %get-tuple-element.142) | data formatting | bytes 8388608
  407.8 0.7 copy.61
  408.4 0.7 copy.62
  409.1 0.7 copy.63
  409.8 0.7 copy.64
  410.4 0.8 copy.65
  411.2 0.8 copy.66
  (33 shorter events, 0.2 us)
Async XLA Ops:
  197.8 23.9 %copy-start.10 = (f32[16]{0:T(128)S(1)}, f32[16]{0:T(128)}, u32[]{:S(2)}) copy-start(f32[16]{0:T(128)} %refs_1_.1) | copy-start | bytes 196
  222.4 100.9 %copy-start.8 = (f32[8,1,512]{2,1,0:T(1,128)S(1)}, f32[8,1,512]{2,1,0:T(1,128)}, u32[]{:S(2)}) copy-start(f32[8,1,512]{2,1,0:T(1,128)} %get-tuple-element.93) | copy-start | bytes 49156
  222.4 101.0 %copy-start.7 = (f32[8,1,512]{2,1,0:T(1,128)S(1)}, f32[8,1,512]{2,1,0:T(1,128)}, u32[]{:S(2)}) copy-start(f32[8,1,512]{2,1,0:T(1,128)} %get-tuple-element.94) | copy-start | bytes 49156
  222.4 101.1 %copy-start.6 = (f32[8,1,512]{2,1,0:T(1,128)S(1)}, f32[8,1,512]{2,1,0:T(1,128)}, u32[]{:S(2)}) copy-start(f32[8,1,512]{2,1,0:T(1,128)} %get-tuple-element.95) | copy-start | bytes 49156
  222.4 101.2 %copy-start.9 = (f32[1,1024]{1,0:T(1,128)S(1)}, f32[1,1024]{1,0:T(1,128)}, u32[]{:S(2)}) copy-start(f32[1,1024]{1,0:T(1,128)} %get-tuple-element.91) | copy-start | bytes 12292
  402.8 4.9 %copy-start.5 = (f32[32,1024]{1,0:T(8,128)S(1)}, f32[32,1024]{1,0:T(8,128)}, u32[]{:S(2)}) copy-start(f32[32,1024]{1,0:T(8,128)} %get-tuple-element.145) | copy-start | bytes 393220
  402.8 5.6 %copy-start.4 = (f32[32,1024]{1,0:T(8,128)S(1)}, f32[32,1024]{1,0:T(8,128)}, u32[]{:S(2)}) copy-start(f32[32,1024]{1,0:T(8,128)} %get-tuple-element.147) | copy-start | bytes 393220
  402.9 6.3 %copy-start.3 = (f32[32,1024]{1,0:T(8,128)S(1)}, f32[32,1024]{1,0:T(8,128)}, u32[]{:S(2)}) copy-start(f32[32,1024]{1,0:T(8,128)} %get-tuple-element.148) | copy-start | bytes 393220
  402.9 6.9 %copy-start.2 = (f32[32,1024]{1,0:T(8,128)S(1)}, f32[32,1024]{1,0:T(8,128)}, u32[]{:S(2)}) copy-start(f32[32,1024]{1,0:T(8,128)} %get-tuple-element.151) | copy-start | bytes 393220
  402.9 7.6 %copy-start.1 = (f32[256,512]{1,0:T(8,128)S(1)}, f32[256,512]{1,0:T(8,128)}, u32[]{:S(2)}) copy-start(f32[256,512]{1,0:T(8,128)} %get-tuple-element.157) | copy-start | bytes 1572868
  402.9 8.3 %copy-start = (f32[256,512]{1,0:T(8,128)S(1)}, f32[256,512]{1,0:T(8,128)}, u32[]{:S(2)}) copy-start(f32[256,512]{1,0:T(8,128)} %get-tuple-element.161) | copy-start | bytes 1572868

commit v5 on v4

--- a/solution.py
+++ b/solution.py
@@ -96,11 +96,12 @@
     def device(self, r, z, c):
         return (r, 2 * z + c)
 
-    def enter(self):
+    def enter(self, near=True):
         barrier = pltpu.get_barrier_semaphore()
         partners = [self.device(self.r, self.z, 1 - self.c)]
-        partners += [self.device(self.row_flip(self.r, bit), self.z, self.c) for bit in range(2)]
-        partners += [self.device(self.r, self.z_at(d), self.c) for d in range(1, self.depth)]
+        if near:
+            partners += [self.device(self.row_flip(self.r, bit), self.z, self.c) for bit in range(2)]
+            partners += [self.device(self.r, self.z_at(d), self.c) for d in range(1, self.depth)]
         for partner in partners:
             pl.semaphore_signal(barrier, inc=1, device_id=partner, device_id_type=pl.DeviceIdType.MESH)
         pl.semaphore_wait(barrier, len(partners))
@@ -191,7 +192,7 @@
     return [dma((jobs,)), dma((jobs, 3)), dma((jobs, rows, depth)), dma((jobs,))]
 
 
-def gather_jobs(place, four, four_all, down, down_all, up, up_all, sems):
+def gather_jobs(place, shards, four_all, down_all, up_all, sems):
     local, send, recv, core = sems
     jobs = []
 
@@ -200,18 +201,18 @@
         jobs.append(Gather(place, src, many, many, (local.at[n], send.at[n], recv.at[n], core.at[n])))
 
     for i in range(4):
-        add(four.at[i], lambda r, z, c, i=i: four_all.at[r, z, c, i])
-    half = down.shape[0] // 2
-    for src, out in ((down, down_all), (up, up_all)):
+        add(shards[i], lambda r, z, c, i=i: four_all.at[r, z, c, i])
+    half = shards[4].shape[0] // 2
+    for src, out in ((shards[4], down_all), (shards[5], up_all)):
         for i in range(2):
             part = pl.ds(i * half, half)
             add(src.at[part], lambda r, z, c, out=out, part=part: out.at[z, c, r, part])
     return jobs
 
 
-def gather_kernel(four, down, up, four_all, down_all, up_all, *sems, rows, ffn):
+def gather_kernel(*refs, rows, ffn):
     place = Place(rows, ffn)
-    jobs = gather_jobs(place, four, four_all, down, down_all, up, up_all, sems)
+    jobs = gather_jobs(place, refs[:6], *refs[6:9], refs[9:])
     place.enter()
     for job in jobs:
         job.begin_z()
@@ -228,31 +229,26 @@
         job.finish()
 
 
-def gathered_shapes(rows, ffn, four, down, up):
+def gathered_shapes(rows, ffn, shards):
     depth = ffn // 2
-    return [sds((rows, depth, 2) + four.shape, BF16)] + [sds((depth, 2, rows) + a.shape, BF16) for a in (down, up)]
-
-
-def gather_all(rows, ffn, four, down, up):
+    return [sds((rows, depth, 2, 4) + shards[0].shape, BF16)] + [sds((depth, 2, rows) + a.shape, BF16) for a in shards[4:]]
+
+
+def gather_all(rows, ffn, shards):
     hbm = pl.BlockSpec(memory_space=pl.ANY)
     return pl.pallas_call(
         functools.partial(gather_kernel, rows=rows, ffn=ffn),
-        in_specs=[hbm] * 3,
+        in_specs=[hbm] * 6,
         out_specs=[hbm] * 3,
-        out_shape=gathered_shapes(rows, ffn, four, down, up),
+        out_shape=gathered_shapes(rows, ffn, shards),
         scratch_shapes=gather_sems(8, rows, ffn // 2),
         compiler_params=pltpu.CompilerParams(has_side_effects=True, collective_id=3),
         name="gather_all",
-    )(four, down, up)
+    )(*shards)
 
 
 ROWS_FIRST = 8
 STRIDE = 6
-BACK_FROM = 0
-BACK_STRIDE = 4
-LAST_ONE = 2
-LAST_TWO = 4
-LAST_ORDER = ("leave", "add_one", "add_two", "stay")
 
 
 def gather_rounds(jobs, depth, rows_first):
@@ -363,15 +359,127 @@
             pltpu.make_async_copy(ref, ref, self.send.at[kind]).wait()
 
 
-def scatter_rounds(jobs, depth):
-    order = list(range(1, depth)) + [0]
-    rounds = []
-    for t in range(jobs + 2):
-        rounds.append([(t, "leave", d) for d in order] if t < jobs else [])
-        rounds.append([(t - 1, "add_one", d) for d in order] if 0 <= t - 1 < jobs else [])
-        rounds.append([(t - 2, "add_two", d) for d in order] if 0 <= t - 2 < jobs else [])
-        rounds.append([(t, "stay", d) for d in order] if t < jobs else [])
-    return rounds
+class Exchange:
+    def __init__(self, place):
+        self.place = place
+        self.order = list(range(1, place.depth)) + [0]
+
+    def bits(self, d):
+        return (0, 1) if d % 2 == 0 else (1, 0)
+
+    def arrived(self, ref, arrival):
+        pltpu.make_async_copy(ref, ref, arrival).wait()
+
+    def rows_of_pair(self, d, leaving):
+        p = self.place
+        first, second = self.bits(d)
+        base = p.row_flip(p.r, first) if leaving else p.r
+        return base, p.row_flip(base, second)
+
+    def first_exchange(self, d, k, src):
+        p = self.place
+        partner = p.row_flip(p.r, self.bits(d)[0])
+        remote(
+            src, self.pair.at[d, k], self.send.at[1], self.recv.at[k, d], p.device(partner, p.z, p.c)
+        ).start()
+
+    def one(self):
+        p = self.place
+        for d in self.order:
+            partner = p.row_flip(p.r, self.bits(d)[1])
+            for k in (1, 0):
+                self.arrived(self.pair.at[d, k], self.recv.at[k, d])
+                here = self.kept(d, k)
+                here[...] = here[...] + self.other(d, k)[...]
+                if k == 1:
+                    remote(
+                        here, self.last.at[d], self.send.at[2], self.recv.at[2, d], p.device(partner, p.z, p.c)
+                    ).start()
+
+    def two(self):
+        p = self.place
+        for d in self.order:
+            self.arrived(self.last.at[d], self.recv.at[2, d])
+            here = self.kept(d, 0)
+            here[...] = here[...] + self.last[d]
+            if d > 0:
+                remote(
+                    here, self.far.at[d], self.send.at[3], self.recv.at[3, d], p.device(p.r, p.z_at(d), p.c)
+                ).start()
+
+    def total(self):
+        out = self.kept(0, 0)[...].astype(F32)
+        for d in range(1, self.place.depth):
+            self.arrived(self.far.at[d], self.recv.at[3, d])
+            out = out + self.far[d].astype(F32)
+        for kind, ref in ((1, self.pair), (2, self.last), (3, self.far.at[pl.ds(1, self.place.depth - 1)])):
+            self.arrived(ref, self.send.at[kind])
+        return out
+
+
+class PairExchange(Exchange):
+    def __init__(self, place, view, stage, load, pair, last, far, send, recv):
+        super().__init__(place)
+        self.view, self.stage, self.load = view, stage, load
+        self.pair, self.last, self.far, self.send, self.recv = pair, last, far, send, recv
+
+    def kept(self, d, k):
+        return self.pair.at[d, k]
+
+    def other(self, d, k):
+        self.fetch(d, k).wait()
+        return self.stage.at[d, k]
+
+    def fetch(self, d, k):
+        r = self.rows_of_pair(d, False)[k]
+        return pltpu.make_async_copy(self.view(r, self.place.z_at(d)), self.stage.at[d, k], self.load.at[d, k])
+
+    def leave(self):
+        for d in self.order:
+            z = self.place.z_at(d)
+            for k, r in enumerate(self.rows_of_pair(d, True)):
+                self.first_exchange(d, k, self.view(r, z))
+            for k in range(2):
+                self.fetch(d, k).start()
+
+
+class CoreExchange(Exchange):
+    def __init__(self, place, view, whole, half, pair, last, far, send, recv):
+        super().__init__(place)
+        self.view, self.whole, self.half = view, whole, half
+        self.pair, self.last, self.far, self.send, self.recv = pair, last, far, send, recv
+
+    def kept(self, d, k):
+        return self.half.at[d, self.rows_of_pair(d, False)[k]]
+
+    def other(self, d, k):
+        return self.pair.at[d, k]
+
+    def begin(self):
+        p = self.place
+        for d in self.order:
+            for leaving in (True, False):
+                for r in self.rows_of_pair(d, leaving):
+                    remote(
+                        self.view(r, p.z_at(d), 1 - p.c), self.half.at[d, r], self.send.at[0], self.recv.at[4 + r, d],
+                        p.device(p.r, p.z, 1 - p.c),
+                    ).start()
+
+    def add_core(self, d, r):
+        p = self.place
+        here = self.half.at[d, r]
+        self.arrived(here, self.recv.at[4 + r, d])
+        here[...] = here[...] + self.view(r, p.z_at(d), p.c)[...]
+
+    def leave(self):
+        for d in self.order:
+            for k, r in enumerate(self.rows_of_pair(d, True)):
+                self.add_core(d, r)
+                self.first_exchange(d, k, self.half.at[d, r])
+        for d in self.order:
+            for r in self.rows_of_pair(d, False):
+                self.add_core(d, r)
+        self.arrived(self.half, self.send.at[0])
 
 
 def scatter_kernel(src, out, own, half, pair, last, far, load, send, recv, *, rows, ffn, view):
@@ -449,11 +557,10 @@
 
 
 def front_kernel(*refs, rows, ffn, block, head, factor, fused):
-    n_in = 14 if fused else 12
     (length_ref, scale_ref, x_ref, lg_ref, lb_ref, qb_ref, vb_ref, ob_ref, pg_ref, pb_ref, fg_ref) = refs[:11]
     fb_ref = refs[11]
-    comm_in = refs[12 : 15 if fused else 13]
-    refs = refs[15 if fused else 13 :]
+    comm_in = refs[12 : 18 if fused else 13]
+    refs = refs[18 if fused else 13 :]
     h_ref, q_ref, k_ref, v_ref, c_ref, lse_ref, o_ref, x2_ref, h2_ref = refs[:9]
     comm_out = refs[9:12] if fused else ()
     refs = refs[12 if fused else 9 :]
@@ -474,9 +581,7 @@
     late = {}
     if fused:
         place = Place(rows, ffn)
-        jobs = gather_jobs(
-            place, comm_in[0], comm_out[0], comm_in[1], comm_out[1], comm_in[2], comm_out[2], refs[6:10]
-        )
+        jobs = gather_jobs(place, comm_in, *comm_out, refs[6:10])
         rounds = gather_rounds(len(jobs), place.depth, ROWS_FIRST)
         cut = 1 + 3 * 6
         opening = sum(rounds[:cut], [])
@@ -521,8 +626,7 @@
         q = ((dot_nn(h, weight(0)) + qb_ref[...]).astype(BF16).astype(F32) * factor).astype(BF16)
         k = dot_nn(h, weight(1)).astype(BF16)
         v = (dot_nn(h, weight(2)) + vb_ref[...]).astype(BF16)
-        for ref, scratch, value in ((q_ref, q_s, q), (k_ref, k_s, k), (v_ref, v_s, v)):
-            ref[...] = value
+        for scratch, value in ((q_s, q), (k_s, k), (v_s, v)):
             scratch[here, :] = value
 
     @pl.when((step >= nb) & (step < nb + pairs))
@@ -535,6 +639,8 @@
             for n in range(2):
                 lse_ref[0, n : n + 1, i * block : (i + 1) * block] = logs[n * head : n * head + 1, :]
 
+        for ref, scratch in ((q_ref, q_s), (k_ref, k_s), (v_ref, v_s)):
+            ref[...] = scratch[:, cols]
         attend_pair(
             length_ref[0], [scale_ref[2 * pair + n] for n in range(2)],
             lambda i: q_s[i * block : (i + 1) * block, cols], k_s[:, cols], v_s[:, cols], seq, block, head, store,
@@ -572,15 +678,16 @@
     final = pl.BlockSpec((block, width), lambda i: (clip(i, nb + pairs, nb), 0))
     smem = pl.BlockSpec(memory_space=pltpu.SMEM)
     hbm = pl.BlockSpec(memory_space=pl.ANY)
-    out_specs = [first] * 4 + [final, pl.BlockSpec((1, 2, seq), lambda i: (clip(i, nb, pairs), 0, 0))] + [final] * 3
-    out_shape = [sds((seq, width), BF16)] * 5 + [sds((pairs, 2, seq), F32)] + [sds((seq, width), F32)] * 2
+    out_specs = [first] + [pl.BlockSpec((None, seq, 2 * head), lambda i: (clip(i, nb, pairs), 0, 0))] * 3
+    out_specs += [final, pl.BlockSpec((1, 2, seq), lambda i: (clip(i, nb, pairs), 0, 0))] + [final] * 3
+    out_shape = [sds((seq, width), BF16)] + [sds((pairs, seq, 2 * head), BF16)] * 3 + [sds((seq, width), BF16)]
+    out_shape += [sds((pairs, 2, seq), F32)] + [sds((seq, width), F32)] * 2
     out_shape += [sds((seq, width), BF16)]
     scratch = [pltpu.VMEM((seq, width), BF16)] * 4 + [pltpu.SemaphoreType.DMA((4,))]
     if fused:
-        four, down, up = weights
-        out_shape += gathered_shapes(rows, ffn, four, down, up)
+        out_shape += gathered_shapes(rows, ffn, weights)
         out_specs += [hbm] * 3
-        scratch = [pltpu.VMEM((4, rows, ffn // 2, 2) + four.shape[1:], BF16)] + scratch
+        scratch = [pltpu.VMEM((4, rows, ffn // 2, 2) + weights[0].shape, BF16)] + scratch
         scratch += gather_sems(8, rows, ffn // 2)
     else:
         scratch = [pltpu.VMEM((4, width, width), BF16)] + scratch
@@ -597,13 +704,25 @@
 
 
 def ffn_kernel(
-    length_ref, h2_ref, ct_ref, x2_ref, wup_ref, wdn_ref, ub_ref, mg_ref, mb_ref, db_ref,
+    length_ref, h2_ref, ct_ref, x2_ref, up_ref, dn_ref, ub_ref, mg_ref, mb_ref, db_ref,
     res_ref, dh2_ref, m_ref, du_ref, gub_ref, gmg_ref, gmb_ref, gdb_ref,
-    e_s, gp_s, dm_s,
+    e_s, gp_s, dm_s, wup_ref, wdn_ref, load,
 ):
     step = pl.program_id(0)
     block, width = h2_ref.shape
     nb, _, hb = wup_ref.shape
+
+    def loads(j):
+        return [
+            pltpu.make_async_copy(src.at[j], dst.at[j], load.at[n, j])
+            for n, (src, dst) in enumerate(((up_ref, wup_ref), (dn_ref, wdn_ref)))
+        ]
+
+    @pl.when(step == 0)
+    def _():
+        for j in range(nb):
+            for copy in loads(j):
+                copy.start()
     units = nb * hb
     row = lax.broadcasted_iota(jnp.int32, (block, width), 0) + step * block
     valid = row < length_ref[0]
@@ -619,7 +738,10 @@
 
     gdb_ref[...] += col_sum(dfr.astype(F32))
 
-    def first(j, sums):
+    def first(j, sums, wait):
+        if wait:
+            for copy in loads(j):
+                copy.wait()
         u = dot_nn(h2, wup_ref[j]) + ub_ref[j]
         dm = dot_nn(dfr, wdn_ref[j])
         cdf = 0.5 * (1.0 + lax.erf(u * math.sqrt(0.5)))
@@ -632,33 +754,47 @@
         terms = (e, e * e, dmh, dmh * e)
         return tuple(s + jnp.sum(t, axis=-1, keepdims=True) for s, t in zip(sums, terms))
 
-    zero = jnp.zeros((block, 1), F32)
-    sum_e, sum_ee, sum_d, sum_de = lax.fori_loop(0, nb, first, (zero,) * 4, unroll=2)
-    mu = sum_e / units
-    inverse = lax.rsqrt(sum_ee / units - mu * mu + epsilon)
-    mean_d = sum_d / units
-    mean_dh = (sum_de - mu * sum_d) * inverse / units
-
-    def second(j, sums):
+    def rows(wait):
+        zero = jnp.zeros((block, 1), F32)
+        sums = (zero,) * 4
+        for j in range(nb):
+            sums = first(j, sums, wait)
+        sum_e, sum_ee, sum_d, sum_de = sums
+        mu = sum_e / units
+        inverse = lax.rsqrt(sum_ee / units - mu * mu + epsilon)
+        mean_d = sum_d / units
+        mean_dh = (sum_de - mu * sum_d) * inverse / units
+
+        def second(j, sums):
+            f, dh2 = sums
+            ehat = (e_s[j] - mu) * inverse
+            dm = dm_s[j]
+            m = (ehat * mg_ref[j] + mb_ref[j]).astype(BF16)
+            m_ref[j] = m
+            f = f + dot_nt(m, wdn_ref[j])
+            de = (dm * mg_ref[j] - mean_d - ehat * mean_dh) * inverse
+            du = (de * gp_s[j]).astype(BF16)
+            du_ref[j] = du
+            dh2 = dh2 + dot_nt(du, wup_ref[j])
+            gub_ref[j] += col_sum(du.astype(F32))
+            gmg_ref[j] += col_sum(dm * ehat)
+            gmb_ref[j] += col_sum(dm)
+            return f, dh2
+
+        sums = (jnp.zeros((block, width), F32),) * 2
+        for j in range(nb):
+            sums = second(j, sums)
         f, dh2 = sums
-        ehat = (e_s[j] - mu) * inverse
-        dm = dm_s[j]
-        m = (ehat * mg_ref[j] + mb_ref[j]).astype(BF16)
-        m_ref[j] = m
-        f = f + dot_nt(m, wdn_ref[j])
-        de = (dm * mg_ref[j] - mean_d - ehat * mean_dh) * inverse
-        du = (de * gp_s[j]).astype(BF16)
-        du_ref[j] = du
-        dh2 = dh2 + dot_nt(du, wup_ref[j])
-        gub_ref[j] += col_sum(du.astype(F32))
-        gmg_ref[j] += col_sum(dm * ehat)
-        gmb_ref[j] += col_sum(dm)
-        return f, dh2
-
-    zeros = jnp.zeros((block, width), F32)
-    f, dh2 = lax.fori_loop(0, nb, second, (zeros, zeros), unroll=2)
-    res_ref[...] = jnp.where(valid, x2_ref[...] + f + db_ref[...], 0.0)
-    dh2_ref[...] = dh2
+        res_ref[...] = jnp.where(valid, x2_ref[...] + f + db_ref[...], 0.0)
+        dh2_ref[...] = dh2
+
+    @pl.when(step == 0)
+    def _():
+        rows(True)
+
+    @pl.when(step > 0)
+    def _():
+        rows(False)
 
 
 def feed_forward(length, h2, ct, x2, wup, wdn, ub, mg, mb, db, block):
@@ -666,6 +802,7 @@
     nb, _, hb = wup.shape
     rows = pl.BlockSpec((block, width), lambda i: (i, 0))
     smem = pl.BlockSpec(memory_space=pltpu.SMEM)
+    hbm = pl.BlockSpec(memory_space=pl.ANY)
     units = whole((nb, 1, hb))
     blocks = pl.BlockSpec((nb, block, hb), lambda i: (0, i, 0))
     sums = out_whole((nb, 1, hb))
@@ -673,7 +810,7 @@
         ffn_kernel,
         grid=(seq // block,),
         in_specs=[
-            smem, rows, rows, rows, whole((nb, width, hb)), whole((nb, width, hb)),
+            smem, rows, rows, rows, hbm, hbm,
             units, units, units, whole((1, width)),
         ],
         out_specs=[rows, rows, blocks, blocks, sums, sums, sums, out_whole((1, width))],
@@ -681,7 +818,8 @@
             sds((seq, width), F32), sds((seq, width), F32), sds((nb, seq, hb), BF16), sds((nb, seq, hb), BF16),
             sds((nb, 1, hb), F32), sds((nb, 1, hb), F32), sds((nb, 1, hb), F32), sds((1, width), F32),
         ],
-        scratch_shapes=[pltpu.VMEM((nb, block, hb), F32)] * 3,
+        scratch_shapes=[pltpu.VMEM((nb, block, hb), F32)] * 3 + [pltpu.VMEM((nb, width, hb), BF16)] * 2
+        + [pltpu.SemaphoreType.DMA((2, nb))],
         compiler_params=params(60 * MIB),
         cost_estimate=pl.CostEstimate(
             flops=16 * seq * width * nb * hb, bytes_accessed=60 * MIB, transcendentals=2 * seq * nb * hb
@@ -702,6 +840,68 @@
 
     gdn_ref[0] = dot_nn(dft_s[...], m_ref[0]).astype(BF16)
     gup_ref[0] = dot_nn(h2t_s[...], du_ref[0]).astype(BF16)
+
+
+def ffn_weights_pair_kernel(
+    length_ref, h2_ref, ct_ref, m_ref, du_ref, gdn_ref, gup_ref, h2t_s, dft_s, grads_s, half_s, send, recv, *, rows, ffn,
+):
+    step = pl.program_id(0)
+    place = Place(rows, ffn)
+    seq, width = h2_ref.shape
+    depth = place.depth
+
+    def give(a, z):
+        return remote(
+            grads_s.at[a, z, 1 - place.c], half_s.at[a, z], send.at[a, z], recv.at[a, z],
+            place.device(place.r, place.z, 1 - place.c),
+        )
+
+    @pl.when(step == 0)
+    def _():
+        place.enter(near=False)
+        row = lax.broadcasted_iota(jnp.int32, (seq, width), 0)
+        dfr = jnp.where(row < length_ref[0], ct_ref[...], 0)
+        h2t_s[...] = h2_ref[...].T
+        dft_s[...] = dfr.T
+
+    @pl.when(step < depth)
+    def _():
+        for c in range(2):
+            grads_s[0, step, c] = dot_nn(dft_s[...], m_ref[c]).astype(BF16)
+            grads_s[1, step, c] = dot_nn(h2t_s[...], du_ref[c]).astype(BF16)
+        for a in range(2):
+            give(a, step).start()
+
+    @pl.when(step > 0)
+    def _():
+        z = step - 1
+        for a, out in enumerate((gdn_ref, gup_ref)):
+            give(a, z).wait()
+            out[0] = grads_s[a, z, place.c] + half_s[a, z]
+
+
+def ffn_weight_pair_sums(length, h2, ct, m, du, rows, ffn):
+    seq, width = h2.shape
+    nb, _, hb = m.shape
+    depth = nb // 2
+    smem = pl.BlockSpec(memory_space=pltpu.SMEM)
+    block = pl.BlockSpec((2, seq, hb), lambda j: (clip(j, 0, depth), 0, 0))
+    out = pl.BlockSpec((1, width, hb), lambda j: (clip(j, 1, depth), 0, 0))
+    return pl.pallas_call(
+        functools.partial(ffn_weights_pair_kernel, rows=rows, ffn=ffn),
+        grid=(depth + 1,),
+        in_specs=[smem, whole((seq, width)), whole((seq, width)), block, block],
+        out_specs=[out, out],
+        out_shape=[sds((depth, width, hb), BF16)] * 2,
+        scratch_shapes=[pltpu.VMEM((width, seq), BF16)] * 2 + [
+            pltpu.VMEM((2, depth, 2, width, hb), BF16),
+            pltpu.VMEM((2, depth, width, hb), BF16),
+            pltpu.SemaphoreType.DMA((2, depth)),
+            pltpu.SemaphoreType.DMA((2, depth)),
+        ],
+        compiler_params=params(60 * MIB, **comm_params(True, 1)),
+        name="ffn_weight_pair_sums",
+    )(length, h2, ct, m, du)
 
 
 def ffn_weight_grads(length, h2, ct, m, du):
@@ -757,79 +957,65 @@
         store(j, dk.astype(BF16), dv.astype(BF16))
 
 
-def back_kernel(*refs, rows, ffn, block, head, factor, fused):
-    (
-        length_ref, dh2_ref, ct_ref, x2_ref, o_ref, c_ref, w_ref, fg_ref, pg_ref, hs_ref, q_ref, k_ref, v_ref, lse_ref,
-    ) = refs[:14]
-    comm_in = refs[14:16] if fused else ()
-    refs = refs[16 if fused else 14 :]
-    (
-        dx2_ref, dor_ref, dq_ref, dk_ref, dv_ref, ghs_ref, gfg_ref, gfb_ref, gpg_ref, gpb_ref, gob_ref,
-    ) = refs[:11]
-    comm_out = refs[11:13] if fused else ()
-    refs = refs[13 if fused else 11 :]
-    g_s, inner_s, dq_s = refs[:3]
+def norms_back(dh2, x2, o, c, dy, w, fg, pg, hs, head, sums, g_store, dx2_store, dor_store):
+    block, width = dh2.shape
+    heads = width // head
+    hat2, inverse2 = norm_parts(x2)
+    dx2 = dy + norm_back(dh2 * fg, hat2, inverse2)
+    dx2_store(dx2)
+    hat, inverse = norm_parts(o)
+    dor = norm_back(dx2 * pg, hat, inverse).astype(BF16)
+    dor_store(dor)
+    sums(
+        col_sum(dor.astype(F32)), col_sum(dx2 * hat), col_sum(dx2), col_sum(dh2 * hat2), col_sum(dh2),
+    )
+    dc = dot_nt(dor, w)
+    g_store((dc * hs).astype(BF16))
+    product = dc * c.astype(F32)
+    high = product.astype(BF16)
+    low = (product - high.astype(F32)).astype(BF16)
+    owner = lax.broadcasted_iota(jnp.int32, (heads, width), 1) // head
+    pick = (owner == lax.broadcasted_iota(jnp.int32, (heads, width), 0)).astype(BF16)
+    return dot_nt(pick, high) + dot_nt(pick, low)
+
+
+def valid_grad(ct, length, first):
+    row = lax.broadcasted_iota(jnp.int32, ct.shape, 0) + first
+    return jnp.where(row < length, ct.astype(F32), 0.0)
+
+
+def back_kernel(
+    length_ref, dh2_ref, ct_ref, x2_ref, o_ref, c_ref, w_ref, fg_ref, pg_ref, hs_ref, q_ref, k_ref, v_ref, lse_ref,
+    dx2_ref, dor_ref, dq_ref, dk_ref, dv_ref, ghs_ref, sums_ref, g_s, inner_s, dq_s, *, block, head, factor,
+):
     step = pl.program_id(0)
     seq, width = g_s.shape
     nb = seq // block
-    pairs = width // (2 * head)
-    heads = width // head
-    last = nb + pairs - 1
-
-    if fused:
-        place = Place(rows, ffn)
-        depth = place.depth
-        jobs = []
-        half = comm_out[0].shape[0] // 2
-        for n in range(4):
-            bufs = refs[3 + 8 * n : 11 + 8 * n]
-            part = pl.ds(n % 2 * half, half)
-            jobs.append(Scatter(place, by_unit(comm_in[n // 2], part), *bufs[:5], bufs[5:]))
-        rounds = scatter_rounds(4, depth)
-        table = {}
-        for k, keys in enumerate(rounds):
-            table.setdefault(min(max(0, k - BACK_FROM) * BACK_STRIDE // 8, last), []).extend(keys)
-
-        def actions(keys):
-            return [functools.partial(getattr(jobs[n], name), d) for n, name, d in keys]
-
-        order = list(range(1, depth)) + [0]
-        begin = [functools.partial(job.begin, d) for job in jobs for d in order]
-        plan = {i: actions(keys) for i, keys in table.items() if i < last}
-        plan[0] = [place.enter] + begin + plan[0]
-        at_steps(step, {i: todo for i, todo in plan.items() if todo})
+
+    @pl.when(step == 0)
+    def _():
+        ghs_ref[...] = jnp.zeros_like(ghs_ref)
+        sums_ref[...] = jnp.zeros_like(sums_ref)
 
     @pl.when(step < nb)
     def _():
-        row = lax.broadcasted_iota(jnp.int32, (block, width), 0) + step * block
-        dy = jnp.where(row < length_ref[0], ct_ref[...].astype(F32), 0.0)
-
-        @pl.when(step == 0)
-        def _():
-            for ref in (gfg_ref, gfb_ref, gpg_ref, gpb_ref, gob_ref, ghs_ref):
-                ref[...] = jnp.zeros_like(ref)
-
-        dh2 = dh2_ref[...]
-        hat2, inverse2 = norm_parts(x2_ref[...])
-        gfg_ref[...] += col_sum(dh2 * hat2)
-        gfb_ref[...] += col_sum(dh2)
-        dx2 = dy + norm_back(dh2 * fg_ref[...], hat2, inverse2)
-        dx2_ref[...] = dx2
-        hat, inverse = norm_parts(o_ref[...])
-        gpg_ref[...] += col_sum(dx2 * hat)
-        gpb_ref[...] += col_sum(dx2)
-        dor = norm_back(dx2 * pg_ref[...], hat, inverse).astype(BF16)
-        dor_ref[...] = dor
-        gob_ref[...] += col_sum(dor.astype(F32))
-        dc = dot_nt(dor, w_ref[...].reshape(width, width))
         here = pl.ds(pl.multiple_of(step * block, block), block)
-        g_s[here, :] = (dc * hs_ref[...]).astype(BF16)
-        product = dc * c_ref[...].astype(F32)
-        high = product.astype(BF16)
-        low = (product - high.astype(F32)).astype(BF16)
-        owner = lax.broadcasted_iota(jnp.int32, (heads, width), 1) // head
-        pick = (owner == lax.broadcasted_iota(jnp.int32, (heads, width), 0)).astype(BF16)
-        inner = dot_nt(pick, high) + dot_nt(pick, low)
+
+        def sums(*parts):
+            for n, part in enumerate(parts):
+                sums_ref[n : n + 1, :] += part
+
+        def put(ref, *index):
+            def store(value):
+                ref[index if index else ...] = value
+
+            return store
+
+        inner = norms_back(
+            dh2_ref[...], x2_ref[...], o_ref[...], c_ref[...], valid_grad(ct_ref[...], length_ref[0], step * block),
+            w_ref[...], fg_ref[...], pg_ref[...], hs_ref[...], head, sums, put(g_s, here, slice(None)), put(dx2_ref),
+            put(dor_ref),
+        )
         inner_s[step] = inner
         ghs_ref[...] += jnp.broadcast_to(jnp.sum(inner, axis=-1, keepdims=True), ghs_ref.shape)
 
@@ -852,49 +1038,87 @@
         )
         dq_ref[...] = (dq_s[...] * factor).astype(BF16)
 
-    if fused:
-
-        @pl.when(step == last)
-        def _():
-            for action in actions(table.get(last, [])):
-                action()
-            for n, job in enumerate(jobs):
-                comm_out[n // 2][n % 2 * half : (n % 2 + 1) * half, :] = job.total()
-                job.finish()
-
-
-def back(length, dh2, ct, x2, o, c, w, w_spec, fg, pg, hs, q, k, v, lse, grads, rows, ffn, block, head, factor, fused):
+
+def back(length, dh2, ct, x2, o, c, w, fg, pg, hs, q, k, v, lse, block, head, factor):
     seq, width = dh2.shape
     nb, pairs, heads = seq // block, width // (2 * head), width // head
     part = pl.BlockSpec((block, width), lambda i: (clip(i, 0, nb), 0))
     cols = pl.BlockSpec((seq, 2 * head), lambda i: (0, clip(i, nb, pairs)))
+    heads_in = pl.BlockSpec((None, seq, 2 * head), lambda i: (clip(i, nb, pairs), 0, 0))
     smem = pl.BlockSpec(memory_space=pltpu.SMEM)
-    hbm = pl.BlockSpec(memory_space=pl.ANY)
-    vec, ovec = whole((1, width)), out_whole((1, width))
-    out_specs = [part] * 2 + [cols] * 3 + [out_whole((heads, 128))] + [ovec] * 5
-    out_shape = [sds((seq, width), F32), sds((seq, width), BF16)] + [sds((seq, width), BF16)] * 3
-    out_shape += [sds((heads, 128), F32)] + [sds((1, width), F32)] * 5
-    scratch = [
-        pltpu.VMEM((seq, width), BF16), pltpu.VMEM((nb, heads, block), F32), pltpu.VMEM((seq, 2 * head), F32),
-    ]
-    if fused:
-        piece = grads[0].shape[3:]
-        out_specs += [pl.BlockSpec(memory_space=pltpu.VMEM)] * 2
-        out_shape += [sds(piece, F32)] * 2
-        scratch += scatter_scratch((piece[0] // 2, piece[1]), rows, ffn // 2, True) * 4
-    else:
-        grads = ()
+    vec = whole((1, width))
     return pl.pallas_call(
-        functools.partial(back_kernel, rows=rows, ffn=ffn, block=block, head=head, factor=factor, fused=fused),
+        functools.partial(back_kernel, block=block, head=head, factor=factor),
         grid=(nb + pairs,),
-        in_specs=[smem] + [part] * 5 + [w_spec] + [vec] * 3 + [cols] * 3
-        + [pl.BlockSpec((1, 2, seq), lambda i: (clip(i, nb, pairs), 0, 0))] + [hbm] * len(grads),
-        out_specs=out_specs,
-        out_shape=out_shape,
-        scratch_shapes=scratch,
-        compiler_params=params(60 * MIB, **comm_params(fused, 1)),
+        in_specs=[smem] + [part] * 5 + [whole((width, width))] + [vec] * 3 + [heads_in] * 3
+        + [pl.BlockSpec((1, 2, seq), lambda i: (clip(i, nb, pairs), 0, 0))],
+        out_specs=[part] * 2 + [cols] * 3 + [out_whole((heads, 128)), out_whole((8, width))],
+        out_shape=[sds((seq, width), F32)] + [sds((seq, width), BF16)] * 4
+        + [sds((heads, 128), F32), sds((8, width), F32)],
+        scratch_shapes=[
+            pltpu.VMEM((seq, width), BF16), pltpu.VMEM((nb, heads, block), F32), pltpu.VMEM((seq, 2 * head), F32),
+        ],
+        compiler_params=params(60 * MIB),
         name="backward_attention",
-    )(length, dh2, ct, x2, o, c, w, fg, pg, hs, q, k, v, lse, *grads)
+    )(length, dh2, ct, x2, o, c, w, fg, pg, hs, q, k, v, lse)
+
+
+def weights_kernel(left_ref, right_ref, out_ref, left_s):
+    @pl.when(pl.program_id(0) == 0)
+    def _():
+        left_s[...] = left_ref[...].T
+
+    out_ref[...] = dot_nn(left_s[...], right_ref[...]).astype(BF16)
+
+
+def weight_grad(left, right, block):
+    seq, width = left.shape
+    cols = right.shape[1]
+    return pl.pallas_call(
+        weights_kernel,
+        grid=(cols // block,),
+        in_specs=[whole((seq, width)), pl.BlockSpec((seq, block), lambda j: (0, j))],
+        out_specs=pl.BlockSpec((width, block), lambda j: (0, j)),
+        out_shape=sds((width, cols), BF16),
+        scratch_shapes=[pltpu.VMEM((width, seq), BF16)],
+        compiler_params=params(),
+        name="weight_grad",
+    )(left, right)
+
+
+def input_back(dq, dk, dv, w, x, dx2, gain, sums):
+    dh = dot_nt(dq, w(0)) + dot_nt(dk, w(1)) + dot_nt(dv, w(2))
+    hat, inverse = norm_parts(x.astype(F32))
+    sums(col_sum(dh * hat), col_sum(dh), col_sum(dq.astype(F32)), col_sum(dv.astype(F32)))
+    return dx2 + norm_back(dh * gain, hat, inverse)
+
+
+def input_kernel(dq_ref, dk_ref, dv_ref, w_ref, x_ref, dx2_ref, gain_ref, dx_ref, sums_ref):
+    @pl.when(pl.program_id(0) == 0)
+    def _():
+        sums_ref[...] = jnp.zeros_like(sums_ref)
+
+    def sums(*parts):
+        for n, part in enumerate(parts):
+            sums_ref[n : n + 1, :] += part
+
+    dx_ref[...] = input_back(
+        dq_ref[...], dk_ref[...], dv_ref[...], lambda i: w_ref[i], x_ref[...], dx2_ref[...], gain_ref[...], sums
+    )
+
+
+def input_grad(dq, dk, dv, w, x, dx2, gain, block):
+    seq, width = dq.shape
+    rows = pl.BlockSpec((block, width), lambda i: (i, 0))
+    return pl.pallas_call(
+        input_kernel,
+        grid=(seq // block,),
+        in_specs=[rows, rows, rows, whole((3, width, width)), rows, rows, whole((1, width))],
+        out_specs=[rows, out_whole((8, width))],
+        out_shape=[sds((seq, width), F32), sds((8, width), F32)],
+        compiler_params=params(),
+        name="input_grad",
+    )(dq, dk, dv, w, x, dx2, gain)
 
 
 class AllSum:
@@ -945,150 +1169,232 @@
             self.along(d).wait_send()
 
 
-def last_kernel(*refs, rows, ffn, block, fused):
-    (
-        dq_ref, dk_ref, dv_ref, dor_ref, h_ref, c_ref, wq_ref, wk_ref, wv_ref, x_ref, dx2_ref, gain_ref, small_ref,
-    ) = refs[:13]
-    refs = refs[13:]
-    dx_ref, small_out = refs[:2]
-    refs = refs[2:]
-    grad_refs = refs[:4]
-    refs = refs[4:]
-    if fused:
-        grads = refs[:4]
-        left_s, sums_s = refs[4:6]
-        refs = refs[6:]
-    else:
-        grads = grad_refs
-        left_s, sums_s = refs[:2]
+def tail_kernel(
+    length_ref, dh2_ref, ct_ref, x2_ref, o_ref, c_ref, x_ref, fg_ref, pg_ref, hs_ref, gain_ref, small_ref,
+    q_ref, k_ref, v_ref, lse_ref, h_ref, w_ref, down_ref, up_ref,
+    dx_ref, small_out, down_out, up_out, wo_out, wv_out, wk_out, wq_out,
+    w_s, g_s, dq_s, dk_s, dv_s, left_s, dx2_s, inner_s, dqa_s, acc_s, ghs_s, load,
+    stage, stage_load, grads, *bufs, rows, ffn, block, head, factor,
+):
     step = pl.program_id(0)
-    seq, width = dq_ref.shape
+    seq, width = g_s.shape
     nb = seq // block
-    last = 4 + nb - 1
-
-    if fused:
-        place = Place(rows, ffn)
-        depth = place.depth
-        jobs = []
-        for n in range(4):
-            bufs = refs[7 * n : 7 * n + 7]
-            jobs.append(Scatter(place, by_device(grads[n]), None, *bufs[:4], bufs[4:]))
-        small = AllSum(place, *refs[28:32])
-        table = {}
-        for n in range(4):
-            for k, (name, when) in enumerate((("leave", 1), ("stay", 1), ("add_one", 1 + LAST_ONE), ("add_two", 1 + LAST_TWO))):
-                table.setdefault(min(n + when, last + 1), []).extend((n, name, d) for d in list(range(1, depth)) + [0])
-
-        def actions(keys):
-            return [functools.partial(getattr(jobs[n], name), d) for n, name, d in keys]
-
-        order = list(range(1, depth)) + [0]
-        plan = {i: actions(sorted(keys, key=lambda key: LAST_ORDER.index(key[1]))) for i, keys in table.items() if i <= last}
-        rest = table.get(last + 1, [])
-        plan[0] = []
-        plan[0] = [place.enter] + plan[0]
-        at_steps(step, {i: todo for i, todo in plan.items() if todo})
-
-    for n, right in enumerate((dor_ref, dv_ref, dk_ref, dq_ref)):
-
-        @pl.when(step == n)
-        def _(n=n, right=right):
-            if n == 0:
-                left_s[...] = c_ref[...].T
-            if n == 1:
-                left_s[...] = h_ref[...].T
-            half = width // 2
-            for part in range(2):
-                cols = slice(part * half, (part + 1) * half)
-                value = dot_nn(left_s[...], right[:, cols]).astype(BF16)
-                if fused:
-                    grads[n][..., cols] = value.reshape(grads[n].shape[:-1] + (half,))
-                else:
-                    grads[n][:, cols] = value
-            if fused:
-                for d in order:
-                    jobs[n].begin(d)
-
-    @pl.when(step >= 4)
-    def _():
-        here = pl.ds(pl.multiple_of((step - 4) * block, block), block)
-        dq, dk, dv = dq_ref[here, :], dk_ref[here, :], dv_ref[here, :]
-
-        @pl.when(step == 4)
-        def _():
-            sums_s[...] = jnp.zeros_like(sums_s)
-
-        dh = (
-            dot_nt(dq, wq_ref[...].reshape(width, width))
-            + dot_nt(dk, wk_ref[...].reshape(width, width))
-            + dot_nt(dv, wv_ref[...].reshape(width, width))
+    fine = block // 2
+    nf = seq // fine
+    pairs = width // (2 * head)
+    place = Place(rows, ffn)
+    depth = place.depth
+    weight_at = nf
+    attend_at = weight_at + 1
+    input_at = attend_at + pairs
+    others_at = input_at + nb
+    last = others_at + 2
+
+    take = iter(bufs)
+    half_rows = down_out.shape[0] // 2
+    ffn_jobs = []
+    for n in range(4):
+        part = pl.ds(n % 2 * half_rows, half_rows)
+        ref = (down_ref, up_ref)[n // 2]
+        ffn_jobs.append(
+            PairExchange(
+                place, lambda r, z, ref=ref, part=part: ref.at[z, r, part], stage.at[n % 2], stage_load.at[n],
+                *(next(take) for _ in range(5)),
+            )
         )
-        hat, inverse = norm_parts(x_ref[...].astype(F32))
-        sums_s[0:1, :] += col_sum(dh * hat)
-        sums_s[1:2, :] += col_sum(dh)
-        sums_s[2:3, :] += col_sum(dq.astype(F32))
-        sums_s[3:4, :] += col_sum(dv.astype(F32))
-        dx_ref[...] = dx2_ref[...] + norm_back(dh * gain_ref[...], hat, inverse)
+    proj_jobs = []
+    for n in range(4):
+        held = grads.at[n % 2]
+        proj_jobs.append(
+            CoreExchange(place, lambda r, z, c, held=held: held.at[r, z, c], held, *(next(take) for _ in range(6)))
+        )
+    small, late = (AllSum(place, *(next(take) for _ in range(4))) for _ in range(2))
+    outs = (wo_out, wv_out, wk_out, wq_out)
+
+    def matrix(slot, i):
+        return pltpu.make_async_copy(w_ref.at[:, :, :, i], w_s.at[slot], load.at[slot])
+
+    h_copy = pltpu.make_async_copy(h_ref, g_s, load.at[3])
+
+    def start():
+        place.enter()
+        matrix(0, 3).start()
+        matrix(1, 1).start()
+        matrix(2, 2).start()
+        ffn_jobs[0].leave()
+        ffn_jobs[1].leave()
+        acc_s[...] = jnp.zeros_like(acc_s)
+        ghs_s[...] = jnp.zeros_like(ghs_s)
+        matrix(0, 3).wait()
+
+    def start_small():
+        small.stages[0] = small_ref[...]
+        small.stages[0, 0:5, :] = acc_s[4:9, :]
+        small.stages[0, 6:7, 0 : ghs_s.shape[0]] = ghs_s[...].T[0:1, :]
+        small.begin()
+
+    def start_late():
+        late.stages[0] = acc_s[0:8, :]
+        late.begin()
+
+    def take_h():
+        h_copy.wait()
+        left_s[...] = g_s[...].T
+
+    at_steps(step, {
+        0: [start],
+        weight_at: [start_small],
+        attend_at: [matrix(0, 0).start, ffn_jobs[0].one, functools.partial(small.add, 0), ffn_jobs[2].leave],
+        attend_at + 2: [ffn_jobs[1].one, functools.partial(small.add, 1)],
+        attend_at + 3: [ffn_jobs[0].two, proj_jobs[0].leave, ffn_jobs[3].leave],
+        attend_at + 6: [ffn_jobs[2].one, functools.partial(small.add, 2)],
+        attend_at + 7: [ffn_jobs[1].two, proj_jobs[0].one],
+        input_at: [h_copy.start, matrix(0, 0).wait, matrix(1, 1).wait, matrix(2, 2).wait],
+        input_at + 2: [ffn_jobs[3].one, ffn_jobs[2].two, proj_jobs[0].two],
+        others_at: [start_late, take_h, ffn_jobs[3].two],
+        others_at + 1: [proj_jobs[1].leave, functools.partial(late.add, 0)],
+        others_at + 2: [proj_jobs[2].leave, proj_jobs[1].one, functools.partial(late.add, 1)],
+    })
+
+    def sums_from(first):
+        def sums(*parts):
+            for n, part in enumerate(parts):
+                acc_s[first + n : first + n + 1, :] += part
+
+        return sums
+
+    @pl.when(step < nf)
+    def _():
+        here = pl.ds(pl.multiple_of(step * fine, fine), fine)
+
+        def put(ref):
+            def store(value):
+                ref[here, :] = value
+
+            return store
+
+        c = c_ref[...]
+        left_s[:, here] = c.T
+        inner = norms_back(
+            dh2_ref[...], x2_ref[...], o_ref[...], c, valid_grad(ct_ref[...], length_ref[0], step * fine),
+            w_s[0].reshape(width, width), fg_ref[...], pg_ref[...], hs_ref[...], head, sums_from(4), put(g_s), put(dx2_s),
+            put(dq_s),
+        )
+        inner_s[step] = inner
+        ghs_s[...] += jnp.broadcast_to(jnp.sum(inner, axis=-1, keepdims=True), ghs_s.shape)
+
+    def project(n, right_s):
+        cut = width // 2
+        for i in range(2):
+            cols = slice(i * cut, (i + 1) * cut)
+            value = dot_nn(left_s[...], right_s[:, cols]).astype(BF16)
+            grads[n % 2, ..., cols] = value.reshape(grads.shape[1:-1] + (cut,))
+        proj_jobs[n].begin()
+
+    @pl.when(step == weight_at)
+    def _():
+        project(0, dq_s)
+
+    @pl.when((step >= attend_at) & (step < input_at))
+    def _():
+        pair = step - attend_at
+        cols = pl.ds(pl.multiple_of(pair * (2 * head), 2 * head), 2 * head)
+        inner_rows = [
+            jnp.concatenate([inner_s[i, pl.ds(2 * pair + n, 1), :] for i in range(nf)], axis=1) for n in range(2)
+        ]
+
+        def store(j, dk, dv):
+            dk_s[j * block : (j + 1) * block, cols] = dk
+            dv_s[j * block : (j + 1) * block, cols] = dv
+
+        attend_back_pair(
+            length_ref[0], q_ref[...], lambda j: k_ref[j * block : (j + 1) * block, :],
+            lambda j: v_ref[j * block : (j + 1) * block, :], g_s[:, cols], lse_ref, lambda n: inner_rows[n], dqa_s, store,
+            seq, block, head,
+        )
+        dq_s[:, cols] = (dqa_s[...] * factor).astype(BF16)
+
+    @pl.when((step >= input_at) & (step < others_at))
+    def _():
+        here = pl.ds(pl.multiple_of((step - input_at) * block, block), block)
+        dx_ref[...] = input_back(
+            dq_s[here, :], dk_s[here, :], dv_s[here, :], lambda i: w_s[i].reshape(width, width), x_ref[...], dx2_s[here, :],
+            gain_ref[...], sums_from(0),
+        )
+
+    for n, right_s in ((1, dv_s), (2, dk_s), (3, dq_s)):
+
+        @pl.when(step == others_at + n - 1)
+        def _(n=n, right_s=right_s):
+            project(n, right_s)
 
     @pl.when(step == last)
     def _():
-        if fused:
-            stages = refs[28]
-            stages[0] = small_ref[...]
-            stages[0, 0:4, :] = sums_s[0:4, :]
-            small.begin()
-            half = len(rest) // 2
-            for action in actions(rest[:half]):
-                action()
-            small.add(0)
-            for action in actions(rest[half:]):
-                action()
-            small.add(1)
-            small.add(2)
-            for job, out in zip(jobs, grad_refs):
-                out[...] = job.total()
-            small_out[...] = small.total()
-            small.finish()
-            for job in jobs:
-                job.finish()
-        else:
-            small_out[...] = small_ref[...]
-            small_out[0:4, :] = sums_s[0:4, :]
-
-
-def last_stage(dq, dk, dv, dor, h, c, w, w_specs, x, dx2, gain, small, rows, ffn, block, fused):
-    seq, width = dq.shape
-    nb = seq // block
-    part = pl.BlockSpec((block, width), lambda i: (clip(i, 4, nb), 0))
-    full = whole((seq, width))
-    piece = (width // (rows * ffn), width)
+        _, wv, wk, wq = proj_jobs
+        for action in (
+            wq.leave, functools.partial(late.add, 2), wk.one, wv.two, wq.one, wk.two, wq.two,
+        ):
+            action()
+        for n, job in enumerate(ffn_jobs):
+            (down_out, up_out)[n // 2][n % 2 * half_rows : (n % 2 + 1) * half_rows, :] = job.total()
+        small_out[0:8, :] = late.total()
+        small_out[8:, :] = small.total()
+        for job in (small, late):
+            job.finish()
+        for job, out in zip(proj_jobs, outs):
+            out[...] = job.total()
+
+
+def tail(
+    length, dh2, ct, x2, o, c, x, fg, pg, hs, gain, small, q, k, v, lse, h, w, down, up, rows, ffn, block, head, factor
+):
+    seq, width = dh2.shape
+    nb, pairs, heads = seq // block, width // (2 * head), width // head
     depth = ffn // 2
-    scratch = [pltpu.VMEM((width, seq), BF16), pltpu.VMEM((8, width), F32)]
-    out_specs = [part, out_whole(small.shape)]
-    out_shape = [sds((seq, width), F32), sds(small.shape, F32)]
-    if fused:
-        scratch = [pltpu.VMEM((rows, depth, 2) + piece, BF16)] * 4 + scratch
-        scratch += scatter_scratch(piece, rows, depth, False) * 4 + [
-            pltpu.VMEM((6,) + small.shape, F32),
-            pltpu.VMEM((depth,) + small.shape, F32),
-            pltpu.SemaphoreType.DMA((2 + depth,)),
-            pltpu.SemaphoreType.DMA((2 + depth,)),
-        ]
-        out_specs += [pl.BlockSpec(memory_space=pltpu.VMEM)] * 4
-        out_shape += [sds(piece, F32)] * 4
-    else:
-        out_specs += [out_whole((width, width))] * 4
-        out_shape += [sds((width, width), BF16)] * 4
+    fine = block // 2
+    nf = seq // fine
+    input_at = nf + 1 + pairs
+    first = pl.BlockSpec((fine, width), lambda i: (clip(i, 0, nf), 0))
+    final = pl.BlockSpec((block, width), lambda i: (clip(i, input_at, nb), 0))
+    cols = pl.BlockSpec((None, seq, 2 * head), lambda i: (clip(i, nf + 1, pairs), 0, 0))
+    smem = pl.BlockSpec(memory_space=pltpu.SMEM)
+    hbm = pl.BlockSpec(memory_space=pl.ANY)
+    vmem = pl.BlockSpec(memory_space=pltpu.VMEM)
+    vec = whole((1, width))
+    unit = down.shape[2:]
+    piece = (unit[0] // 2, unit[1])
+    proj = (width // (rows * ffn), width)
+    dma = pltpu.SemaphoreType.DMA
+
+    def arrivals(shape):
+        return [pltpu.VMEM((depth, 2) + shape, BF16), pltpu.VMEM((depth,) + shape, BF16), pltpu.VMEM((depth,) + shape, BF16)]
+
+    scratch = [
+        pltpu.VMEM((3, rows, depth, 2) + proj, BF16),
+        pltpu.VMEM((seq, width), BF16), pltpu.VMEM((seq, width), BF16), pltpu.VMEM((seq, width), BF16),
+        pltpu.VMEM((seq, width), BF16), pltpu.VMEM((width, seq), BF16), pltpu.VMEM((seq, width), F32),
+        pltpu.VMEM((nf, heads, fine), F32), pltpu.VMEM((seq, 2 * head), F32), pltpu.VMEM((16, width), F32),
+        pltpu.VMEM((heads, 128), F32), dma((4,)),
+        pltpu.VMEM((2, depth, 2) + piece, BF16), dma((4, depth, 2)), pltpu.VMEM((2, rows, depth, 2) + proj, BF16),
+    ]
+    for _ in range(4):
+        scratch += arrivals(piece) + [dma((4,)), dma((4, depth))]
+    for _ in range(4):
+        scratch += [pltpu.VMEM((depth, rows) + proj, BF16)] + arrivals(proj) + [dma((4,)), dma((8, depth))]
+    late = (8, width)
+    for shape in (small.shape, late):
+        scratch += [pltpu.VMEM((6,) + shape, F32), pltpu.VMEM((depth,) + shape, F32), dma((2 + depth,)), dma((2 + depth,))]
     return pl.pallas_call(
-        functools.partial(last_kernel, rows=rows, ffn=ffn, block=block, fused=fused),
-        grid=(4 + nb,),
-        in_specs=[full] * 6 + list(w_specs) + [part, part, whole((1, width)), whole(small.shape)],
-        out_specs=out_specs,
-        out_shape=out_shape,
+        functools.partial(tail_kernel, rows=rows, ffn=ffn, block=block, head=head, factor=factor),
+        grid=(input_at + nb + 3,),
+        in_specs=[smem] + [first] * 5 + [final] + [vec] * 4 + [whole(small.shape)] + [cols] * 3
+        + [pl.BlockSpec((1, 2, seq), lambda i: (clip(i, nf + 1, pairs), 0, 0))] + [hbm] * 4,
+        out_specs=[final] + [vmem] * 7,
+        out_shape=[sds((seq, width), F32), sds((8 + small.shape[0], width), F32), sds(unit, F32), sds(unit, F32)] + [sds(proj, F32)] * 4,
         scratch_shapes=scratch,
-        compiler_params=params(60 * MIB, **comm_params(fused, 2)),
-        name="input_and_weights",
-    )(dq, dk, dv, dor, h, c, *[w] * 3, x, dx2, gain, small)
+        compiler_params=params(62 * MIB, **comm_params(True, 2)),
+        name="backward_and_sums",
+    )(length, dh2, ct, x2, o, c, x, fg, pg, hs, gain, small, q, k, v, lse, h, w, down, up)
 
 
 def widen(blocks, lanes):
@@ -1124,18 +1430,16 @@
     rows, ffn = lax.axis_size("rows"), lax.axis_size("ffn")
     own_units = w_up.shape[1]
     hidden = own_units * ffn
-    fused = w_query.shape[0] % 16 == 0 and own_units % 128 == 0
-    four = jnp.stack([w_query, w_key, w_value, w_out])
+    fused = ffn == 8 and w_query.shape[0] % 16 == 0 and own_units % 512 == 0
+    weights = (w_query, w_key, w_value, w_out, w_down, w_up)
     vectors = [
         rows_of(v)
         for v in (
             ln_attn_gain, ln_attn_bias, query_bias, value_bias, out_bias, post_gain, post_bias, ffn_gain, ffn_bias,
         )
     ]
-    if fused:
-        weights = (four, w_down, w_up)
-    else:
-        attn, down_all, up_all = gather_all(rows, ffn, four, w_down, w_up)
+    if not fused:
+        attn, down_all, up_all = gather_all(rows, ffn, weights)
         attn = attn.transpose(3, 0, 1, 2, 4, 5).reshape(4, width, width)
         weights = (attn,)
     h, q, k, v, c, lse, o, x2, h2, *gathered = front(
@@ -1143,17 +1447,6 @@
     )
     if fused:
         attn, down_all, up_all = gathered
-
-        def w_spec(i):
-            return pl.BlockSpec(
-                (rows, ffn // 2, 2, None) + four.shape[1:], lambda *_: (0, 0, 0, i, 0, 0), pipeline_mode=pl.Buffered(1)
-            )
-
-    else:
-
-        def w_spec(i):
-            return pl.BlockSpec((None, width, width), lambda *_: (i, 0, 0), pipeline_mode=pl.Buffered(1))
-
     wup = widen(up_all.reshape(ffn, width, own_units), 512)
     wdn = widen(down_all.reshape(ffn, width, own_units), 512)
     nb, _, hb = wup.shape
@@ -1162,40 +1455,83 @@
         lengths, h2, cotangent, x2, wup, wdn, units(up_bias), units(mid_gain), units(mid_bias), rows_of(down_bias),
         block,
     )
-    g_up, g_dn = ffn_weight_grads(lengths, h2, cotangent, m, du)
-    g_up, g_dn = (narrow(part, own_units).reshape((ffn // 2, 2, rows) + w_up.shape) for part in (g_up, g_dn))
     scale_cols = rows_of(jnp.repeat(head_scale, head))
-    dx2, dor, dq, dk, dv, g_hs, g_fg, g_fb, g_pg, g_pb, g_ob, *summed = back(
-        lengths, dh2, cotangent, x2, o, c, attn, w_spec(3), rows_of(ffn_gain), rows_of(post_gain), scale_cols, q, k, v,
-        lse, (g_dn, g_up), rows, ffn, block, head, factor, fused,
+    wide = [part.reshape(-1, width) for part in (g_ub, g_mg, g_mb)]
+    above = jnp.concatenate([g_db, jnp.zeros((1, width), F32)] + wide, axis=0)
+    above = jnp.pad(above, ((5, -(5 + above.shape[0]) % 8), (0, 0)))
+    if fused:
+        g_dn, g_up = (
+            part.reshape((ffn // 2, rows) + w_up.shape)
+            for part in ffn_weight_pair_sums(lengths, h2, cotangent, m, du, rows, ffn)
+        )
+        dx, small, grad_down, grad_up, g_wo, g_wv, g_wk, g_wq = tail(
+            lengths, dh2, cotangent, x2, o, c, tokens, rows_of(ffn_gain), rows_of(post_gain), scale_cols,
+            rows_of(ln_attn_gain), above, q, k, v, lse, h, attn, g_dn, g_up, rows, ffn, block, head, factor,
+        )
+    else:
+        g_up, g_dn = ffn_weight_grads(lengths, h2, cotangent, m, du)
+        dx2, dor, dq, dk, dv, g_hs, late = back(
+            lengths, dh2, cotangent, x2, o, c, attn[3], rows_of(ffn_gain), rows_of(post_gain), scale_cols, q, k, v, lse,
+            block, head, factor,
+        )
+        dx, early = input_grad(dq, dk, dv, attn[:3], tokens, dx2, rows_of(ln_attn_gain), block)
+        g_hs = jnp.pad(g_hs[:, :1].T, ((0, 0), (0, width - heads)))
+        small = jnp.concatenate([early, late[:5], above[5:6], g_hs, above[7:]], axis=0)
+        small = lax.psum(small, BOTH)
+        grad_down, grad_up = (
+            scatter_sum(rows, ffn, narrow(part, own_units).reshape((ffn // 2, 2, rows) + w_up.shape), by_unit)
+            for part in (g_dn, g_up)
+        )
+        g_wo, g_wv, g_wk, g_wq = (
+            scatter_sum(
+                rows, ffn, weight_grad(left, right, 512).reshape((rows, ffn // 2, 2) + w_query.shape), by_device
+            )
+            for left, right in ((c, dor), (h, dv), (h, dk), (h, dq))
+        )
+    n = hidden // width
+    vectors = jnp.concatenate([small[:4], small[8:14]], axis=0)
+    owned = small[15 : 15 + 3 * n].reshape(3, ffn, own_units)
+    if fused:
+        (
+            dx, grad_up, grad_down, g_wq, g_wk, g_wv, g_wo, g_lg, g_lb, g_qb, g_vb, g_ob, g_pg, g_pb, g_fg, g_fb, g_db,
+        ) = hand_on(dx, grad_up, grad_down, g_wq, g_wk, g_wv, g_wo, vectors)
+    else:
+        g_lg, g_lb, g_qb, g_vb, g_ob, g_pg, g_pb, g_fg, g_fb, g_db = vectors
+    g_hs = small[14, :heads] / head_scale
+    mine = lax.dynamic_index_in_dim(owned, lax.axis_index("ffn"), axis=1, keepdims=False)
+    return (
+        result, dx, g_lg, g_lb, g_wq, g_qb, g_wk, g_wv, g_vb, g_hs, g_wo, g_ob, g_pg, g_pb, g_fg, g_fb, grad_up, mine[0],
+        mine[1], mine[2], grad_down, g_db,
     )
-    if fused:
-        grad_down, grad_up = summed
-    else:
-        grad_down, grad_up = (scatter_sum(rows, ffn, part, by_unit) for part in (g_dn, g_up))
-    g_hs = jnp.pad(rows_of(g_hs[:, 0] / head_scale), ((0, 0), (0, width - heads)))
-    wide = [part.reshape(-1, width) for part in (g_ub, g_mg, g_mb)]
-    small = jnp.concatenate([jnp.zeros((4, width), F32), g_ob, g_pg, g_pb, g_fg, g_fb, g_db, g_hs] + wide, axis=0)
-    small = jnp.pad(small, ((0, -small.shape[0] % 8), (0, 0)))
-    dx, small, *attn_grads = last_stage(
-        dq, dk, dv, dor, h, c, attn, [w_spec(i) for i in range(3)], tokens, dx2, rows_of(ln_attn_gain), small, rows, ffn,
-        block, fused,
-    )
-    if not fused:
-        small = lax.psum(small, BOTH)
-        attn_grads = [
-            scatter_sum(rows, ffn, part.reshape((rows, ffn // 2, 2) + w_query.shape), by_device) for part in attn_grads
-        ]
-    g_wo, g_wv, g_wk, g_wq = attn_grads
-    n = hidden // width
-    mine = lax.axis_index("ffn") * own_units
-    g_ub, g_mg, g_mb = (
-        lax.dynamic_slice(small[11 + i * n : 11 + (i + 1) * n].reshape(hidden), (mine,), (own_units,)) for i in range(3)
-    )
-    return (
-        result, dx, small[0], small[1], g_wq, small[2], g_wk, g_wv, small[3], small[10, :heads], g_wo, small[4],
-        small[5], small[6], small[7], small[8], grad_up, g_ub, g_mg, g_mb, grad_down, small[9],
-    )
+
+
+def hand_on_kernel(*refs):
+    ins, vectors, outs, lines = refs[:7], refs[7], refs[8:15], refs[15:]
+    outs[0][...] = ins[0][...]
+
+    @pl.when(pl.program_id(0) == 0)
+    def _():
+        for src, out in zip(ins[1:], outs[1:]):
+            out[...] = src[...]
+        for n, line in enumerate(lines):
+            line[...] = vectors[n, :]
+
+
+def hand_on(dx, *rest):
+    *grads, vectors = rest
+    seq, width = dx.shape
+    n = vectors.shape[0]
+    block = seq // 4
+    rows = pl.BlockSpec((block, width), lambda i: (i, 0))
+    return pl.pallas_call(
+        hand_on_kernel,
+        grid=(4,),
+        in_specs=[rows] + [whole(a.shape) for a in grads] + [whole(vectors.shape)],
+        out_specs=[rows] + [out_whole(a.shape) for a in grads] + [out_whole((width,))] * n,
+        out_shape=[sds(a.shape, F32) for a in (dx, *grads)] + [sds((width,), F32)] * n,
+        compiler_params=params(),
+        name="hand_on",
+    )(dx, *grads, vectors)
 
 
 def solution(mesh):

time: 420 us -> 375 us (0.89)
  Pallas kernels: 390 us -> 362 us
  local copies, waits for them, and re-layouts: 18.7 us -> 3.85 us
    pallas_call x3, Pallas kernels: 195 us -> 165 us  [the longest x1 130 us: tail(): pl.pallas_call(functools.partial(tail_kernel, rows=rows, ffn=ffn, block=b...]
    unnamed x31 -> x12, local copies, waits for them, and re-layouts: 10 us -> 0.04 us
where the time goes in v5:
time: 375 us; the launch traced here: 368 us
  Pallas kernels  362 us (97%)
  local copies, waits for them, and re-layouts  3.85 us (1%)
    pallas_call x1, Pallas kernels, tail(): pl.pallas_call(functools.partial(tail_kernel, rows=rows, ffn=ffn, block=b...  130 us
    pallas_call x1, Pallas kernels, front(): pl.pallas_call(functools.partial(front_kernel, rows=rows, ffn=ffn, block=...  127 us
    pallas_call x1, Pallas kernels, feed_forward(): pl.pallas_call(ffn_kernel, grid=(seq // block,), in_specs=[smem, rows, ro...  69.3 us
    pallas_call x1, Pallas kernels, ffn_weight_pair_sums(): pl.pallas_call(functools.partial(ffn_weights_pair_kernel, rows=rows, ffn=...  29.1 us

profile of v5, /device:TPU:0, one launch (start us, length us, event | category | flops | bytes accessed | tf_op | source)
XLA Modules:
  0.0 368.4 jit_solution(84332022416176369)
XLA Ops:
  1.3 127.0 %forward_attention.1 = (bf16[1024,1024]{1,0:T(8,128)(2,1)}, bf16[8,1024,128]{2,1,0:T(8,128)(2,1)}, bf16[8,1024,128]{2,1,0:T(8,128)(2,1)}, bf16[8,1024,128]{2,1,0...) custom-call(s32[1]{0:T(128)S(6)} %copy.45.refs_0_.length_ref, ...), custom_call_target="tpu_custom_call" | custom-call | tf_op jit(solution)/shard_map/forward_attention/pallas_call | solution.py:694
  128.3 69.3 %feed_forward.1 = (f32[1024,1024]{1,0:T(8,128)}, f32[1024,1024]{1,0:T(8,128)}, bf16[8,1024,512]{2,1,0:T(8,128)(2,1)}, bf16[8,1024,512]{2,1,0:T(8,128)(2,1)}, f32...) custom-call(s32[1]{0:T(128)S(6)} %copy.45.refs_0_.length_ref, ...), custom_call_target="tpu_custom_call" | custom-call | flops 68719476736 | bytes 62914560 | tf_op jit(solution)/shard_map/feed_forward/pallas_call | solution.py:809
  197.6 0.0 copy-start.3
  197.7 0.0 copy-start.2
  197.7 0.0 copy-start.1
  197.7 0.0 copy-start.4
  197.7 0.0 copy-start.5
  197.7 29.1 %ffn_weight_pair_sums.1 = (bf16[4,1024,512]{2,1,0:T(8,128)(2,1)}, bf16[4,1024,512]{2,1,0:T(8,128)(2,1)}) custom-call(s32[1]{0:T(128)S(6)} %copy.45.refs_0_.length_ref, bf16[1024,1024]{1,0:T(8,128)(2,1)} %get-tuple-element.69.h2_ref, bf16[1024,1024]{1,0:T(8,128)(2,1)} %ct_ref.5, bf16[8,1024,512]{2,1,0:T(8,128)(2,1)} %get-tuple-element.87.m_ref, ...), custom_call_target="tpu_custom_call" | custom-call | tf_op jit(solution)/shard_map/ffn_weight_pair_sums/pallas_call | solution.py:890
  226.8 0.0 copy-done.3
  226.9 0.0 copy-done.2
  227.0 0.0 copy-done.1
  227.1 0.0 copy-done.4
  227.1 0.2 concatenate.6
  227.2 0.7 pad.4.small_ref
  227.9 0.0 copy-done.5
  227.9 0.1 broadcast_in_dim.6
  228.0 0.7 reshape_reshape.3.hs_ref
  228.6 130.3 %backward_and_sums.1 = (f32[1024,1024]{1,0:T(8,128)}, f32[32,1024]{1,0:T(8,128)}, f32[256,512]{1,0:T(8,128)}, f32[256,512]{1,0:T(8,128)}, f32[32,1024]{1,0:T(8,1...) custom-call(s32[1]{0:T(128)S(6)} %copy.45.refs_0_.length_ref, ...), custom_call_target="tpu_custom_call" | custom-call | tf_op jit(solution)/shard_map/backward_and_sums/pallas_call | solution.py:1387
  358.9 0.8 slice.25
  359.8 0.8 slice.24
  360.5 0.6 pad_maximum_fusion.refs_7_
  361.2 5.9 %hand_on.1 = (f32[1024,1024]{1,0:T(8,128)}, f32[256,512]{1,0:T(8,128)}, f32[256,512]{1,0:T(8,128)}, f32[32,1024]{1,0:T(8,128)}, f32[32,1024]{1,0:T(8,128)}, /*in...) custom-call(f32[1024,1024]{1,0:T(8,128)} %get-tuple-element.91.refs_, ...), custom_call_target="tpu_custom_call" | custom-call | tf_op jit(solution)/shard_map/hand_on/pallas_call | solution.py:1526
  367.1 0.6 constant_dynamic-slice_fusion.2
  367.7 0.5 bitcast_divide_fusion
  (11 shorter events, 0.2 us)
Async XLA Ops:
  197.6 29.2 %copy-start.3 = (f32[8,1,512]{2,1,0:T(1,128)S(1)}, f32[8,1,512]{2,1,0:T(1,128)}, u32[]{:S(2)}) copy-start(f32[8,1,512]{2,1,0:T(1,128)} %get-tuple-element.78) | copy-start | bytes 49156
  197.7 29.2 %copy-start.2 = (f32[8,1,512]{2,1,0:T(1,128)S(1)}, f32[8,1,512]{2,1,0:T(1,128)}, u32[]{:S(2)}) copy-start(f32[8,1,512]{2,1,0:T(1,128)} %get-tuple-element.79) | copy-start | bytes 49156
  197.7 29.3 %copy-start.1 = (f32[8,1,512]{2,1,0:T(1,128)S(1)}, f32[8,1,512]{2,1,0:T(1,128)}, u32[]{:S(2)}) copy-start(f32[8,1,512]{2,1,0:T(1,128)} %get-tuple-element.80) | copy-start | bytes 49156
  197.7 29.4 %copy-start.4 = (f32[1,1024]{1,0:T(1,128)S(1)}, f32[1,1024]{1,0:T(1,128)}, u32[]{:S(2)}) copy-start(f32[1,1024]{1,0:T(1,128)} %get-tuple-element.77) | copy-start | bytes 12292
  197.7 30.2 %copy-start.5 = (f32[16]{0:T(128)S(1)}, f32[16]{0:T(128)}, u32[]{:S(2)}) copy-start(f32[16]{0:T(128)} %refs_1_.1) | copy-start | bytes 196
  358.9 8.1 %copy-start = (f32[32,1024]{1,0:T(8,128)S(1)}, f32[32,1024]{1,0:T(8,128)}, u32[]{:S(2)}) copy-start(f32[32,1024]{1,0:T(8,128)} %get-tuple-element.98) | copy-start | bytes 393220

commit v6 on v5

--- a/solution.py
+++ b/solution.py
@@ -704,25 +704,14 @@
 
 
 def ffn_kernel(
-    length_ref, h2_ref, ct_ref, x2_ref, up_ref, dn_ref, ub_ref, mg_ref, mb_ref, db_ref,
+    length_ref, h2_ref, ct_ref, x2_ref, wup_ref, wdn_ref, ub_ref, mg_ref, mb_ref, db_ref,
     res_ref, dh2_ref, m_ref, du_ref, gub_ref, gmg_ref, gmb_ref, gdb_ref,
-    e_s, gp_s, dm_s, wup_ref, wdn_ref, load,
+    e_s, gp_s, dm_s,
 ):
     step = pl.program_id(0)
     block, width = h2_ref.shape
     nb, _, hb = wup_ref.shape
 
-    def loads(j):
-        return [
-            pltpu.make_async_copy(src.at[j], dst.at[j], load.at[n, j])
-            for n, (src, dst) in enumerate(((up_ref, wup_ref), (dn_ref, wdn_ref)))
-        ]
-
-    @pl.when(step == 0)
-    def _():
-        for j in range(nb):
-            for copy in loads(j):
-                copy.start()
     units = nb * hb
     row = lax.broadcasted_iota(jnp.int32, (block, width), 0) + step * block
     valid = row < length_ref[0]
@@ -739,9 +728,6 @@
     gdb_ref[...] += col_sum(dfr.astype(F32))
 
     def first(j, sums, wait):
-        if wait:
-            for copy in loads(j):
-                copy.wait()
         u = dot_nn(h2, wup_ref[j]) + ub_ref[j]
         dm = dot_nn(dfr, wdn_ref[j])
         cdf = 0.5 * (1.0 + lax.erf(u * math.sqrt(0.5)))
@@ -788,13 +774,7 @@
         res_ref[...] = jnp.where(valid, x2_ref[...] + f + db_ref[...], 0.0)
         dh2_ref[...] = dh2
 
-    @pl.when(step == 0)
-    def _():
-        rows(True)
-
-    @pl.when(step > 0)
-    def _():
-        rows(False)
+    rows(False)
 
 
 def feed_forward(length, h2, ct, x2, wup, wdn, ub, mg, mb, db, block):
@@ -810,7 +790,7 @@
         ffn_kernel,
         grid=(seq // block,),
         in_specs=[
-            smem, rows, rows, rows, hbm, hbm,
+            smem, rows, rows, rows, whole((nb, width, hb)), whole((nb, width, hb)),
             units, units, units, whole((1, width)),
         ],
         out_specs=[rows, rows, blocks, blocks, sums, sums, sums, out_whole((1, width))],
@@ -818,8 +798,7 @@
             sds((seq, width), F32), sds((seq, width), F32), sds((nb, seq, hb), BF16), sds((nb, seq, hb), BF16),
             sds((nb, 1, hb), F32), sds((nb, 1, hb), F32), sds((nb, 1, hb), F32), sds((1, width), F32),
         ],
-        scratch_shapes=[pltpu.VMEM((nb, block, hb), F32)] * 3 + [pltpu.VMEM((nb, width, hb), BF16)] * 2
-        + [pltpu.SemaphoreType.DMA((2, nb))],
+        scratch_shapes=[pltpu.VMEM((nb, block, hb), F32)] * 3,
         compiler_params=params(60 * MIB),
         cost_estimate=pl.CostEstimate(
             flops=16 * seq * width * nb * hb, bytes_accessed=60 * MIB, transcendentals=2 * seq * nb * hb
@@ -866,9 +845,11 @@
 
     @pl.when(step < depth)
     def _():
-        for c in range(2):
+        @pl.loop(0, 2)
+        def _(c):
             grads_s[0, step, c] = dot_nn(dft_s[...], m_ref[c]).astype(BF16)
             grads_s[1, step, c] = dot_nn(h2t_s[...], du_ref[c]).astype(BF16)
+
         for a in range(2):
             give(a, step).start()
 
@@ -1171,11 +1152,12 @@
 
 def tail_kernel(
     length_ref, dh2_ref, ct_ref, x2_ref, o_ref, c_ref, x_ref, fg_ref, pg_ref, hs_ref, gain_ref, small_ref,
-    q_ref, k_ref, v_ref, lse_ref, h_ref, w_ref, down_ref, up_ref,
+    q_ref, k_ref, v_ref, lse_ref, wo_ref, h_ref, w_ref, down_ref, up_ref,
     dx_ref, small_out, down_out, up_out, wo_out, wv_out, wk_out, wq_out,
-    w_s, g_s, dq_s, dk_s, dv_s, left_s, dx2_s, inner_s, dqa_s, acc_s, ghs_s, load,
+    w_s, g_s, right_s, left_s, dx2_s, inner_s, dqa_s, acc_s, ghs_s, load,
     stage, stage_load, grads, *bufs, rows, ffn, block, head, factor,
 ):
+    dq_s, dk_s, dv_s = (right_s.at[i] for i in range(3))
     step = pl.program_id(0)
     seq, width = g_s.shape
     nb = seq // block
@@ -1218,14 +1200,12 @@
 
     def start():
         place.enter()
-        matrix(0, 3).start()
-        matrix(1, 1).start()
-        matrix(2, 2).start()
+        for i in range(3):
+            matrix(i, i).start()
         ffn_jobs[0].leave()
         ffn_jobs[1].leave()
         acc_s[...] = jnp.zeros_like(acc_s)
         ghs_s[...] = jnp.zeros_like(ghs_s)
-        matrix(0, 3).wait()
 
     def start_small():
         small.stages[0] = small_ref[...]
@@ -1244,7 +1224,7 @@
     at_steps(step, {
         0: [start],
         weight_at: [start_small],
-        attend_at: [matrix(0, 0).start, ffn_jobs[0].one, functools.partial(small.add, 0), ffn_jobs[2].leave],
+        attend_at: [ffn_jobs[0].one, functools.partial(small.add, 0), ffn_jobs[2].leave],
         attend_at + 2: [ffn_jobs[1].one, functools.partial(small.add, 1)],
         attend_at + 3: [ffn_jobs[0].two, proj_jobs[0].leave, ffn_jobs[3].leave],
         attend_at + 6: [ffn_jobs[2].one, functools.partial(small.add, 2)],
@@ -1277,23 +1257,26 @@
         left_s[:, here] = c.T
         inner = norms_back(
             dh2_ref[...], x2_ref[...], o_ref[...], c, valid_grad(ct_ref[...], length_ref[0], step * fine),
-            w_s[0].reshape(width, width), fg_ref[...], pg_ref[...], hs_ref[...], head, sums_from(4), put(g_s), put(dx2_s),
+            wo_ref[...].reshape(width, width), fg_ref[...], pg_ref[...], hs_ref[...], head, sums_from(4), put(g_s), put(dx2_s),
             put(dq_s),
         )
         inner_s[step] = inner
         ghs_s[...] += jnp.broadcast_to(jnp.sum(inner, axis=-1, keepdims=True), ghs_s.shape)
 
-    def project(n, right_s):
+    @pl.when((step == weight_at) | (step >= others_at))
+    def _():
+        first = step == weight_at
+        right = right_s.at[jnp.where(first, 0, last - step)]
+        slot = jnp.where(first, 0, lax.rem(step - others_at + 1, 2))
         cut = width // 2
-        for i in range(2):
-            cols = slice(i * cut, (i + 1) * cut)
-            value = dot_nn(left_s[...], right_s[:, cols]).astype(BF16)
-            grads[n % 2, ..., cols] = value.reshape(grads.shape[1:-1] + (cut,))
-        proj_jobs[n].begin()
-
-    @pl.when(step == weight_at)
-    def _():
-        project(0, dq_s)
+
+        @pl.loop(0, 2)
+        def _(i):
+            cols = pl.ds(pl.multiple_of(i * cut, cut), cut)
+            value = dot_nn(left_s[...], right[:, cols]).astype(BF16)
+            grads[slot, ..., cols] = value.reshape(grads.shape[1:-1] + (cut,))
+
+    at_steps(step, {weight_at: [proj_jobs[0].begin], **{others_at + n: [proj_jobs[n + 1].begin] for n in range(3)}})
 
     @pl.when((step >= attend_at) & (step < input_at))
     def _():
@@ -1321,12 +1304,6 @@
             dq_s[here, :], dk_s[here, :], dv_s[here, :], lambda i: w_s[i].reshape(width, width), x_ref[...], dx2_s[here, :],
             gain_ref[...], sums_from(0),
         )
-
-    for n, right_s in ((1, dv_s), (2, dk_s), (3, dq_s)):
-
-        @pl.when(step == others_at + n - 1)
-        def _(n=n, right_s=right_s):
-            project(n, right_s)
 
     @pl.when(step == last)
     def _():
@@ -1361,6 +1338,9 @@
     hbm = pl.BlockSpec(memory_space=pl.ANY)
     vmem = pl.BlockSpec(memory_space=pltpu.VMEM)
     vec = whole((1, width))
+    out_weight = pl.BlockSpec(
+        (rows, depth, 2, None) + w.shape[4:], lambda i: (0, 0, 0, 3, 0, 0), pipeline_mode=pl.Buffered(1)
+    )
     unit = down.shape[2:]
     piece = (unit[0] // 2, unit[1])
     proj = (width // (rows * ffn), width)
@@ -1371,8 +1351,8 @@
 
     scratch = [
         pltpu.VMEM((3, rows, depth, 2) + proj, BF16),
-        pltpu.VMEM((seq, width), BF16), pltpu.VMEM((seq, width), BF16), pltpu.VMEM((seq, width), BF16),
-        pltpu.VMEM((seq, width), BF16), pltpu.VMEM((width, seq), BF16), pltpu.VMEM((seq, width), F32),
+        pltpu.VMEM((seq, width), BF16), pltpu.VMEM((3, seq, width), BF16), pltpu.VMEM((width, seq), BF16),
+        pltpu.VMEM((seq, width), F32),
         pltpu.VMEM((nf, heads, fine), F32), pltpu.VMEM((seq, 2 * head), F32), pltpu.VMEM((16, width), F32),
         pltpu.VMEM((heads, 128), F32), dma((4,)),
         pltpu.VMEM((2, depth, 2) + piece, BF16), dma((4, depth, 2)), pltpu.VMEM((2, rows, depth, 2) + proj, BF16),
@@ -1388,13 +1368,13 @@
         functools.partial(tail_kernel, rows=rows, ffn=ffn, block=block, head=head, factor=factor),
         grid=(input_at + nb + 3,),
         in_specs=[smem] + [first] * 5 + [final] + [vec] * 4 + [whole(small.shape)] + [cols] * 3
-        + [pl.BlockSpec((1, 2, seq), lambda i: (clip(i, nf + 1, pairs), 0, 0))] + [hbm] * 4,
+        + [pl.BlockSpec((1, 2, seq), lambda i: (clip(i, nf + 1, pairs), 0, 0)), out_weight] + [hbm] * 4,
         out_specs=[final] + [vmem] * 7,
         out_shape=[sds((seq, width), F32), sds((8 + small.shape[0], width), F32), sds(unit, F32), sds(unit, F32)] + [sds(proj, F32)] * 4,
         scratch_shapes=scratch,
         compiler_params=params(62 * MIB, **comm_params(True, 2)),
         name="backward_and_sums",
-    )(length, dh2, ct, x2, o, c, x, fg, pg, hs, gain, small, q, k, v, lse, h, w, down, up)
+    )(length, dh2, ct, x2, o, c, x, fg, pg, hs, gain, small, q, k, v, lse, w, h, w, down, up)
 
 
 def widen(blocks, lanes):

time: 375 us -> 369 us (0.984); the launches traced: 368 us -> 366 us
    pallas_call x1, Pallas kernels: 69.3 us -> 56.1 us  [feed_forward(): pl.pallas_call(ffn_kernel, grid=(seq // block,), in_specs=[smem, rows, ro...]
    pallas_call x1, Pallas kernels: 130 us -> 141 us  [tail(): pl.pallas_call(functools.partial(tail_kernel, rows=rows, ffn=ffn, block=b...]
where the time goes in v6:
time: 369 us; the launch traced here: 366 us
  Pallas kernels  360 us (98%)
  local copies, waits for them, and re-layouts  3.85 us (1%)
    pallas_call x1, Pallas kernels, tail(): pl.pallas_call(functools.partial(tail_kernel, rows=rows, ffn=ffn, block=b...  141 us
    pallas_call x1, Pallas kernels, front(): pl.pallas_call(functools.partial(front_kernel, rows=rows, ffn=ffn, block=...  127 us
    pallas_call x1, Pallas kernels, feed_forward(): pl.pallas_call(ffn_kernel, grid=(seq // block,), in_specs=[smem, rows, ro...  56.1 us
    pallas_call x1, Pallas kernels, ffn_weight_pair_sums(): pl.pallas_call(functools.partial(ffn_weights_pair_kernel, rows=rows, ffn=...  29.8 us

profile of v6, /device:TPU:0, one launch (start us, length us, event | category | flops | bytes accessed | tf_op | source)
XLA Modules:
  0.0 366.4 jit_solution(4551440551991605993)
XLA Ops:
  1.3 127.0 %forward_attention.1 = (bf16[1024,1024]{1,0:T(8,128)(2,1)}, bf16[8,1024,128]{2,1,0:T(8,128)(2,1)}, bf16[8,1024,128]{2,1,0:T(8,128)(2,1)}, bf16[8,1024,128]{2,1,0...) custom-call(s32[1]{0:T(128)S(6)} %copy.45.refs_0_.length_ref, ...), custom_call_target="tpu_custom_call" | custom-call | tf_op jit(solution)/shard_map/forward_attention/pallas_call | solution.py:694
  128.3 56.1 %feed_forward.1 = (f32[1024,1024]{1,0:T(8,128)}, f32[1024,1024]{1,0:T(8,128)}, bf16[8,1024,512]{2,1,0:T(8,128)(2,1)}, bf16[8,1024,512]{2,1,0:T(8,128)(2,1)}, f32...) custom-call(s32[1]{0:T(128)S(6)} %copy.45.refs_0_.length_ref, ...), custom_call_target="tpu_custom_call" | custom-call | flops 68719476736 | bytes 62914560 | tf_op jit(solution)/shard_map/feed_forward/pallas_call | solution.py:789
  184.4 0.0 copy-start.3
  184.4 0.0 copy-start.2
  184.5 0.0 copy-start.1
  184.5 0.0 copy-start.4
  184.5 0.0 copy-start.5
  184.5 29.8 %ffn_weight_pair_sums.1 = (bf16[4,1024,512]{2,1,0:T(8,128)(2,1)}, bf16[4,1024,512]{2,1,0:T(8,128)(2,1)}) custom-call(s32[1]{0:T(128)S(6)} %copy.45.refs_0_.length_ref, bf16[1024,1024]{1,0:T(8,128)(2,1)} %get-tuple-element.69.h2_ref, bf16[1024,1024]{1,0:T(8,128)(2,1)} %ct_ref.5, bf16[8,1024,512]{2,1,0:T(8,128)(2,1)} %get-tuple-element.87.m_ref, ...), custom_call_target="tpu_custom_call" | custom-call | tf_op jit(solution)/shard_map/ffn_weight_pair_sums/pallas_call | solution.py:871
  214.3 0.0 copy-done.3
  214.4 0.0 copy-done.2
  214.4 0.0 copy-done.1
  214.5 0.0 copy-done.4
  214.5 0.2 concatenate.6
  214.7 0.7 pad.4.small_ref
  215.4 0.0 copy-done.5
  215.4 0.1 broadcast_in_dim.6
  215.4 0.7 reshape_reshape.3.hs_ref
  216.1 140.8 %backward_and_sums.1 = (f32[1024,1024]{1,0:T(8,128)}, f32[32,1024]{1,0:T(8,128)}, f32[256,512]{1,0:T(8,128)}, f32[256,512]{1,0:T(8,128)}, f32[32,1024]{1,0:T(8,1...) custom-call(s32[1]{0:T(128)S(6)} %copy.45.refs_0_.length_ref, ...), custom_call_target="tpu_custom_call" | custom-call | tf_op jit(solution)/shard_map/backward_and_sums/pallas_call | solution.py:1367
  356.9 0.8 slice.25
  357.8 0.8 slice.24
  358.5 0.6 pad_maximum_fusion.refs_7_
  359.2 5.9 %hand_on.1 = (f32[1024,1024]{1,0:T(8,128)}, f32[256,512]{1,0:T(8,128)}, f32[256,512]{1,0:T(8,128)}, f32[32,1024]{1,0:T(8,128)}, f32[32,1024]{1,0:T(8,128)}, /*in...) custom-call(f32[1024,1024]{1,0:T(8,128)} %get-tuple-element.91.refs_, ...), custom_call_target="tpu_custom_call" | custom-call | tf_op jit(solution)/shard_map/hand_on/pallas_call | solution.py:1506
  365.1 0.6 constant_dynamic-slice_fusion.2
  365.7 0.5 bitcast_divide_fusion
  (11 shorter events, 0.2 us)
Async XLA Ops:
  184.4 29.9 %copy-start.3 = (f32[8,1,512]{2,1,0:T(1,128)S(1)}, f32[8,1,512]{2,1,0:T(1,128)}, u32[]{:S(2)}) copy-start(f32[8,1,512]{2,1,0:T(1,128)} %get-tuple-element.78) | copy-start | bytes 49156
  184.4 29.9 %copy-start.2 = (f32[8,1,512]{2,1,0:T(1,128)S(1)}, f32[8,1,512]{2,1,0:T(1,128)}, u32[]{:S(2)}) copy-start(f32[8,1,512]{2,1,0:T(1,128)} %get-tuple-element.79) | copy-start | bytes 49156
  184.5 30.0 %copy-start.1 = (f32[8,1,512]{2,1,0:T(1,128)S(1)}, f32[8,1,512]{2,1,0:T(1,128)}, u32[]{:S(2)}) copy-start(f32[8,1,512]{2,1,0:T(1,128)} %get-tuple-element.80) | copy-start | bytes 49156
  184.5 30.1 %copy-start.4 = (f32[1,1024]{1,0:T(1,128)S(1)}, f32[1,1024]{1,0:T(1,128)}, u32[]{:S(2)}) copy-start(f32[1,1024]{1,0:T(1,128)} %get-tuple-element.77) | copy-start | bytes 12292
  184.5 30.9 %copy-start.5 = (f32[16]{0:T(128)S(1)}, f32[16]{0:T(128)}, u32[]{:S(2)}) copy-start(f32[16]{0:T(128)} %refs_1_.1) | copy-start | bytes 196
  356.9 8.1 %copy-start = (f32[32,1024]{1,0:T(8,128)S(1)}, f32[32,1024]{1,0:T(8,128)}, u32[]{:S(2)}) copy-start(f32[32,1024]{1,0:T(8,128)} %get-tuple-element.98) | copy-start | bytes 393220
